TPU v7x, 128 devices: a whole 4x4x4 slice. The times are simulated.
128 devices in a mesh: ctx: 16 (over z, x), tp: 8 (over y, core).
Axes of the slice: x: 4, y: 4, z: 4, core: 2. Of those that a mesh axis runs over, the one named last changes fastest.
Arguments:
- projected: bfloat16 [3, 8192, 8192], P(None, 'ctx', 'tp'), may hold values from -6 to 6
- short_filter: float32 [3, 3, 8192], P(None, None, 'tp'), may hold values from -3.5 to 3.5
- long_filter: bfloat16 [128, 8192], P(None, 'tp'), may hold values from -0.5 to 0.5
- skip_gain: float32 [8192], P('tp'), may hold values from -3 to 3
- out_weight: bfloat16 [8192, 8192], P('tp', 'ctx'), may hold values from -0.0625 to 0.0625
- out_grad: bfloat16 [8192, 8192], P('ctx'), may hold values from -6 to 6
- left_source: int32 [16], replicated, may hold values from -1 to 15, as said below
Outputs:
- mixed: bfloat16 [8192, 8192], P(('ctx', 'tp'))
- grad_projected: bfloat16 [3, 8192, 8192], P(None, 'ctx', 'tp')
- grad_long: float32 [128, 8192], P(None, 'tp')
- grad_short: float32 [3, 3, 8192], P(None, None, 'tp')
Inputs may be any that keep to these rules, and one draw needn't show every extreme that they name: left_source[b] is -1 where block b begins a contig, else another block; no block is named by two blocks, and following left_source from any block ends at -1 without repeating a block.
All inputs are finite; a program needn't handle non-finite values.
Results may differ from a plain program's by a relative error of at most 0.015.
Values may be sent and summed in bfloat16 or wider, within the bound.
No kernel may reach another device: no remote copies, remote signals or barrier semaphores. Data moves between devices by JAX's collectives and lax.ppermute only.
A program may use at most 128 MiB of HBM per device.

v0:
```python
import math

import jax
import jax.numpy as jnp
import numpy as np
from jax import lax
from jax.experimental import pallas as pl
from jax.experimental.pallas import tpu as pltpu
from jax.sharding import PartitionSpec as P


f32, bf16 = jnp.float32, jnp.bfloat16
BLK = 128
SIDE = 4
PAD = 8


def split_hi_lo(matrix):
    hi = matrix.astype(np.float32).astype(bf16)
    lo = (matrix - hi.astype(np.float64)).astype(np.float32).astype(bf16)
    return hi, lo


def angles(times):
    freqs = np.concatenate([np.arange(0, BLK, 2), np.arange(1, BLK, 2)]) + 0.5
    return 2.0 * np.pi * freqs[:, None] * times[None, :] / (2 * BLK)


def forward_matrix():
    th = angles(np.arange(BLK, dtype=np.float64))
    hi, lo = split_hi_lo(np.concatenate([np.cos(th), -np.sin(th)], 0))
    return np.concatenate([hi, lo], 1)


def inverse_matrix(start):
    th = angles(np.arange(start, start + BLK, dtype=np.float64)).T / 1.0
    hi, lo = split_hi_lo(np.concatenate([np.cos(th), -np.sin(th)], 1) / BLK)
    return np.concatenate([hi, lo], 0)


def spectrum(fwd, rows):
    return jnp.dot(fwd, jnp.concatenate([rows, rows], 0), preferred_element_type=f32)


def delay(v):
    h = BLK // 2
    re, im = v[:BLK], v[BLK:]
    return jnp.concatenate([im[:h], -im[h:], -re[:h], re[h:]], 0)


def product(a, b):
    ar, ai, br, bi = a[:BLK], a[BLK:], b[:BLK], b[BLK:]
    return jnp.concatenate([ar * br - ai * bi, ar * bi + ai * br], 0)


def product_conj(a, b):
    ar, ai, br, bi = a[:BLK], a[BLK:], b[:BLK], b[BLK:]
    return jnp.concatenate([ar * br + ai * bi, ai * br - ar * bi], 0)


def invert(inv, y):
    hi = y.astype(bf16)
    lo = (y - hi.astype(f32)).astype(bf16)
    both = jnp.dot(inv, hi, preferred_element_type=f32)
    return both[:BLK] + both[BLK:] + jnp.dot(inv[:BLK], lo, preferred_element_type=f32)


def forward_kernel(order, proj, halo, sf, lf, skip, fwd, inv, gated, conv, act, mspec, fspec, ext):
    rows = proj.shape[1]
    fmat, imat = fwd[...], inv[...]
    for m in range(3):
        ext[PAD : PAD + rows] = proj[m].astype(f32)
        edge = halo[BLK : BLK + PAD].astype(f32)
        ext[PAD - 2 : PAD] = edge[2 * m : 2 * m + 2]
        total = sf[m, 0:1] * ext[PAD : PAD + rows]
        for s in (1, 2):
            total = total + sf[m, s : s + 1] * ext[PAD - s : PAD - s + rows]
        act[m] = total
    filt = spectrum(fmat, lf[...])
    fspec[...] = filt
    before = spectrum(fmat, halo[:BLK])
    for b in range(rows // BLK):
        span = slice(b * BLK, (b + 1) * BLK)
        mixin = (act[1, span] * act[2, span]).astype(bf16)
        here = spectrum(fmat, mixin)
        window = before + delay(here)
        before = here
        mspec[b] = window
        out = invert(imat, product(filt, window)) + skip[...] * mixin.astype(f32)
        conv[span] = out
        gate = (act[0, span] * out).astype(bf16)
        for half in range(2):
            start = pl.multiple_of(order[2 * b + half], BLK // 2)
            gated[pl.ds(start, BLK // 2)] = gate[half * (BLK // 2) : (half + 1) * (BLK // 2)]


def backward_kernel(place, acc, act0, act12, convh, mspec, fspec, skip, fwd, inv, invlag, *refs):
    og, refs = refs[: 2 * SIDE], refs[2 * SIDE :]
    weights, (bg, pay0, pay1, pay2, pay3, gmix, lagbuf) = refs[:6], refs[6:]
    rows = bg.shape[0]
    nb = rows // BLK
    fmat, imat = fwd[...], inv[...]
    filt = fspec[...]
    blocks = []
    for first, second, third in (weights[:3], weights[3:]):
        blocks += [first[0], first[1], second[...], third[...]]
    bg[...] = acc[...] + lax.dot_general(
        jnp.concatenate([o[...] for o in og], 1),
        jnp.concatenate(blocks, 1),
        (((1,), (1,)), ((), ())),
        preferred_element_type=f32,
    )
    grads, specs = [], []
    lag = jnp.zeros(filt.shape, f32)
    for b in range(nb):
        span = slice(b * BLK, (b + 1) * BLK)
        g = (bg[span] * act0[0, span]).astype(bf16)
        here = spectrum(fmat, g)
        lag = lag + product_conj(here, mspec[b])
        grads.append(g)
        specs.append(here)
    lagbuf[...] = invert(invlag[...], lag)
    for b in range(nb):
        span = slice(b * BLK, (b + 1) * BLK)
        window = specs[b] + delay(specs[b + 1]) if b + 1 < nb else specs[b]
        gm = invert(imat, product_conj(window, filt)) + skip[...] * grads[b].astype(f32)
        gmix[span] = gm
        if b == 0:
            head = gm[:PAD]
            ga0 = bg[:PAD] * convh[...]
            ga1 = head * act12[1]
            ga2 = head * act12[0]
            edge = jnp.concatenate(
                [ga0[:2], ga1[:2], ga2[:2], jnp.zeros((2, gm.shape[1]), f32)], 0
            ).astype(bf16)
    quarter = BLK // SIDE
    for k, pay in enumerate((pay0, pay1, pay2, pay3)):
        pay[:BLK] = grads[0]
        pay[BLK : BLK + PAD] = edge
        start = pl.multiple_of((place[0] ^ k) * quarter, quarter)
        pay[BLK + PAD :] = lagbuf[pl.ds(start, quarter)].astype(bf16)


def finish_body(bg, conv, gmix, act, proj, sf, extra, gp, ext):
    rows = bg.shape[0]
    sums = []
    for m in range(3):
        if m == 0:
            ga = bg[...] * conv[...]
        else:
            ga = gmix[...] * act[2 - m]
        ext[:rows] = ga
        ext[rows : rows + PAD] = extra[m]
        x = proj[m].astype(f32)
        total = sf[m, 0:1] * ga
        sums.append(jnp.sum(x * ga, axis=0, keepdims=True))
        for s in (1, 2):
            moved = ext[s : s + rows]
            total = total + sf[m, s : s + 1] * moved
            sums.append(jnp.sum(x * moved, axis=0, keepdims=True))
        gp[m] = total.astype(bf16)
    return jnp.concatenate(sums + [jnp.zeros((7, bg.shape[1]), f32)], 0)


def top_kernel(bg, conv, gmix, act, bgn, convn, gmixn, actn, proj, sf, gp, short, ext):
    extra = [bgn[...] * convn[...], gmixn[...] * actn[1], gmixn[...] * actn[0]]
    short[...] = finish_body(bg, conv, gmix, act, proj, sf, extra, gp, ext)


def bottom_kernel(
    bg, conv, gmix, act, halo, proj, sf, fspec, fwd, inv, short_in, gp_in, gp, short, ext, gfull
):
    del gp_in
    rows = bg.shape[0]
    late = delay(spectrum(fwd[...], halo[:BLK]))
    gfull[: rows - BLK] = gmix[: rows - BLK]
    gfull[rows - BLK :] = gmix[rows - BLK :] + invert(inv[...], product_conj(late, fspec[...]))
    edge = halo[BLK : BLK + PAD].astype(f32)
    zeros = jnp.zeros((PAD - 2, edge.shape[1]), f32)
    extra = [jnp.concatenate([edge[2 * m : 2 * m + 2], zeros], 0) for m in range(3)]
    short[...] = short_in[...] + finish_body(bg, conv, gfull, act, proj, sf, extra, gp, ext)


def pieces_kernel(layout, first, back, *refs):
    nw = sum(len(counts) for counts in layout)
    weights, refs = refs[:nw], refs[nw:]
    gated, refs = refs[0], refs[1:]
    if back:
        og, refs = refs[:SIDE], refs[SIDE:]
        if not first:
            acc_in, refs = refs[0], refs[1:]
        mine, other, acc, buf = refs
    else:
        mine, other, buf = refs
    step = pl.program_id(0)
    if back:

        @pl.when(step == 0)
        def _():
            acc[...] = jnp.zeros_like(acc) if first else acc_in[...]

    chans = gated.shape[1]
    half = gated.shape[0] // 2
    begin = 0
    for i, counts in enumerate(layout):
        part = weights[begin : begin + len(counts)]
        begin += len(counts)

        @pl.when(step == i)
        def _(part=part, counts=counts):
            at = 0
            for r, c in zip(part, counts):
                for n in range(c):
                    buf[:, at : at + r.shape[1]] = r[n * chans : (n + 1) * chans]
                    at += r.shape[1]

    out = jnp.dot(gated[...], buf[...], preferred_element_type=f32).astype(bf16)
    mine[...] = out[:half]
    other[...] = out[half:]
    if back:
        acc[...] += lax.dot_general(
            jnp.concatenate([o[...] for o in og], 1),
            buf[...],
            (((1,), (1,)), ((), ())),
            preferred_element_type=f32,
        )


def multiply_pieces(groups, cols, gated, out_grad, acc, back=True):
    rows, chans = gated.shape
    width = groups[0][0].shape[1]
    layout = [tuple(w.shape[0] // chans for w in group) for group in groups]
    steps = len(groups)
    first = acc is None
    one = pl.Buffered(1)
    weights = [w for group in groups for w in group]
    in_specs = [pl.BlockSpec(w.shape, lambda i, c: (0, 0), pipeline_mode=one) for w in weights]
    whole = pl.BlockSpec((rows, chans), lambda i, c: (0, 0), pipeline_mode=one)
    in_specs.append(whole)
    operands = [*weights, gated]
    if back:
        in_specs += [
            pl.BlockSpec((rows, width), lambda i, c, j=j: (0, c[SIDE * i + j])) for j in range(SIDE)
        ]
        operands += [out_grad] * SIDE
        if not first:
            in_specs.append(whole)
            operands.append(acc)
    half_shape = jax.ShapeDtypeStruct((rows // 2, steps * SIDE * width), bf16)
    half_spec = pl.BlockSpec((rows // 2, SIDE * width), lambda i, c: (0, i))

    def kernel(cols_ref, *refs):
        del cols_ref
        pieces_kernel(layout, first, back, *refs)

    return pl.pallas_call(
        kernel,
        grid_spec=pltpu.PrefetchScalarGridSpec(
            num_scalar_prefetch=1,
            grid=(steps,),
            in_specs=in_specs,
            out_specs=[half_spec, half_spec] + [whole] * back,
            scratch_shapes=[pltpu.VMEM((chans, SIDE * width), bf16)],
        ),
        out_shape=[half_shape, half_shape] + [jax.ShapeDtypeStruct((rows, chans), f32)] * back,
        cost_estimate=pl.CostEstimate(
            flops=(2 + 2 * back) * rows * chans * width * SIDE * steps,
            bytes_accessed=SIDE * steps * (2 * chans * width + 4 * rows * width) + 10 * rows * chans,
            transcendentals=0,
        ),
        name="pieces",
    )(cols, *operands)


def collect_kernel(counts, cols, *refs):
    mixed = refs[-1]
    width = mixed.shape[1] // sum(counts)
    begin = 0
    for i, count in enumerate(counts):
        parts = refs[4 * i : 4 * i + 4]

        @pl.loop(0, count)
        def _(p, parts=parts, begin=begin):
            lanes = pl.ds(pl.multiple_of(p * width, width), width)
            vals = [r[:, lanes].astype(f32) for r in parts]
            start = pl.multiple_of(cols[begin + p] * width, width)
            mixed[:, pl.ds(start, width)] = (
                (vals[0] + vals[1]) + (vals[2] + vals[3])
            ).astype(bf16)

        begin += count


def on_device(projected, short_filter, long_filter, skip_gain, out_weight, out_grad, left_source):
    rows, chans = projected.shape[1:]
    width = out_weight.shape[1] // 2
    ctx_count, tp_count = lax.axis_size("ctx"), lax.axis_size("tp")
    me, tp = lax.axis_index("ctx"), lax.axis_index("tp")
    zi, xi, yi, ci = me // SIDE, me % SIDE, tp // 2, tp % 2

    def ring(value, axis, step):
        if axis == "x":
            pairs = [(d, d // SIDE * SIDE + (d + step) % SIDE) for d in range(ctx_count)]
        else:
            pairs = [(d, (d + SIDE * step) % ctx_count) for d in range(ctx_count)]
        return lax.ppermute(value, "ctx", pairs)

    def swap(value, axis, k):
        shift = {"x": k, "z": k * SIDE, "core": k, "y": 2 * k}[axis]
        name = "ctx" if axis in "xz" else "tp"
        return lax.ppermute(value, name, [(d, d ^ shift) for d in range(lax.axis_size(name))])

    def gather(piece, first, second):
        h = piece.shape[0] // 2
        p, q = ring(piece, first, 1), ring(piece, first, -1)
        t, b = ring(p[:h], first, 1), ring(q[h:], first, -1)
        line = jnp.concatenate([piece, p, q], 0)
        lp, lq = ring(line, second, 1), ring(line, second, -1)
        far = jnp.concatenate([t, b], 0)
        fp, fq = ring(far, second, 1), ring(far, second, -1)
        ft, fb = ring(lp[: 4 * h], second, 1), ring(lq[4 * h :], second, -1)
        ff = ring(fq, second, -1)
        return [line, far], [[lp, fp], [lq, fq]], [ft, fb, ff]

    def blocks(half, near, far_steps):
        out = []
        for f in far_steps:
            for n in near:
                z, x = (f, n) if half == 0 else (n, f)
                out.append(2 * ((zi + z) % SIDE * SIDE + (xi + x) % SIDE) + half)
        return out

    order4 = (0, -1, 1, 2)
    cols1 = jnp.stack(blocks(0, order4, (0,)) + blocks(1, order4, (0,)))
    cols2 = jnp.stack(blocks(0, order4, (-1, 1)) + blocks(1, order4, (-1, 1)))
    cols3 = jnp.stack(blocks(0, order4, (2,)) + blocks(1, order4, (2,)))

    positions = jnp.arange(ctx_count, dtype=jnp.int32)
    matches = left_source[None, :] == positions[:, None]
    readers = jnp.where(
        jnp.any(matches, 1), jnp.sum(jnp.where(matches, positions[None, :], 0), 1), -1
    )

    def pick(options, index):
        low = jnp.where(index == 1, options[1], options[0])
        high = jnp.where(index == 3, options[3], options[2])
        return jnp.where(index >= 2, high, low)

    def at(table, index):
        return lax.dynamic_index_in_dim(table, index, 0, keepdims=False)

    def along_x(payloads):
        return [payloads[0]] + [swap(payloads[k], "x", k) for k in (1, 2, 3)]

    def along_z(payloads):
        return [payloads[0]] + [swap(payloads[k], "z", k) for k in (1, 2, 3)]

    def chosen(got, table):
        out = []
        for k in range(SIDE):
            source = jnp.maximum(at(table, (zi ^ k) * SIDE + xi), 0)
            out.append(pick(got, (source % SIDE) ^ xi))
        return out

    def landed(got, table):
        source = at(table, me)
        value = pick(got, (jnp.maximum(source, 0) // SIDE) ^ zi)
        return jnp.where(source >= 0, value, jnp.zeros_like(value))

    near = projected[1:, rows - BLK - PAD :].astype(f32)
    tail = jnp.zeros((2, BLK, chans), f32)
    for s in range(3):
        tail = tail + short_filter[1:, s][:, None] * near[:, PAD - s : PAD - s + BLK]
    raw = projected[:, rows - 2 :].reshape(6, chans)
    sent = jnp.concatenate(
        [(tail[0] * tail[1]).astype(bf16), raw, jnp.zeros((2, chans), bf16)], 0
    )
    got = along_x([sent] * SIDE)
    to_z = chosen(got, left_source)
    got = along_z(to_z)
    left = landed(got, left_source)

    wa, wb, _ = lax.optimization_barrier((out_weight[:, :width], out_weight[:, width:], sent))
    near_a, mid_a, far_a = gather(wa, "x", "z")
    near_b, mid_b, far_b = gather(wb, "z", "x")

    fwd = jnp.asarray(forward_matrix())
    inv_late, inv_now, inv_lag = (jnp.asarray(inverse_matrix(s)) for s in (BLK, 0, -BLK))
    skip_row = skip_gain[None, :]
    share = rows // tp_count
    order = jnp.stack(
        [
            (((t % 2) ^ ci) * SIDE + ((t // 2) ^ yi)) * share
            for t in range(tp_count)
        ]
    ).astype(jnp.int32)
    tile = 256
    grid = (chans // tile,)
    nb = rows // BLK

    def col(*lead):
        return pl.BlockSpec((*lead, tile), lambda i, *_: (*([0] * len(lead)), i))

    const = pl.BlockSpec((2 * BLK, 2 * BLK), lambda i, *_: (0, 0))
    forward = pl.pallas_call(
        forward_kernel,
        grid_spec=pltpu.PrefetchScalarGridSpec(
            num_scalar_prefetch=1,
            grid=grid,
            in_specs=[
                col(3, rows), col(BLK + PAD), col(3, 3), col(BLK), col(1), const, const,
            ],
            out_specs=[col(rows), col(rows), col(3, rows), col(nb, 2 * BLK), col(2 * BLK)],
            scratch_shapes=[pltpu.VMEM((rows + PAD, tile), f32)],
        ),
        out_shape=[
            jax.ShapeDtypeStruct((rows, chans), bf16),
            jax.ShapeDtypeStruct((rows, chans), f32),
            jax.ShapeDtypeStruct((3, rows, chans), f32),
            jax.ShapeDtypeStruct((nb, 2 * BLK, chans), f32),
            jax.ShapeDtypeStruct((2 * BLK, chans), f32),
        ],
        cost_estimate=pl.CostEstimate(
            flops=12_000_000_000, bytes_accessed=20 << 20, transcendentals=0
        ),
        name="forward",
    )
    gated, conv, act, mspec, fspec = forward(
        order, projected, left, short_filter, long_filter, skip_row, fwd, inv_late
    )

    def scatter(mine, other):
        got = swap(other, "core", 1)
        total = (mine.astype(f32) + got.astype(f32)).astype(bf16)
        parts = [total[k * share : (k + 1) * share] for k in range(SIDE)]
        return [parts[0]] + [swap(parts[k], "y", k) for k in (1, 2, 3)]

    mine1, other1, acc = multiply_pieces([near_a, near_b], cols1, gated, out_grad, None)
    out1 = scatter(mine1, other1)
    mine2, other2, acc = multiply_pieces(mid_a + mid_b, cols2, gated, out_grad, acc)
    out2 = scatter(mine2, other2)

    quarter = BLK // SIDE
    place = jnp.concatenate([jnp.reshape(xi, (1,)), cols3]).astype(jnp.int32)

    def third(w):
        count = w.shape[0] // chans
        if count == 1:
            return w, pl.BlockSpec((tile, width), lambda i, c: (i, 0))
        return w.reshape(count, chans, width), pl.BlockSpec(
            (count, tile, width), lambda i, c: (0, i, 0)
        )

    lasts, last_specs = zip(*[third(w) for w in far_a + far_b])
    pay_shape = jax.ShapeDtypeStruct((BLK + PAD + quarter, chans), bf16)
    pay_spec = col(BLK + PAD + quarter)
    backward = pl.pallas_call(
        backward_kernel,
        grid_spec=pltpu.PrefetchScalarGridSpec(
            num_scalar_prefetch=1,
            grid=grid,
            in_specs=[
                col(rows),
                pl.BlockSpec((1, rows, tile), lambda i, c: (0, 0, i)),
                pl.BlockSpec(
                    (pl.Element(2), pl.Element(PAD), pl.Element(tile)),
                    lambda i, c: (1, 0, i * tile),
                ),
                col(PAD),
                col(nb, 2 * BLK),
                col(2 * BLK),
                col(1),
                const,
                const,
                const,
                *[
                    pl.BlockSpec((rows, width), lambda i, c, j=j: (0, c[1 + j]))
                    for j in range(2 * SIDE)
                ],
                *last_specs,
            ],
            out_specs=[col(rows), pay_spec, pay_spec, pay_spec, pay_spec, col(rows)],
            scratch_shapes=[pltpu.VMEM((BLK, tile), f32)],
        ),
        out_shape=[
            jax.ShapeDtypeStruct((rows, chans), f32),
            pay_shape, pay_shape, pay_shape, pay_shape,
            jax.ShapeDtypeStruct((rows, chans), f32),
        ],
        cost_estimate=pl.CostEstimate(
            flops=8_000_000_000, bytes_accessed=20 << 20, transcendentals=0
        ),
        name="backward",
    )
    bg, pay0, pay1, pay2, pay3, gmix = backward(
        place, acc, act, act, conv, mspec, fspec, skip_row, fwd, inv_now, inv_lag,
        *[out_grad] * (2 * SIDE), *lasts,
    )

    got = along_x([pay0, pay1, pay2, pay3])
    sums = [g[BLK + PAD :].astype(f32) for g in got]
    quarter_sum = ((sums[0] + sums[1]) + (sums[2] + sums[3])).astype(bf16)
    to_z = chosen([g[: BLK + PAD] for g in got], readers)
    got = along_z([jnp.concatenate([v, quarter_sum], 0) for v in to_z])
    right = landed([g[: BLK + PAD] for g in got], readers)
    sums = [g[BLK + PAD :].astype(f32) for g in got]
    my_quarter = (sums[0] + sums[1]) + (sums[2] + sums[3])

    mine3, other3 = multiply_pieces([far_a, far_b], cols3, gated, None, None, back=False)
    out3 = scatter(mine3, other3)

    low = rows - BLK - PAD

    def rows_at(start, n, *lead):
        zeros = [0] * len(lead)
        dims = [pl.Element(d) for d in (*lead, n, tile)]
        return pl.BlockSpec(tuple(dims), lambda i: (*zeros, start, i * tile))

    def acts_at(start, n):
        return pl.BlockSpec(
            (pl.Element(2), pl.Element(n), pl.Element(tile)), lambda i: (1, start, i * tile)
        )

    gp_shape = jax.ShapeDtypeStruct((3, rows, chans), bf16)
    short_shape = jax.ShapeDtypeStruct((16, chans), f32)
    top = pl.pallas_call(
        top_kernel,
        grid=grid,
        in_specs=[
            rows_at(0, low), rows_at(0, low), rows_at(0, low), acts_at(0, low),
            rows_at(low, PAD), rows_at(low, PAD), rows_at(low, PAD), acts_at(low, PAD),
            rows_at(0, low, 3), col(3, 3),
        ],
        out_specs=[rows_at(0, low, 3), col(16)],
        out_shape=[gp_shape, short_shape],
        scratch_shapes=[pltpu.VMEM((low + PAD, tile), f32)],
        cost_estimate=pl.CostEstimate(
            flops=200_000_000, bytes_accessed=10 << 20, transcendentals=0
        ),
        name="top",
    )
    gp, short = top(bg, conv, gmix, act, bg, conv, gmix, act, projected, short_filter)
    rest = rows - low
    bottom = pl.pallas_call(
        bottom_kernel,
        grid=grid,
        in_specs=[
            rows_at(low, rest), rows_at(low, rest), rows_at(low, rest), acts_at(low, rest),
            col(BLK + PAD), rows_at(low, rest, 3), col(3, 3), col(2 * BLK), const, const, col(16),
            pl.BlockSpec(memory_space=pl.ANY),
        ],
        out_specs=[rows_at(low, rest, 3), col(16)],
        out_shape=[gp_shape, short_shape],
        scratch_shapes=[pltpu.VMEM((rest + PAD, tile), f32), pltpu.VMEM((rest, tile), f32)],
        input_output_aliases={11: 0},
        cost_estimate=pl.CostEstimate(
            flops=2_000_000_000, bytes_accessed=5 << 20, transcendentals=0
        ),
        name="bottom",
    )
    gp, short = bottom(
        bg, conv, gmix, act, right, projected, short_filter, fspec, fwd, inv_now, short, gp
    )

    got = along_x([my_quarter] * SIDE)
    long_total = jnp.concatenate([pick(got, xi ^ q) for q in range(SIDE)], 0)
    sums = along_x([short] * SIDE)
    sums = (sums[0] + sums[1]) + (sums[2] + sums[3])
    sums = along_z([sums] * SIDE)
    short_total = ((sums[0] + sums[1]) + (sums[2] + sums[3]))[:9].reshape(3, 3, chans)

    counts = tuple(o[0].shape[1] // width for o in (out1, out2, out3))
    mixed = pl.pallas_call(
        lambda cols, *refs: collect_kernel(counts, cols, *refs),
        grid_spec=pltpu.PrefetchScalarGridSpec(
            num_scalar_prefetch=1,
            grid=(1,),
            in_specs=[
                pl.BlockSpec(o[0].shape, lambda i, c: (0, 0))
                for o in (out1, out2, out3)
                for _ in range(SIDE)
            ],
            out_specs=pl.BlockSpec((share, 2 * width * ctx_count), lambda i, c: (0, 0)),
        ),
        out_shape=jax.ShapeDtypeStruct((share, 2 * width * ctx_count), bf16),
        cost_estimate=pl.CostEstimate(flops=10_000_000, bytes_accessed=5 << 20, transcendentals=0),
        name="collect",
    )(jnp.concatenate([cols1, cols2, cols3]), *out1, *out2, *out3)

    scale = 1.0 / math.sqrt(rows * ctx_count)
    return mixed, gp, long_total * scale, short_total * scale


def solution(mesh):
    placed = (
        P(None, "ctx", "tp"),
        P(None, None, "tp"),
        P(None, "tp"),
        P("tp"),
        P("tp", "ctx"),
        P("ctx", None),
        P(),
    )
    return jax.shard_map(
        on_device,
        mesh=mesh,
        in_specs=placed,
        out_specs=(
            P(("ctx", "tp"), None),
            P(None, "ctx", "tp"),
            P(None, "tp"),
            P(None, None, "tp"),
        ),
        check_vma=False,
    )
```

profile of v0, /device:TPU:24, one launch (start us, length us, event | category | flops | bytes accessed | tf_op | source)
XLA Modules:
  0.0 320.2 jit_solution(978284365635647036)
XLA Ops:
  31.4 5.6 %collective-permute-done.8 = bf16[136,1024]{1,0:T(8,128)(2,1)S(1)} collective-permute-done((bf16[136,1024]{1,0:T(8,128)(2,1)}, bf16[136,1024]{1,0:T(8,128)(2,1)S(1)}, u32[]{:S(2)}, u32[]{:S(2)}) %collective-permute-start.8) | collective-permute-done | bytes 278560 | tf_op jit(solution)/shard_map/ppermute | solution.py:311
  40.6 3.3 %collective-permute-start.3 = (bf16[512,256]{1,0:T(8,128)(2,1)S(1)}, bf16[512,256]{1,0:T(8,128)(2,1)S(1)}, u32[]{:S(2)}, u32[]{:S(2)}) collective-permute-start(bf16[512,256]{1,0:T(8,128)(2,1)S(1)} %slice.194), channel_id=1, source_target_pairs={{0,24},{8,0},{16,8},{24,16},{32,56},{40,32},{48,40},{56,48},{64,88... | collective-permute-start | bytes 786440 | tf_op jit(solution)/shard_map/ppermute | solution.py:306
  43.9 20.8 %collective-permute-done.13 = bf16[136,1024]{1,0:T(8,128)(2,1)S(1)} collective-permute-done((bf16[136,1024]{1,0:T(8,128)(2,1)S(1)}, bf16[136,1024]{1,0:T(8,128)(2,1)S(1)}, u32[]{:S(2)}, u32[]{:S(2)}) %collective-permute-start.13) | collective-permute-done | bytes 278560 | tf_op jit(solution)/shard_map/ppermute | solution.py:311
  64.7 4.6 %collective-permute-start.11 = (bf16[136,1024]{1,0:T(8,128)(2,1)S(1)}, bf16[136,1024]{1,0:T(8,128)(2,1)}, u32[]{:S(2)}, u32[]{:S(2)}) collective-permute-start(bf16[136,1024]{1,0:T(8,128)(2,1)S(1)} %get-tuple-element.62), channel_id=1, source_target_pairs={{0,96},{8,104},{16,112},{24,120},{32,64},{40,72},{48,80},{56,88},{... | collective-permute-start | bytes 835592 | tf_op jit(solution)/shard_map/ppermute | solution.py:311
  70.2 4.2 %collective-permute-done.2 = bf16[512,256]{1,0:T(8,128)(2,1)S(1)} collective-permute-done((bf16[512,256]{1,0:T(8,128)(2,1)S(1)}, bf16[512,256]{1,0:T(8,128)(2,1)S(1)}, u32[]{:S(2)}, u32[]{:S(2)}) %collective-permute-start.2) | collective-permute-done | bytes 262176 | tf_op jit(solution)/shard_map/ppermute | solution.py:306
  78.7 6.9 %collective-permute-done.6 = bf16[512,256]{1,0:T(8,128)(2,1)S(1)} collective-permute-done((bf16[512,256]{1,0:T(8,128)(2,1)S(1)}, bf16[512,256]{1,0:T(8,128)(2,1)S(1)}, u32[]{:S(2)}, u32[]{:S(2)}) %collective-permute-start.6) | collective-permute-done | bytes 262176 | tf_op jit(solution)/shard_map/ppermute | solution.py:306
  89.5 12.0 %collective-permute-done.12 = bf16[136,1024]{1,0:T(8,128)(2,1)S(1)} collective-permute-done((bf16[136,1024]{1,0:T(8,128)(2,1)S(1)}, bf16[136,1024]{1,0:T(8,128)(2,1)S(1)}, u32[]{:S(2)}, u32[]{:S(2)}) %collective-permute-start.12) | collective-permute-done | bytes 278560 | tf_op jit(solution)/shard_map/ppermute | solution.py:311
  118.8 3.2 collective-permute-start.35
  122.0 10.1 %forward.1 = (bf16[512,1024]{1,0:T(8,128)(2,1)}, f32[512,1024]{1,0:T(8,128)}, f32[3,512,1024]{2,1,0:T(8,128)}, f32[4,256,1024]{2,1,0:T(8,128)}, f32[256,1024]{1,0:T(8,128)}) custom-call(s32[8]{0:T(128)} %stack.173.order, bf16[3,512,1024]{2,1,0:T(8,128)(2,1)} %proj.5, bf16[136,1024]{1,0:T(8,128)(2,1)} %select_select_fusion.3.halo, f32[3,3,1024]{2,1,0:T(4,128)} %sf.5, ...), custom_call_target="tpu_custom_call" | custom-call | flops 12000000000 | bytes 20971520 | tf_op jit(solution)/shard_map/forward/pallas_call | solution.py:428
  134.2 6.4 %collective-permute-done.20.refs_2_ = bf16[3072,256]{1,0:T(8,128)(2,1)} collective-permute-done((bf16[3072,256]{1,0:T(8,128)(2,1)}, bf16[3072,256]{1,0:T(8,128)(2,1)}, u32[]{:S(2)}, u32[]{:S(2)}) %collective-permute-start.20) | collective-permute-done | bytes 1572896 | tf_op jit(solution)/shard_map/ppermute | solution.py:306
  142.4 7.9 %collective-permute-done.24.refs_6_ = bf16[3072,256]{1,0:T(8,128)(2,1)} collective-permute-done((bf16[3072,256]{1,0:T(8,128)(2,1)}, bf16[3072,256]{1,0:T(8,128)(2,1)}, u32[]{:S(2)}, u32[]{:S(2)}) %collective-permute-start.24) | collective-permute-done | bytes 1572896 | tf_op jit(solution)/shard_map/ppermute | solution.py:306
  150.4 10.4 %pieces.3 = (bf16[256,2048]{1,0:T(8,128)(2,1)}, bf16[256,2048]{1,0:T(8,128)(2,1)}, f32[512,1024]{1,0:T(8,128)}) custom-call(s32[8]{0:T(128)} %stack.164.cols_ref, bf16[3072,256]{1,0:T(8,128)(2,1)} %constant_dynamic-update-slice_fusion.refs_0_, bf16[1024,256]{1,0:T(8,128)(2,1)} %copy-done.4, bf16[3072,256]{1,0:T(8,128)(2,1)} %constant_dynamic-update-slice_fusion.5.refs_2_, ...), custom_call_target="tpu_custom_call" | custom-call | flops 4294967296 | bytes 13631488 | tf_op jit(solution)/shard_map/pieces/pallas_call | solution.py:256
  165.3 3.2 %collective-permute-start.34 = (bf16[1024,256]{1,0:T(8,128)(2,1)}, bf16[1024,256]{1,0:T(8,128)(2,1)}, u32[]{:S(2)}, u32[]{:S(2)}) collective-permute-start(bf16[1024,256]{1,0:T(8,128)(2,1)} %slice.208), channel_id=1, source_target_pairs={{0,24},{8,0},{16,8},{24,16},{32,56},{40,32},{48,40},{56,48},{64,88... | collective-permute-start | bytes 1572872 | tf_op jit(solution)/shard_map/ppermute | solution.py:306
  168.5 17.9 %pieces.4 = (bf16[256,4096]{1,0:T(8,128)(2,1)}, bf16[256,4096]{1,0:T(8,128)(2,1)}, f32[512,1024]{1,0:T(8,128)}) custom-call(s32[16]{0:T(128)} %stack.174.cols_ref, bf16[3072,256]{1,0:T(8,128)(2,1)} %copy-done, bf16[1024,256]{1,0:T(8,128)(2,1)} %copy-done.18, bf16[3072,256]{1,0:T(8,128)(2,1)} %collective-permute-done.20.refs_2_, ...), custom_call_target="tpu_custom_call" | custom-call | flops 8589934592 | bytes 22020096 | tf_op jit(solution)/shard_map/pieces/pallas_call | solution.py:256
  187.9 14.0 %backward.1 = (f32[512,1024]{1,0:T(8,128)}, bf16[168,1024]{1,0:T(8,128)(2,1)}, bf16[168,1024]{1,0:T(8,128)(2,1)}, bf16[168,1024]{1,0:T(8,128)(2,1)}, bf16[168,1024]{1,0:T(8,128)(2,1)}, /*index=5*/f32[512,1024]{1,0:T(8,128)}) custom-call(s32[9]{0:T(128)} %concatenate.41.place, f32[512,1024]{1,0:T(8,128)} %get-tuple-element.39.acc, ...), custom_call_target="tpu_custom_call" | custom-call | flops 8000000000 | bytes 20971520 | tf_op jit(solution)/shard_map/backward/pallas_call | solution.py:495
  202.9 3.2 %collective-permute-start.42 = (bf16[168,1024]{1,0:T(8,128)(2,1)}, bf16[168,1024]{1,0:T(8,128)(2,1)S(1)}, u32[]{:S(2)}, u32[]{:S(2)}) collective-permute-start(bf16[168,1024]{1,0:T(8,128)(2,1)} %get-tuple-element.48), channel_id=1, source_target_pairs={{0,8},{8,0},{16,24},{24,16},{32,40},{40,32},{48,56},{56,48},{64,72... | collective-permute-start | bytes 1032200 | tf_op jit(solution)/shard_map/ppermute | solution.py:311
  209.1 11.5 %collective-permute-done.40 = bf16[168,1024]{1,0:T(8,128)(2,1)S(1)} collective-permute-done((bf16[168,1024]{1,0:T(8,128)(2,1)}, bf16[168,1024]{1,0:T(8,128)(2,1)S(1)}, u32[]{:S(2)}, u32[]{:S(2)}) %collective-permute-start.40) | collective-permute-done | bytes 344096 | tf_op jit(solution)/shard_map/ppermute | solution.py:311
  228.9 8.3 %top.1 = (bf16[3,512,1024]{2,1,0:T(8,128)(2,1)}, f32[16,1024]{1,0:T(8,128)}) custom-call(f32[512,1024]{1,0:T(8,128)} %get-tuple-element.44.bg.bgn, f32[512,1024]{1,0:T(8,128)} %get-tuple-element.41.convh.conv.convn, f32[512,1024]{1,0:T(8,128)} %get-tuple-element.45.gmix.gmixn, f32[3,512,1024]{2,1,0:T(8,128)} %get-tuple-element.40.act0.act12.act.actn, ...), custom_call_target="tpu_custom_call" | custom-call | flops 200000000 | bytes 10485760 | tf_op jit(solution)/shard_map/top/pallas_call | solution.py:542
  237.3 7.3 %pieces.5 = (bf16[256,2048]{1,0:T(8,128)(2,1)}, bf16[256,2048]{1,0:T(8,128)(2,1)}) custom-call(s32[8]{0:T(128)} %stack.175.cols_ref, bf16[2048,256]{1,0:T(8,128)(2,1)} %copy-done.13, bf16[1024,256]{1,0:T(8,128)(2,1)} %collective-permute-done.31.refs_1_.refs_9_, bf16[1024,256]{1,0:T(8,128)(2,1)} %collective-permute-done.32.refs_2_.refs_10_, ...), custom_call_target="tpu_custom_call" | custom-call | flops 2147483648 | bytes 13631488 | tf_op jit(solution)/shard_map/pieces/pallas_call | solution.py:256
  246.3 6.1 %bottom.1 = (bf16[3,512,1024]{2,1,0:T(8,128)(2,1)}, f32[16,1024]{1,0:T(8,128)}) custom-call(f32[512,1024]{1,0:T(8,128)} %get-tuple-element.44.bg.bgn, f32[512,1024]{1,0:T(8,128)} %get-tuple-element.41.convh.conv.convn, f32[512,1024]{1,0:T(8,128)} %get-tuple-element.45.gmix.gmixn, ...), custom_call_target="tpu_custom_call", output_to_operand_aliasing={{0}: (11, {})} | custom-call | flops 2000000000 | bytes 5242880 | tf_op jit(solution)/shard_map/bottom/pallas_call | solution.py:561
  259.4 3.0 collective-permute-start.17
  287.4 21.1 %collective-permute-done.38.refs_10_ = bf16[64,2048]{1,0:T(8,128)(2,1)S(1)} collective-permute-done((bf16[64,2048]{1,0:T(8,128)(2,1)}, bf16[64,2048]{1,0:T(8,128)(2,1)S(1)}, u32[]{:S(2)}, u32[]{:S(2)}) %collective-permute-start.38) | collective-permute-done | bytes 262176 | tf_op jit(solution)/shard_map/ppermute | solution.py:311
  308.5 6.0 %collective-permute-done.39.refs_11_ = bf16[64,2048]{1,0:T(8,128)(2,1)S(1)} collective-permute-done((bf16[64,2048]{1,0:T(8,128)(2,1)}, bf16[64,2048]{1,0:T(8,128)(2,1)S(1)}, u32[]{:S(2)}, u32[]{:S(2)}) %collective-permute-start.39) | collective-permute-done | bytes 262176 | tf_op jit(solution)/shard_map/ppermute | solution.py:311
  315.7 4.5 %collect.1 = bf16[64,8192]{1,0:T(8,128)(2,1)} custom-call(s32[32]{0:T(128)} %concatenate.35.cols, bf16[64,2048]{1,0:T(8,128)(2,1)} %get-tuple-element.70.refs_0_, bf16[64,2048]{1,0:T(8,128)(2,1)} %collective-permute-done.15.refs_1_, bf16[64,2048]{1,0:T(8,128)(2,1)} %copy-done.25, bf16[64,2048]{1,0:T(8,128)(2,1)} %copy-done.26, ...), custom_call_target="tpu_custom_call" | custom-call | flops 10000000 | bytes 5242880 | tf_op jit(solution)/shard_map/collect/pallas_call | solution.py:573
  (219 shorter events, 109.6 us)
Async XLA Ops:
  25.3 92.6 %collective-permute-start.18 = (bf16[3072,256]{1,0:T(8,128)(2,1)}, bf16[3072,256]{1,0:T(8,128)(2,1)S(1)}, u32[]{:S(2)}, u32[]{:S(2)}) collective-permute-start(bf16[3072,256]{1,0:T(8,128)(2,1)} %constant_dynamic-update-slice_fusion.refs_0_), channel_id=1, source_target_pairs={{0,32},{8,40},{16,48},{24,56},{32,64},{40,72},{48,80},{56,88},{64,... | collective-permute-start | bytes 4718600 | tf_op jit(solution)/shard_map/ppermute | solution.py:306
  30.8 88.0 %collective-permute-start.22 = (bf16[3072,256]{1,0:T(8,128)(2,1)}, bf16[3072,256]{1,0:T(8,128)(2,1)S(1)}, u32[]{:S(2)}, u32[]{:S(2)}) collective-permute-start(bf16[3072,256]{1,0:T(8,128)(2,1)} %constant_dynamic-update-slice_fusion.5.refs_2_), channel_id=1, source_target_pairs={{0,8},{8,16},{16,24},{24,0},{32,40},{40,48},{48,56},{56,32},{64,72... | collective-permute-start | bytes 4718600 | tf_op jit(solution)/shard_map/ppermute | solution.py:306
  38.5 26.1 %collective-permute-start.13 = (bf16[136,1024]{1,0:T(8,128)(2,1)S(1)}, bf16[136,1024]{1,0:T(8,128)(2,1)S(1)}, u32[]{:S(2)}, u32[]{:S(2)}) collective-permute-start(bf16[136,1024]{1,0:T(8,128)(2,1)S(1)} %get-tuple-element.61), channel_id=1, source_target_pairs={{0,32},{8,40},{16,48},{24,56},{32,0},{40,8},{48,16},{56,24},{64,96... | collective-permute-start | bytes 835592 | tf_op jit(solution)/shard_map/ppermute | solution.py:311
  40.5 34.0 %collective-permute-start.2 = (bf16[512,256]{1,0:T(8,128)(2,1)S(1)}, bf16[512,256]{1,0:T(8,128)(2,1)S(1)}, u32[]{:S(2)}, u32[]{:S(2)}) collective-permute-start(bf16[512,256]{1,0:T(8,128)(2,1)S(1)} %slice.193), channel_id=1, source_target_pairs={{0,8},{8,16},{16,24},{24,0},{32,40},{40,48},{48,56},{56,32},{64,72... | collective-permute-start | bytes 786440 | tf_op jit(solution)/shard_map/ppermute | solution.py:306
  40.6 35.7 %collective-permute-start.3 = (bf16[512,256]{1,0:T(8,128)(2,1)S(1)}, bf16[512,256]{1,0:T(8,128)(2,1)S(1)}, u32[]{:S(2)}, u32[]{:S(2)}) collective-permute-start(bf16[512,256]{1,0:T(8,128)(2,1)S(1)} %slice.194), channel_id=1, source_target_pairs={{0,24},{8,0},{16,8},{24,16},{32,56},{40,32},{48,40},{56,48},{64,88... | collective-permute-start | bytes 786440 | tf_op jit(solution)/shard_map/ppermute | solution.py:306
  78.6 23.0 %collective-permute-start.19 = (bf16[1024,256]{1,0:T(8,128)(2,1)S(1)}, bf16[1024,256]{1,0:T(8,128)(2,1)S(1)}, u32[]{:S(2)}, u32[]{:S(2)}) collective-permute-start(bf16[1024,256]{1,0:T(8,128)(2,1)S(1)} %constant_dynamic-update-slice_fusion.3.refs_1_), channel_id=1, source_target_pairs={{0,32},{8,40},{16,48},{24,56},{32,64},{40,72},{48,80},{56,88},{64,... | collective-permute-start | bytes 1572872 | tf_op jit(solution)/shard_map/ppermute | solution.py:306
  101.6 39.0 %collective-permute-start.20 = (bf16[3072,256]{1,0:T(8,128)(2,1)}, bf16[3072,256]{1,0:T(8,128)(2,1)}, u32[]{:S(2)}, u32[]{:S(2)}) collective-permute-start(bf16[3072,256]{1,0:T(8,128)(2,1)} %constant_dynamic-update-slice_fusion.refs_0_), channel_id=1, source_target_pairs={{0,96},{8,104},{16,112},{24,120},{32,0},{40,8},{48,16},{56,24},{64... | collective-permute-start | bytes 4718600 | tf_op jit(solution)/shard_map/ppermute | solution.py:306
  103.7 46.7 %collective-permute-start.24 = (bf16[3072,256]{1,0:T(8,128)(2,1)}, bf16[3072,256]{1,0:T(8,128)(2,1)}, u32[]{:S(2)}, u32[]{:S(2)}) collective-permute-start(bf16[3072,256]{1,0:T(8,128)(2,1)} %constant_dynamic-update-slice_fusion.5.refs_2_), channel_id=1, source_target_pairs={{0,24},{8,0},{16,8},{24,16},{32,56},{40,32},{48,40},{56,48},{64,88... | collective-permute-start | bytes 4718600 | tf_op jit(solution)/shard_map/ppermute | solution.py:306
  116.9 47.7 %collective-permute-start.23 = (bf16[1024,256]{1,0:T(8,128)(2,1)}, bf16[1024,256]{1,0:T(8,128)(2,1)}, u32[]{:S(2)}, u32[]{:S(2)}) collective-permute-start(bf16[1024,256]{1,0:T(8,128)(2,1)} %constant_dynamic-update-slice_fusion.8.refs_3_), channel_id=1, source_target_pairs={{0,8},{8,16},{16,24},{24,0},{32,40},{40,48},{48,56},{56,32},{64,72... | collective-permute-start | bytes 1572872 | tf_op jit(solution)/shard_map/ppermute | solution.py:306
  117.9 46.7 %collective-permute-start.32 = (bf16[1024,256]{1,0:T(8,128)(2,1)}, bf16[1024,256]{1,0:T(8,128)(2,1)}, u32[]{:S(2)}, u32[]{:S(2)}) collective-permute-start(bf16[1024,256]{1,0:T(8,128)(2,1)} %collective-permute-done.21.refs_3_), channel_id=1, source_target_pairs={{0,96},{8,104},{16,112},{24,120},{32,0},{40,8},{48,16},{56,24},{64... | collective-permute-start | bytes 1572872 | tf_op jit(solution)/shard_map/ppermute | solution.py:306
  118.8 46.5 %collective-permute-start.35 = (bf16[1024,256]{1,0:T(8,128)(2,1)}, bf16[1024,256]{1,0:T(8,128)(2,1)}, u32[]{:S(2)}, u32[]{:S(2)}) collective-permute-start(bf16[1024,256]{1,0:T(8,128)(2,1)} %collective-permute-done.25.refs_7_), channel_id=1, source_target_pairs={{0,24},{8,0},{16,8},{24,16},{32,56},{40,32},{48,40},{56,48},{64,88... | collective-permute-start | bytes 1572872 | tf_op jit(solution)/shard_map/ppermute | solution.py:306
  140.6 45.9 %collective-permute-start.30 = (bf16[2048,256]{1,0:T(8,128)(2,1)}, bf16[2048,256]{1,0:T(8,128)(2,1)S(1)}, u32[]{:S(2)}, u32[]{:S(2)}) collective-permute-start(bf16[2048,256]{1,0:T(8,128)(2,1)} %slice.205), channel_id=1, source_target_pairs={{0,32},{8,40},{16,48},{24,56},{32,64},{40,72},{48,80},{56,88},{64,... | collective-permute-start | bytes 3145736 | tf_op jit(solution)/shard_map/ppermute | solution.py:306
  150.4 36.1 %collective-permute-start.33 = (bf16[2048,256]{1,0:T(8,128)(2,1)}, bf16[2048,256]{1,0:T(8,128)(2,1)S(1)}, u32[]{:S(2)}, u32[]{:S(2)}) collective-permute-start(bf16[2048,256]{1,0:T(8,128)(2,1)} %slice.207), channel_id=1, source_target_pairs={{0,8},{8,16},{16,24},{24,0},{32,40},{40,48},{48,56},{56,32},{64,72... | collective-permute-start | bytes 3145736 | tf_op jit(solution)/shard_map/ppermute | solution.py:306
  164.6 41.6 %collective-permute-start.14 = (bf16[256,2048]{1,0:T(8,128)(2,1)}, bf16[256,2048]{1,0:T(8,128)(2,1)S(1)}, u32[]{:S(2)}, u32[]{:S(2)}) collective-permute-start(bf16[256,2048]{1,0:T(8,128)(2,1)} %get-tuple-element.33), channel_id=1, source_target_pairs={{0,1},{1,0},{2,3},{3,2},{4,5},{5,4},{6,7},{7,6},{8,9},{9,8},{10,11... | collective-permute-start | bytes 3145736 | tf_op jit(solution)/shard_map/ppermute | solution.py:311
  164.6 21.9 %collective-permute-start.31 = (bf16[1024,256]{1,0:T(8,128)(2,1)}, bf16[1024,256]{1,0:T(8,128)(2,1)}, u32[]{:S(2)}, u32[]{:S(2)}) collective-permute-start(bf16[1024,256]{1,0:T(8,128)(2,1)} %slice.206), channel_id=1, source_target_pairs={{0,96},{8,104},{16,112},{24,120},{32,0},{40,8},{48,16},{56,24},{64... | collective-permute-start | bytes 1572872 | tf_op jit(solution)/shard_map/ppermute | solution.py:306
  165.3 21.2 %collective-permute-start.34 = (bf16[1024,256]{1,0:T(8,128)(2,1)}, bf16[1024,256]{1,0:T(8,128)(2,1)}, u32[]{:S(2)}, u32[]{:S(2)}) collective-permute-start(bf16[1024,256]{1,0:T(8,128)(2,1)} %slice.208), channel_id=1, source_target_pairs={{0,24},{8,0},{16,8},{24,16},{32,56},{40,32},{48,40},{56,48},{64,88... | collective-permute-start | bytes 1572872 | tf_op jit(solution)/shard_map/ppermute | solution.py:306
  209.0 54.3 %collective-permute-start.26 = (bf16[256,4096]{1,0:T(8,128)(2,1)}, bf16[256,4096]{1,0:T(8,128)(2,1)}, u32[]{:S(2)}, u32[]{:S(2)}) collective-permute-start(bf16[256,4096]{1,0:T(8,128)(2,1)} %get-tuple-element.36), channel_id=1, source_target_pairs={{0,1},{1,0},{2,3},{3,2},{4,5},{5,4},{6,7},{7,6},{8,9},{9,8},{10,11... | collective-permute-start | bytes 6291464 | tf_op jit(solution)/shard_map/ppermute | solution.py:311
  222.5 22.1 %collective-permute-start.45 = (bf16[168,1024]{1,0:T(8,128)(2,1)}, bf16[168,1024]{1,0:T(8,128)(2,1)S(1)}, u32[]{:S(2)}, u32[]{:S(2)}) collective-permute-start(bf16[168,1024]{1,0:T(8,128)(2,1)} %get-tuple-element.79), channel_id=1, source_target_pairs={{0,32},{8,40},{16,48},{24,56},{32,0},{40,8},{48,16},{56,24},{64,96... | collective-permute-start | bytes 1032200 | tf_op jit(solution)/shard_map/ppermute | solution.py:311
  228.2 40.6 %collective-permute-start.15 = (bf16[64,2048]{1,0:T(8,128)(2,1)}, bf16[64,2048]{1,0:T(8,128)(2,1)}, u32[]{:S(2)}, u32[]{:S(2)}) collective-permute-start(bf16[64,2048]{1,0:T(8,128)(2,1)} %get-tuple-element.69), channel_id=1, source_target_pairs={{0,2},{1,3},{2,0},{3,1},{4,6},{5,7},{6,4},{7,5},{8,10},{9,11},{10,... | collective-permute-start | bytes 786440 | tf_op jit(solution)/shard_map/ppermute | solution.py:311
  276.6 37.9 %collective-permute-start.27 = (bf16[64,4096]{1,0:T(8,128)(2,1)S(1)}, bf16[64,4096]{1,0:T(8,128)(2,1)S(1)}, u32[]{:S(2)}, u32[]{:S(2)}) collective-permute-start(bf16[64,4096]{1,0:T(8,128)(2,1)S(1)} %get-tuple-element.56), channel_id=1, source_target_pairs={{0,2},{1,3},{2,0},{3,1},{4,6},{5,7},{6,4},{7,5},{8,10},{9,11},{10,... | collective-permute-start | bytes 1572872 | tf_op jit(solution)/shard_map/ppermute | solution.py:311
  278.6 35.9 %collective-permute-start.28 = (bf16[64,4096]{1,0:T(8,128)(2,1)S(1)}, bf16[64,4096]{1,0:T(8,128)(2,1)S(1)}, u32[]{:S(2)}, u32[]{:S(2)}) collective-permute-start(bf16[64,4096]{1,0:T(8,128)(2,1)S(1)} %get-tuple-element.55), channel_id=1, source_target_pairs={{0,4},{1,5},{2,6},{3,7},{4,0},{5,1},{6,2},{7,3},{8,12},{9,13},{10,... | collective-permute-start | bytes 1572872 | tf_op jit(solution)/shard_map/ppermute | solution.py:311
  278.7 35.8 %collective-permute-start.29 = (bf16[64,4096]{1,0:T(8,128)(2,1)S(1)}, bf16[64,4096]{1,0:T(8,128)(2,1)S(1)}, u32[]{:S(2)}, u32[]{:S(2)}) collective-permute-start(bf16[64,4096]{1,0:T(8,128)(2,1)S(1)} %get-tuple-element.54), channel_id=1, source_target_pairs={{0,6},{1,7},{2,4},{3,5},{4,2},{5,3},{6,0},{7,1},{8,14},{9,15},{10,... | collective-permute-start | bytes 1572872 | tf_op jit(solution)/shard_map/ppermute | solution.py:311
  282.0 26.4 %collective-permute-start.38 = (bf16[64,2048]{1,0:T(8,128)(2,1)}, bf16[64,2048]{1,0:T(8,128)(2,1)S(1)}, u32[]{:S(2)}, u32[]{:S(2)}) collective-permute-start(bf16[64,2048]{1,0:T(8,128)(2,1)} %get-tuple-element.64), channel_id=1, source_target_pairs={{0,4},{1,5},{2,6},{3,7},{4,0},{5,1},{6,2},{7,3},{8,12},{9,13},{10,... | collective-permute-start | bytes 786440 | tf_op jit(solution)/shard_map/ppermute | solution.py:311
  282.8 31.6 %collective-permute-start.39 = (bf16[64,2048]{1,0:T(8,128)(2,1)}, bf16[64,2048]{1,0:T(8,128)(2,1)S(1)}, u32[]{:S(2)}, u32[]{:S(2)}) collective-permute-start(bf16[64,2048]{1,0:T(8,128)(2,1)} %get-tuple-element.63), channel_id=1, source_target_pairs={{0,6},{1,7},{2,4},{3,5},{4,2},{5,3},{6,0},{7,1},{8,14},{9,15},{10,... | collective-permute-start | bytes 786440 | tf_op jit(solution)/shard_map/ppermute | solution.py:311
  (64 other events, 700.1 us)
where the time goes:
time: 324 us; the launch traced here: 320 us
  waiting for transfers between devices  107 us (33%)
  Pallas kernels  78.7 us (24%)
  starting transfers between devices  78.3 us (24%)
  local copies, waits for them, and re-layouts  29.9 us (9%)
  other arithmetic  17.7 us (5%)
  between operations  8.98 us (3%)
    ppermute x33, waiting for transfers between devices, swap(): lax.ppermute(value, name, [(d, d ^ shift) for d in range(lax.axis_size(na...  79.3 us
    ppermute x33, starting transfers between devices, swap(): lax.ppermute(value, name, [(d, d ^ shift) for d in range(lax.axis_size(na...  44.6 us
    pallas_call x3, Pallas kernels, multiply_pieces(): pl.pallas_call(kernel, grid_spec=pltpu.PrefetchScalarGridSpec(num_scalar_...  35.6 us
    ppermute x22, starting transfers between devices, ring(): return lax.ppermute(value, 'ctx', pairs)  33.7 us
    ppermute x22, waiting for transfers between devices, ring(): return lax.ppermute(value, 'ctx', pairs)  27.3 us
    pallas_call x1, Pallas kernels, on_device(): backward(place, acc, act, act, conv, mspec, fspec, skip_row, fwd, inv_now...  14 us
    unnamed x74, local copies, waits for them, and re-layouts  10.7 us
    pallas_call x1, Pallas kernels, on_device(): forward(order, projected, left, short_filter, long_filter, skip_row, fwd,...  10.1 us
  transfers between devices with their start and end apart: 55, of which 13 were waited for; matrix products, arithmetic and copies ran while one was open for 12% of the time, Pallas kernels for 23%

commit v1 on v0

--- a/solution.py
+++ b/solution.py
@@ -78,17 +78,21 @@
         act[m] = total
     filt = spectrum(fmat, lf[...])
     fspec[...] = filt
-    before = spectrum(fmat, halo[:BLK])
-    for b in range(rows // BLK):
+    nb, wide = rows // BLK, filt.shape[1]
+    mixins = [
+        (act[1, b * BLK : (b + 1) * BLK] * act[2, b * BLK : (b + 1) * BLK]).astype(bf16)
+        for b in range(nb)
+    ]
+    spec = spectrum(fmat, jnp.concatenate([halo[:BLK]] + mixins, 1))
+    window = spec[:, : nb * wide] + delay(spec[:, wide:])
+    out = invert(imat, product(window, jnp.concatenate([filt] * nb, 1)))
+    for b in range(nb):
         span = slice(b * BLK, (b + 1) * BLK)
-        mixin = (act[1, span] * act[2, span]).astype(bf16)
-        here = spectrum(fmat, mixin)
-        window = before + delay(here)
-        before = here
-        mspec[b] = window
-        out = invert(imat, product(filt, window)) + skip[...] * mixin.astype(f32)
-        conv[span] = out
-        gate = (act[0, span] * out).astype(bf16)
+        lanes = slice(b * wide, (b + 1) * wide)
+        mspec[b] = window[:, lanes]
+        full = out[:, lanes] + skip[...] * mixins[b].astype(f32)
+        conv[span] = full
+        gate = (act[0, span] * full).astype(bf16)
         for half in range(2):
             start = pl.multiple_of(order[2 * b + half], BLK // 2)
             gated[pl.ds(start, BLK // 2)] = gate[half * (BLK // 2) : (half + 1) * (BLK // 2)]
@@ -96,35 +100,34 @@
 
 def backward_kernel(place, acc, act0, act12, convh, mspec, fspec, skip, fwd, inv, invlag, *refs):
     og, refs = refs[: 2 * SIDE], refs[2 * SIDE :]
-    weights, (bg, pay0, pay1, pay2, pay3, gmix, lagbuf) = refs[:6], refs[6:]
+    weights, (bg, pay0, pay1, pay2, pay3, gmix, lagbuf) = refs[:4], refs[4:]
     rows = bg.shape[0]
     nb = rows // BLK
     fmat, imat = fwd[...], inv[...]
     filt = fspec[...]
-    blocks = []
-    for first, second, third in (weights[:3], weights[3:]):
-        blocks += [first[0], first[1], second[...], third[...]]
+    blocks = [w[n] for w in weights for n in range(2)]
     bg[...] = acc[...] + lax.dot_general(
         jnp.concatenate([o[...] for o in og], 1),
         jnp.concatenate(blocks, 1),
         (((1,), (1,)), ((), ())),
         preferred_element_type=f32,
     )
-    grads, specs = [], []
-    lag = jnp.zeros(filt.shape, f32)
+    wide = filt.shape[1]
+    grads = [
+        (bg[b * BLK : (b + 1) * BLK] * act0[0, b * BLK : (b + 1) * BLK]).astype(bf16)
+        for b in range(nb)
+    ]
+    spec = spectrum(fmat, jnp.concatenate(grads, 1))
+    lag = product_conj(spec[:, :wide], mspec[0])
+    for b in range(1, nb):
+        lag = lag + product_conj(spec[:, b * wide : (b + 1) * wide], mspec[b])
+    lagbuf[...] = invert(invlag[...], lag)
+    following = jnp.concatenate([spec[:, wide:], jnp.zeros(filt.shape, f32)], 1)
+    window = spec + delay(following)
+    out = invert(imat, product_conj(window, jnp.concatenate([filt] * nb, 1)))
     for b in range(nb):
-        span = slice(b * BLK, (b + 1) * BLK)
-        g = (bg[span] * act0[0, span]).astype(bf16)
-        here = spectrum(fmat, g)
-        lag = lag + product_conj(here, mspec[b])
-        grads.append(g)
-        specs.append(here)
-    lagbuf[...] = invert(invlag[...], lag)
-    for b in range(nb):
-        span = slice(b * BLK, (b + 1) * BLK)
-        window = specs[b] + delay(specs[b + 1]) if b + 1 < nb else specs[b]
-        gm = invert(imat, product_conj(window, filt)) + skip[...] * grads[b].astype(f32)
-        gmix[span] = gm
+        gm = out[:, b * wide : (b + 1) * wide] + skip[...] * grads[b].astype(f32)
+        gmix[b * BLK : (b + 1) * BLK] = gm
         if b == 0:
             head = gm[:PAD]
             ga0 = bg[:PAD] * convh[...]
@@ -181,77 +184,74 @@
     short[...] = short_in[...] + finish_body(bg, conv, gfull, act, proj, sf, extra, gp, ext)
 
 
-def pieces_kernel(layout, first, back, *refs):
-    nw = sum(len(counts) for counts in layout)
-    weights, refs = refs[:nw], refs[nw:]
-    gated, refs = refs[0], refs[1:]
+def pieces_kernel(steps, back, *refs):
+    weights, refs = refs[: 2 * steps], refs[2 * steps :]
     if back:
-        og, refs = refs[:SIDE], refs[SIDE:]
-        if not first:
-            acc_in, refs = refs[0], refs[1:]
-        mine, other, acc, buf = refs
+        gated, og, (mine, other, acc, buf, sems) = refs[0], refs[1 : 1 + SIDE], refs[1 + SIDE :]
     else:
-        mine, other, buf = refs
+        gated, mine, other, buf, sems = refs
     step = pl.program_id(0)
-    if back:
-
-        @pl.when(step == 0)
-        def _():
-            acc[...] = jnp.zeros_like(acc) if first else acc_in[...]
-
-    chans = gated.shape[1]
-    half = gated.shape[0] // 2
-    begin = 0
-    for i, counts in enumerate(layout):
-        part = weights[begin : begin + len(counts)]
-        begin += len(counts)
+    chans, half = gated.shape[1], gated.shape[0] // 2
+    width = buf.shape[2] // SIDE
+
+    def copies(i):
+        return [
+            pltpu.make_async_copy(
+                weights[2 * i + j // 2].at[pl.ds((j % 2) * chans, chans)],
+                buf.at[i % 2, :, pl.ds(j * width, width)],
+                sems.at[i % 2, j],
+            )
+            for j in range(SIDE)
+        ]
+
+    @pl.when(step == 0)
+    def _():
+        for c in copies(0):
+            c.start()
+        if back:
+            acc[...] = jnp.zeros_like(acc)
+
+    for i in range(steps):
 
         @pl.when(step == i)
-        def _(part=part, counts=counts):
-            at = 0
-            for r, c in zip(part, counts):
-                for n in range(c):
-                    buf[:, at : at + r.shape[1]] = r[n * chans : (n + 1) * chans]
-                    at += r.shape[1]
-
-    out = jnp.dot(gated[...], buf[...], preferred_element_type=f32).astype(bf16)
+        def _(i=i):
+            if i + 1 < steps:
+                for c in copies(i + 1):
+                    c.start()
+            for c in copies(i):
+                c.wait()
+
+    w = buf[step % 2]
+    out = jnp.dot(gated[...], w, preferred_element_type=f32).astype(bf16)
     mine[...] = out[:half]
     other[...] = out[half:]
     if back:
         acc[...] += lax.dot_general(
             jnp.concatenate([o[...] for o in og], 1),
-            buf[...],
+            w,
             (((1,), (1,)), ((), ())),
             preferred_element_type=f32,
         )
 
 
-def multiply_pieces(groups, cols, gated, out_grad, acc, back=True):
+def multiply_pieces(weights, cols, gated, out_grad, back):
     rows, chans = gated.shape
-    width = groups[0][0].shape[1]
-    layout = [tuple(w.shape[0] // chans for w in group) for group in groups]
-    steps = len(groups)
-    first = acc is None
-    one = pl.Buffered(1)
-    weights = [w for group in groups for w in group]
-    in_specs = [pl.BlockSpec(w.shape, lambda i, c: (0, 0), pipeline_mode=one) for w in weights]
-    whole = pl.BlockSpec((rows, chans), lambda i, c: (0, 0), pipeline_mode=one)
-    in_specs.append(whole)
+    width = weights[0].shape[1]
+    steps = len(weights) // 2
+    whole = pl.BlockSpec((rows, chans), lambda i, c: (0, 0), pipeline_mode=pl.Buffered(1))
+    in_specs = [pl.BlockSpec(memory_space=pl.ANY)] * len(weights) + [whole]
     operands = [*weights, gated]
     if back:
         in_specs += [
             pl.BlockSpec((rows, width), lambda i, c, j=j: (0, c[SIDE * i + j])) for j in range(SIDE)
         ]
         operands += [out_grad] * SIDE
-        if not first:
-            in_specs.append(whole)
-            operands.append(acc)
     half_shape = jax.ShapeDtypeStruct((rows // 2, steps * SIDE * width), bf16)
     half_spec = pl.BlockSpec((rows // 2, SIDE * width), lambda i, c: (0, i))
 
     def kernel(cols_ref, *refs):
         del cols_ref
-        pieces_kernel(layout, first, back, *refs)
+        pieces_kernel(steps, back, *refs)
 
     return pl.pallas_call(
         kernel,
@@ -260,12 +260,15 @@
             grid=(steps,),
             in_specs=in_specs,
             out_specs=[half_spec, half_spec] + [whole] * back,
-            scratch_shapes=[pltpu.VMEM((chans, SIDE * width), bf16)],
+            scratch_shapes=[
+                pltpu.VMEM((2, chans, SIDE * width), bf16),
+                pltpu.SemaphoreType.DMA((2, SIDE)),
+            ],
         ),
         out_shape=[half_shape, half_shape] + [jax.ShapeDtypeStruct((rows, chans), f32)] * back,
         cost_estimate=pl.CostEstimate(
             flops=(2 + 2 * back) * rows * chans * width * SIDE * steps,
-            bytes_accessed=SIDE * steps * (2 * chans * width + 4 * rows * width) + 10 * rows * chans,
+            bytes_accessed=SIDE * steps * (2 * chans * width + 4 * rows * width) + 6 * rows * chans,
             transcendentals=0,
         ),
         name="pieces",
@@ -310,17 +313,15 @@
         name = "ctx" if axis in "xz" else "tp"
         return lax.ppermute(value, name, [(d, d ^ shift) for d in range(lax.axis_size(name))])
 
-    def gather(piece, first, second):
-        h = piece.shape[0] // 2
+    def gather(piece, first, second, turn):
         p, q = ring(piece, first, 1), ring(piece, first, -1)
-        t, b = ring(p[:h], first, 1), ring(q[h:], first, -1)
-        line = jnp.concatenate([piece, p, q], 0)
-        lp, lq = ring(line, second, 1), ring(line, second, -1)
-        far = jnp.concatenate([t, b], 0)
-        fp, fq = ring(far, second, 1), ring(far, second, -1)
-        ft, fb = ring(lp[: 4 * h], second, 1), ring(lq[4 * h :], second, -1)
-        ff = ring(fq, second, -1)
-        return [line, far], [[lp, fp], [lq, fq]], [ft, fb, ff]
+        r = ring(p if turn > 0 else q, first, turn)
+        one, two = jnp.concatenate([piece, p], 0), jnp.concatenate([q, r], 0)
+        op, oq = ring(one, second, 1), ring(one, second, -1)
+        tp_, tq = ring(two, second, 1), ring(two, second, -1)
+        far_one = ring(op, second, 1)
+        far_two = ring(tq, second, -1)
+        return [one, two], [op, tp_, oq, tq], [far_one, far_two]
 
     def blocks(half, near, far_steps):
         out = []
@@ -331,8 +332,10 @@
         return out
 
     order4 = (0, -1, 1, 2)
-    cols1 = jnp.stack(blocks(0, order4, (0,)) + blocks(1, order4, (0,)))
-    cols2 = jnp.stack(blocks(0, order4, (-1, 1)) + blocks(1, order4, (-1, 1)))
+    cols1 = jnp.stack(
+        blocks(0, order4, (0,)) + blocks(1, order4, (0,))
+        + blocks(0, order4, (-1, 1)) + blocks(1, order4, (-1, 1))
+    )
     cols3 = jnp.stack(blocks(0, order4, (2,)) + blocks(1, order4, (2,)))
 
     positions = jnp.arange(ctx_count, dtype=jnp.int32)
@@ -381,8 +384,8 @@
     left = landed(got, left_source)
 
     wa, wb, _ = lax.optimization_barrier((out_weight[:, :width], out_weight[:, width:], sent))
-    near_a, mid_a, far_a = gather(wa, "x", "z")
-    near_b, mid_b, far_b = gather(wb, "z", "x")
+    near_a, mid_a, far_a = gather(wa, "x", "z", 1)
+    near_b, mid_b, far_b = gather(wb, "z", "x", -1)
 
     fwd = jnp.asarray(forward_matrix())
     inv_late, inv_now, inv_lag = (jnp.asarray(inverse_matrix(s)) for s in (BLK, 0, -BLK))
@@ -435,18 +438,16 @@
         parts = [total[k * share : (k + 1) * share] for k in range(SIDE)]
         return [parts[0]] + [swap(parts[k], "y", k) for k in (1, 2, 3)]
 
-    mine1, other1, acc = multiply_pieces([near_a, near_b], cols1, gated, out_grad, None)
+    mine1, other1, acc = multiply_pieces(
+        near_a + near_b + mid_a + mid_b, cols1, gated, out_grad, True
+    )
     out1 = scatter(mine1, other1)
-    mine2, other2, acc = multiply_pieces(mid_a + mid_b, cols2, gated, out_grad, acc)
-    out2 = scatter(mine2, other2)
 
     quarter = BLK // SIDE
     place = jnp.concatenate([jnp.reshape(xi, (1,)), cols3]).astype(jnp.int32)
 
     def third(w):
         count = w.shape[0] // chans
-        if count == 1:
-            return w, pl.BlockSpec((tile, width), lambda i, c: (i, 0))
         return w.reshape(count, chans, width), pl.BlockSpec(
             (count, tile, width), lambda i, c: (0, i, 0)
         )
@@ -506,7 +507,7 @@
     sums = [g[BLK + PAD :].astype(f32) for g in got]
     my_quarter = (sums[0] + sums[1]) + (sums[2] + sums[3])
 
-    mine3, other3 = multiply_pieces([far_a, far_b], cols3, gated, None, None, back=False)
+    mine3, other3 = multiply_pieces(far_a + far_b, cols3, gated, None, False)
     out3 = scatter(mine3, other3)
 
     low = rows - BLK - PAD
@@ -562,22 +563,22 @@
         bg, conv, gmix, act, right, projected, short_filter, fspec, fwd, inv_now, short, gp
     )
 
-    got = along_x([my_quarter] * SIDE)
-    long_total = jnp.concatenate([pick(got, xi ^ q) for q in range(SIDE)], 0)
-    sums = along_x([short] * SIDE)
+    got = along_x([jnp.concatenate([my_quarter, short], 0).astype(bf16)] * SIDE)
+    long_total = jnp.concatenate([pick(got, xi ^ q)[:quarter] for q in range(SIDE)], 0)
+    sums = [g[quarter:].astype(f32) for g in got]
     sums = (sums[0] + sums[1]) + (sums[2] + sums[3])
     sums = along_z([sums] * SIDE)
     short_total = ((sums[0] + sums[1]) + (sums[2] + sums[3]))[:9].reshape(3, 3, chans)
 
-    counts = tuple(o[0].shape[1] // width for o in (out1, out2, out3))
-    mixed = pl.pallas_call(
+    counts = tuple(o[0].shape[1] // width for o in (out1, out3))
+    collect = pl.pallas_call(
         lambda cols, *refs: collect_kernel(counts, cols, *refs),
         grid_spec=pltpu.PrefetchScalarGridSpec(
             num_scalar_prefetch=1,
             grid=(1,),
             in_specs=[
                 pl.BlockSpec(o[0].shape, lambda i, c: (0, 0))
-                for o in (out1, out2, out3)
+                for o in (out1, out3)
                 for _ in range(SIDE)
             ],
             out_specs=pl.BlockSpec((share, 2 * width * ctx_count), lambda i, c: (0, 0)),
@@ -585,10 +586,11 @@
         out_shape=jax.ShapeDtypeStruct((share, 2 * width * ctx_count), bf16),
         cost_estimate=pl.CostEstimate(flops=10_000_000, bytes_accessed=5 << 20, transcendentals=0),
         name="collect",
-    )(jnp.concatenate([cols1, cols2, cols3]), *out1, *out2, *out3)
+    )
+    mixed = collect(jnp.concatenate([cols1, cols3]), *out1, *out3)
 
     scale = 1.0 / math.sqrt(rows * ctx_count)
-    return mixed, gp, long_total * scale, short_total * scale
+    return mixed, gp, long_total.astype(f32) * scale, short_total * scale
 
 
 def solution(mesh):

time: 324 us -> 291 us (0.90)
  starting transfers between devices: 78.3 us -> 59.1 us
  local copies, waits for them, and re-layouts: 29.9 us -> 19 us
  Pallas kernels: 78.7 us -> 69.9 us
    ppermute x22 -> x18, waiting for transfers between devices: 27.3 us -> 49.3 us  [ring(): return lax.ppermute(value, 'ctx', pairs)]
    ppermute x33 -> x26, waiting for transfers between devices: 79.3 us -> 59.7 us  [swap(): lax.ppermute(value, name, [(d, d ^ shift) for d in range(lax.axis_size(na...]
    ppermute x33 -> x26, starting transfers between devices: 44.6 us -> 34.5 us  [swap(): lax.ppermute(value, name, [(d, d ^ shift) for d in range(lax.axis_size(na...]
    ppermute x22 -> x18, starting transfers between devices: 33.7 us -> 24.6 us  [ring(): return lax.ppermute(value, 'ctx', pairs)]
    pallas_call x3 -> x2, Pallas kernels: 35.6 us -> 27 us  [multiply_pieces(): pl.pallas_call(kernel, grid_spec=pltpu.PrefetchScalarGridSpec(num_scalar_...]
    slice x8 -> x0, local copies, waits for them, and re-layouts: 6.89 us -> none  [the longest x4 5.86 us: gather(): ft, fb = (ring(lp[:4 * h], second, 1), ring(lq[4 * h:], second, -1))]
    unnamed x74 -> x32, local copies, waits for them, and re-layouts: 10.7 us -> 6.15 us
  transfers between devices with their start and end apart: 55 -> 44, of which waited for: 13 -> 17; matrix products, arithmetic and copies ran while one was open for 12% -> 12% of each run, Pallas kernels for 23% -> 18%
where the time goes in v1:
time: 291 us; the launch traced here: 287 us
  waiting for transfers between devices  109 us (37%)
  Pallas kernels  69.9 us (24%)
  starting transfers between devices  59.1 us (20%)
  other arithmetic  20.9 us (7%)
  local copies, waits for them, and re-layouts  19 us (7%)
  between operations  8.82 us (3%)
    ppermute x26, waiting for transfers between devices, swap(): lax.ppermute(value, name, [(d, d ^ shift) for d in range(lax.axis_size(na...  59.7 us
    ppermute x18, waiting for transfers between devices, ring(): return lax.ppermute(value, 'ctx', pairs)  49.3 us
    ppermute x26, starting transfers between devices, swap(): lax.ppermute(value, name, [(d, d ^ shift) for d in range(lax.axis_size(na...  34.5 us
    pallas_call x2, Pallas kernels, multiply_pieces(): pl.pallas_call(kernel, grid_spec=pltpu.PrefetchScalarGridSpec(num_scalar_...  27 us
    ppermute x18, starting transfers between devices, ring(): return lax.ppermute(value, 'ctx', pairs)  24.6 us
    pallas_call x1, Pallas kernels, on_device(): backward(place, acc, act, act, conv, mspec, fspec, skip_row, fwd, inv_now...  13.8 us
    pallas_call x1, Pallas kernels, on_device(): forward(order, projected, left, short_filter, long_filter, skip_row, fwd,...  10.2 us
    pallas_call x1, Pallas kernels, on_device(): top(bg, conv, gmix, act, bg, conv, gmix, act, projected, short_filter)  8.35 us
  transfers between devices with their start and end apart: 44, of which 17 were waited for; matrix products, arithmetic and copies ran while one was open for 12% of the time, Pallas kernels for 18%

profile of v1, /device:TPU:24, one launch (start us, length us, event | category | flops | bytes accessed | tf_op | source)
XLA Modules:
  0.0 286.8 jit_solution(3572066676714172299)
XLA Ops:
  17.6 4.9 %collective-permute-done.14 = bf16[136,1024]{1,0:T(8,128)(2,1)S(1)} collective-permute-done((bf16[136,1024]{1,0:T(8,128)(2,1)S(1)}, bf16[136,1024]{1,0:T(8,128)(2,1)S(1)}, u32[]{:S(2)}, u32[]{:S(2)}) %collective-permute-start.14) | collective-permute-done | bytes 278560 | tf_op jit(solution)/shard_map/ppermute | solution.py:314
  22.5 4.0 %collective-permute-start.4 = (bf16[1024,256]{1,0:T(8,128)(2,1)S(1)}, bf16[1024,256]{1,0:T(8,128)(2,1)S(1)}, u32[]{:S(2)}, u32[]{:S(2)}) collective-permute-start(bf16[1024,256]{1,0:T(8,128)(2,1)S(1)} %get-tuple-element.27), channel_id=1, source_target_pairs={{0,96},{8,104},{16,112},{24,120},{32,0},{40,8},{48,16},{56,24},{64... | collective-permute-start | bytes 1572872 | tf_op jit(solution)/shard_map/ppermute | solution.py:309
  28.6 3.8 %collective-permute-done = bf16[1024,256]{1,0:T(8,128)(2,1)S(1)} collective-permute-done((bf16[1024,256]{1,0:T(8,128)(2,1)S(1)}, bf16[1024,256]{1,0:T(8,128)(2,1)S(1)}, u32[]{:S(2)}, u32[]{:S(2)}) %collective-permute-start) | collective-permute-done | bytes 524320 | tf_op jit(solution)/shard_map/ppermute | solution.py:309
  32.3 4.0 %collective-permute-start.17 = (bf16[136,1024]{1,0:T(8,128)(2,1)}, bf16[136,1024]{1,0:T(8,128)(2,1)}, u32[]{:S(2)}, u32[]{:S(2)}) collective-permute-start(bf16[136,1024]{1,0:T(8,128)(2,1)} %get-tuple-element.58), channel_id=1, source_target_pairs={{0,96},{8,104},{16,112},{24,120},{32,64},{40,72},{48,80},{56,88},{... | collective-permute-start | bytes 835592 | tf_op jit(solution)/shard_map/ppermute | solution.py:314
  45.5 4.6 %collective-permute-done.17 = bf16[136,1024]{1,0:T(8,128)(2,1)} collective-permute-done((bf16[136,1024]{1,0:T(8,128)(2,1)}, bf16[136,1024]{1,0:T(8,128)(2,1)}, u32[]{:S(2)}, u32[]{:S(2)}) %collective-permute-start.17) | collective-permute-done | bytes 278560 | tf_op jit(solution)/shard_map/ppermute | solution.py:314
  57.8 20.1 %collective-permute-done.2 = bf16[1024,256]{1,0:T(8,128)(2,1)S(1)} collective-permute-done((bf16[1024,256]{1,0:T(8,128)(2,1)S(1)}, bf16[1024,256]{1,0:T(8,128)(2,1)S(1)}, u32[]{:S(2)}, u32[]{:S(2)}) %collective-permute-start.2) | collective-permute-done | bytes 524320 | tf_op jit(solution)/shard_map/ppermute | solution.py:309
  82.4 3.2 %collective-permute-start.9 = (bf16[2048,256]{1,0:T(8,128)(2,1)}, bf16[2048,256]{1,0:T(8,128)(2,1)}, u32[]{:S(2)}, u32[]{:S(2)}) collective-permute-start(bf16[2048,256]{1,0:T(8,128)(2,1)} %constant_dynamic-update-slice_fusion.2.refs_1_), channel_id=1, source_target_pairs={{0,96},{8,104},{16,112},{24,120},{32,0},{40,8},{48,16},{56,24},{64... | collective-permute-start | bytes 3145736 | tf_op jit(solution)/shard_map/ppermute | solution.py:309
  85.6 3.2 %collective-permute-start.13 = (bf16[2048,256]{1,0:T(8,128)(2,1)}, bf16[2048,256]{1,0:T(8,128)(2,1)}, u32[]{:S(2)}, u32[]{:S(2)}) collective-permute-start(bf16[2048,256]{1,0:T(8,128)(2,1)} %constant_dynamic-update-slice_fusion.6.refs_3_), channel_id=1, source_target_pairs={{0,24},{8,0},{16,8},{24,16},{32,56},{40,32},{48,40},{56,48},{64,88... | collective-permute-start | bytes 3145736 | tf_op jit(solution)/shard_map/ppermute | solution.py:309
  88.8 10.2 %forward.1 = (bf16[512,1024]{1,0:T(8,128)(2,1)}, f32[512,1024]{1,0:T(8,128)}, f32[3,512,1024]{2,1,0:T(8,128)}, f32[4,256,1024]{2,1,0:T(8,128)}, f32[256,1024]{1,0:T(8,128)}) custom-call(s32[8]{0:T(128)} %stack.170.order, bf16[3,512,1024]{2,1,0:T(8,128)(2,1)} %proj.5, bf16[136,1024]{1,0:T(8,128)(2,1)} %select_select_fusion.3.halo, f32[3,3,1024]{2,1,0:T(4,128)} %sf.5, ...), custom_call_target="tpu_custom_call" | custom-call | flops 12000000000 | bytes 20971520 | tf_op jit(solution)/shard_map/forward/pallas_call | solution.py:431
  99.1 5.2 %collective-permute-done.12.refs_10_ = bf16[2048,256]{1,0:T(8,128)(2,1)} collective-permute-done((bf16[2048,256]{1,0:T(8,128)(2,1)}, bf16[2048,256]{1,0:T(8,128)(2,1)}, u32[]{:S(2)}, u32[]{:S(2)}) %collective-permute-start.12) | collective-permute-done | bytes 1048608 | tf_op jit(solution)/shard_map/ppermute | solution.py:309
  104.6 4.5 %collective-permute-done.7.refs_5_ = bf16[2048,256]{1,0:T(8,128)(2,1)} collective-permute-done((bf16[2048,256]{1,0:T(8,128)(2,1)}, bf16[2048,256]{1,0:T(8,128)(2,1)}, u32[]{:S(2)}, u32[]{:S(2)}) %collective-permute-start.7) | collective-permute-done | bytes 1048608 | tf_op jit(solution)/shard_map/ppermute | solution.py:309
  111.1 12.6 %collective-permute-done.13.refs_11_ = bf16[2048,256]{1,0:T(8,128)(2,1)} collective-permute-done((bf16[2048,256]{1,0:T(8,128)(2,1)}, bf16[2048,256]{1,0:T(8,128)(2,1)}, u32[]{:S(2)}, u32[]{:S(2)}) %collective-permute-start.13) | collective-permute-done | bytes 1048608 | tf_op jit(solution)/shard_map/ppermute | solution.py:309
  124.3 20.0 %pieces.2 = (bf16[256,6144]{1,0:T(8,128)(2,1)}, bf16[256,6144]{1,0:T(8,128)(2,1)}, f32[512,1024]{1,0:T(8,128)}) custom-call(s32[24]{0:T(128)} %stack.161.cols_ref, bf16[2048,256]{1,0:T(8,128)(2,1)} %constant_dynamic-update-slice_fusion.refs_0_, bf16[2048,256]{1,0:T(8,128)(2,1)} %constant_dynamic-update-slice_fusion.2.refs_1_, ...), custom_call_target="tpu_custom_call" | custom-call | flops 12884901888 | bytes 28311552 | tf_op jit(solution)/shard_map/pieces/pallas_call | solution.py:256
  146.0 13.8 %backward.1 = (f32[512,1024]{1,0:T(8,128)}, bf16[168,1024]{1,0:T(8,128)(2,1)}, bf16[168,1024]{1,0:T(8,128)(2,1)}, bf16[168,1024]{1,0:T(8,128)(2,1)}, bf16[168,1024]{1,0:T(8,128)(2,1)}, /*index=5*/f32[512,1024]{1,0:T(8,128)}) custom-call(s32[9]{0:T(128)} %concatenate.45.place, f32[512,1024]{1,0:T(8,128)} %get-tuple-element.33.acc, ...), custom_call_target="tpu_custom_call" | custom-call | flops 8000000000 | bytes 20971520 | tf_op jit(solution)/shard_map/backward/pallas_call | solution.py:496
  166.1 8.7 %collective-permute-done.32 = bf16[168,1024]{1,0:T(8,128)(2,1)S(1)} collective-permute-done((bf16[168,1024]{1,0:T(8,128)(2,1)}, bf16[168,1024]{1,0:T(8,128)(2,1)S(1)}, u32[]{:S(2)}, u32[]{:S(2)}) %collective-permute-start.32) | collective-permute-done | bytes 344096 | tf_op jit(solution)/shard_map/ppermute | solution.py:314
  181.2 2.8 collective-permute-start.35
  186.6 7.0 %pieces.3 = (bf16[256,2048]{1,0:T(8,128)(2,1)}, bf16[256,2048]{1,0:T(8,128)(2,1)}) custom-call(s32[8]{0:T(128)} %stack.171.cols_ref, bf16[2048,256]{1,0:T(8,128)(2,1)} %copy-done.2, bf16[2048,256]{1,0:T(8,128)(2,1)} %copy-done.4, bf16[2048,256]{1,0:T(8,128)(2,1)} %copy-done.3, bf16[2048,256]{1,0:T(8,128)(2,1)} %collective-permute-done.27.refs_3_, ...), custom_call_target="tpu_custom_call" | custom-call | flops 2147483648 | bytes 11534336 | tf_op jit(solution)/shard_map/pieces/pallas_call | solution.py:256
  193.6 8.3 %top.1 = (bf16[3,512,1024]{2,1,0:T(8,128)(2,1)}, f32[16,1024]{1,0:T(8,128)}) custom-call(f32[512,1024]{1,0:T(8,128)} %get-tuple-element.38.bg.bgn, f32[512,1024]{1,0:T(8,128)} %get-tuple-element.35.convh.conv.convn, f32[512,1024]{1,0:T(8,128)} %get-tuple-element.39.gmix.gmixn, f32[3,512,1024]{2,1,0:T(8,128)} %get-tuple-element.34.act0.act12.act.actn, ...), custom_call_target="tpu_custom_call" | custom-call | flops 200000000 | bytes 10485760 | tf_op jit(solution)/shard_map/top/pallas_call | solution.py:543
  203.1 6.0 %bottom.1 = (bf16[3,512,1024]{2,1,0:T(8,128)(2,1)}, f32[16,1024]{1,0:T(8,128)}) custom-call(f32[512,1024]{1,0:T(8,128)} %get-tuple-element.38.bg.bgn, f32[512,1024]{1,0:T(8,128)} %get-tuple-element.35.convh.conv.convn, f32[512,1024]{1,0:T(8,128)} %get-tuple-element.39.gmix.gmixn, ...), custom_call_target="tpu_custom_call", output_to_operand_aliasing={{0}: (11, {})} | custom-call | flops 2000000000 | bytes 5242880 | tf_op jit(solution)/shard_map/bottom/pallas_call | solution.py:562
  227.2 3.0 %add_convert_fusion = bf16[256,6144]{1,0:T(8,128)(2,1)S(1)} fusion(bf16[256,6144]{1,0:T(8,128)(2,1)} %collective-permute-done.20, bf16[256,6144]{1,0:T(8,128)(2,1)S(1)} %copy-done), kind=kLoop, calls=%fused_computation | loop fusion | flops 6291456 | bytes 9437184 | tf_op jit(solution)/shard_map/convert_element_type | solution.py:437
  237.0 3.0 %collective-permute-start.41 = (f32[16,1024]{1,0:T(8,128)S(1)}, f32[16,1024]{1,0:T(8,128)S(1)}, u32[]{:S(2)}, u32[]{:S(2)}) collective-permute-start(f32[16,1024]{1,0:T(8,128)S(1)} %add_add_fusion), channel_id=1, source_target_pairs={{0,32},{8,40},{16,48},{24,56},{32,0},{40,8},{48,16},{56,24},{64,96... | collective-permute-start | bytes 196616 | tf_op jit(solution)/shard_map/ppermute | solution.py:314
  246.5 26.7 %collective-permute-done.30.refs_6_ = bf16[64,2048]{1,0:T(8,128)(2,1)S(1)} collective-permute-done((bf16[64,2048]{1,0:T(8,128)(2,1)}, bf16[64,2048]{1,0:T(8,128)(2,1)S(1)}, u32[]{:S(2)}, u32[]{:S(2)}) %collective-permute-start.30) | collective-permute-done | bytes 262176 | tf_op jit(solution)/shard_map/ppermute | solution.py:314
  273.2 8.2 %collective-permute-done.31.refs_7_ = bf16[64,2048]{1,0:T(8,128)(2,1)} collective-permute-done((bf16[64,2048]{1,0:T(8,128)(2,1)}, bf16[64,2048]{1,0:T(8,128)(2,1)}, u32[]{:S(2)}, u32[]{:S(2)}) %collective-permute-start.31) | collective-permute-done | bytes 262176 | tf_op jit(solution)/shard_map/ppermute | solution.py:314
  282.3 4.5 %collect.1 = bf16[64,8192]{1,0:T(8,128)(2,1)} custom-call(s32[32]{0:T(128)} %concatenate.39.cols, bf16[64,6144]{1,0:T(8,128)(2,1)} %get-tuple-element.53.refs_0_, bf16[64,6144]{1,0:T(8,128)(2,1)} %copy-done.6, bf16[64,6144]{1,0:T(8,128)(2,1)} %collective-permute-done.22.refs_2_, bf16[64,6144]{1,0:T(8,128)(2,1)} %collective-permute-done.23.refs_3_, ...), custom_call_target="tpu_custom_call" | custom-call | flops 10000000 | bytes 5242880 | tf_op jit(solution)/shard_map/collect/pallas_call | solution.py:590
  (146 shorter events, 85.4 us)
Async XLA Ops:
  8.6 23.7 %collective-permute-start = (bf16[1024,256]{1,0:T(8,128)(2,1)S(1)}, bf16[1024,256]{1,0:T(8,128)(2,1)S(1)}, u32[]{:S(2)}, u32[]{:S(2)}) collective-permute-start(bf16[1024,256]{1,0:T(8,128)(2,1)S(1)} %get-tuple-element.26), channel_id=1, source_target_pairs={{0,8},{8,16},{16,24},{24,0},{32,40},{40,48},{48,56},{56,32},{64,72... | collective-permute-start | bytes 1572872 | tf_op jit(solution)/shard_map/ppermute | solution.py:309
  10.0 27.2 %collective-permute-start.3 = (bf16[1024,256]{1,0:T(8,128)(2,1)S(1)}, bf16[1024,256]{1,0:T(8,128)(2,1)}, u32[]{:S(2)}, u32[]{:S(2)}) collective-permute-start(bf16[1024,256]{1,0:T(8,128)(2,1)S(1)} %get-tuple-element.27), channel_id=1, source_target_pairs={{0,32},{8,40},{16,48},{24,56},{32,64},{40,72},{48,80},{56,88},{64,... | collective-permute-start | bytes 1572872 | tf_op jit(solution)/shard_map/ppermute | solution.py:309
  15.7 23.4 %collective-permute-start.1 = (bf16[1024,256]{1,0:T(8,128)(2,1)S(1)}, bf16[1024,256]{1,0:T(8,128)(2,1)}, u32[]{:S(2)}, u32[]{:S(2)}) collective-permute-start(bf16[1024,256]{1,0:T(8,128)(2,1)S(1)} %get-tuple-element.26), channel_id=1, source_target_pairs={{0,24},{8,0},{16,8},{24,16},{32,56},{40,32},{48,40},{56,48},{64,88... | collective-permute-start | bytes 1572872 | tf_op jit(solution)/shard_map/ppermute | solution.py:309
  39.1 43.3 %collective-permute-start.6 = (bf16[2048,256]{1,0:T(8,128)(2,1)}, bf16[2048,256]{1,0:T(8,128)(2,1)}, u32[]{:S(2)}, u32[]{:S(2)}) collective-permute-start(bf16[2048,256]{1,0:T(8,128)(2,1)} %constant_dynamic-update-slice_fusion.refs_0_), channel_id=1, source_target_pairs={{0,32},{8,40},{16,48},{24,56},{32,64},{40,72},{48,80},{56,88},{64,... | collective-permute-start | bytes 3145736 | tf_op jit(solution)/shard_map/ppermute | solution.py:309
  39.9 45.6 %collective-permute-start.8 = (bf16[2048,256]{1,0:T(8,128)(2,1)}, bf16[2048,256]{1,0:T(8,128)(2,1)}, u32[]{:S(2)}, u32[]{:S(2)}) collective-permute-start(bf16[2048,256]{1,0:T(8,128)(2,1)} %constant_dynamic-update-slice_fusion.refs_0_), channel_id=1, source_target_pairs={{0,96},{8,104},{16,112},{24,120},{32,0},{40,8},{48,16},{56,24},{64... | collective-permute-start | bytes 3145736 | tf_op jit(solution)/shard_map/ppermute | solution.py:309
  42.3 43.3 %collective-permute-start.10 = (bf16[2048,256]{1,0:T(8,128)(2,1)}, bf16[2048,256]{1,0:T(8,128)(2,1)}, u32[]{:S(2)}, u32[]{:S(2)}) collective-permute-start(bf16[2048,256]{1,0:T(8,128)(2,1)} %constant_dynamic-update-slice_fusion.4.refs_2_), channel_id=1, source_target_pairs={{0,8},{8,16},{16,24},{24,0},{32,40},{40,48},{48,56},{56,32},{64,72... | collective-permute-start | bytes 3145736 | tf_op jit(solution)/shard_map/ppermute | solution.py:309
  50.1 27.8 %collective-permute-start.2 = (bf16[1024,256]{1,0:T(8,128)(2,1)S(1)}, bf16[1024,256]{1,0:T(8,128)(2,1)S(1)}, u32[]{:S(2)}, u32[]{:S(2)}) collective-permute-start(bf16[1024,256]{1,0:T(8,128)(2,1)S(1)} %collective-permute-done), channel_id=1, source_target_pairs={{0,8},{8,16},{16,24},{24,0},{32,40},{40,48},{48,56},{56,32},{64,72... | collective-permute-start | bytes 1572872 | tf_op jit(solution)/shard_map/ppermute | solution.py:309
  50.8 30.2 %collective-permute-start.5 = (bf16[1024,256]{1,0:T(8,128)(2,1)S(1)}, bf16[1024,256]{1,0:T(8,128)(2,1)S(1)}, u32[]{:S(2)}, u32[]{:S(2)}) collective-permute-start(bf16[1024,256]{1,0:T(8,128)(2,1)S(1)} %collective-permute-done.4), channel_id=1, source_target_pairs={{0,96},{8,104},{16,112},{24,120},{32,0},{40,8},{48,16},{56,24},{64... | collective-permute-start | bytes 1572872 | tf_op jit(solution)/shard_map/ppermute | solution.py:309
  77.9 26.3 %collective-permute-start.12 = (bf16[2048,256]{1,0:T(8,128)(2,1)}, bf16[2048,256]{1,0:T(8,128)(2,1)}, u32[]{:S(2)}, u32[]{:S(2)}) collective-permute-start(bf16[2048,256]{1,0:T(8,128)(2,1)} %constant_dynamic-update-slice_fusion.4.refs_2_), channel_id=1, source_target_pairs={{0,24},{8,0},{16,8},{24,16},{32,56},{40,32},{48,40},{56,48},{64,88... | collective-permute-start | bytes 3145736 | tf_op jit(solution)/shard_map/ppermute | solution.py:309
  81.0 28.0 %collective-permute-start.7 = (bf16[2048,256]{1,0:T(8,128)(2,1)}, bf16[2048,256]{1,0:T(8,128)(2,1)}, u32[]{:S(2)}, u32[]{:S(2)}) collective-permute-start(bf16[2048,256]{1,0:T(8,128)(2,1)} %constant_dynamic-update-slice_fusion.2.refs_1_), channel_id=1, source_target_pairs={{0,32},{8,40},{16,48},{24,56},{32,64},{40,72},{48,80},{56,88},{64,... | collective-permute-start | bytes 3145736 | tf_op jit(solution)/shard_map/ppermute | solution.py:309
  82.4 26.6 %collective-permute-start.9 = (bf16[2048,256]{1,0:T(8,128)(2,1)}, bf16[2048,256]{1,0:T(8,128)(2,1)}, u32[]{:S(2)}, u32[]{:S(2)}) collective-permute-start(bf16[2048,256]{1,0:T(8,128)(2,1)} %constant_dynamic-update-slice_fusion.2.refs_1_), channel_id=1, source_target_pairs={{0,96},{8,104},{16,112},{24,120},{32,0},{40,8},{48,16},{56,24},{64... | collective-permute-start | bytes 3145736 | tf_op jit(solution)/shard_map/ppermute | solution.py:309
  85.6 38.7 %collective-permute-start.11 = (bf16[2048,256]{1,0:T(8,128)(2,1)}, bf16[2048,256]{1,0:T(8,128)(2,1)}, u32[]{:S(2)}, u32[]{:S(2)}) collective-permute-start(bf16[2048,256]{1,0:T(8,128)(2,1)} %constant_dynamic-update-slice_fusion.6.refs_3_), channel_id=1, source_target_pairs={{0,8},{8,16},{16,24},{24,0},{32,40},{40,48},{48,56},{56,32},{64,72... | collective-permute-start | bytes 3145736 | tf_op jit(solution)/shard_map/ppermute | solution.py:309
  85.6 38.1 %collective-permute-start.13 = (bf16[2048,256]{1,0:T(8,128)(2,1)}, bf16[2048,256]{1,0:T(8,128)(2,1)}, u32[]{:S(2)}, u32[]{:S(2)}) collective-permute-start(bf16[2048,256]{1,0:T(8,128)(2,1)} %constant_dynamic-update-slice_fusion.6.refs_3_), channel_id=1, source_target_pairs={{0,24},{8,0},{16,8},{24,16},{32,56},{40,32},{48,40},{56,48},{64,88... | collective-permute-start | bytes 3145736 | tf_op jit(solution)/shard_map/ppermute | solution.py:309
  104.2 40.1 %collective-permute-start.24 = (bf16[2048,256]{1,0:T(8,128)(2,1)}, bf16[2048,256]{1,0:T(8,128)(2,1)S(1)}, u32[]{:S(2)}, u32[]{:S(2)}) collective-permute-start(bf16[2048,256]{1,0:T(8,128)(2,1)} %collective-permute-done.6.refs_4_), channel_id=1, source_target_pairs={{0,32},{8,40},{16,48},{24,56},{32,64},{40,72},{48,80},{56,88},{64,... | collective-permute-start | bytes 3145736 | tf_op jit(solution)/shard_map/ppermute | solution.py:309
  109.0 35.3 %collective-permute-start.26 = (bf16[2048,256]{1,0:T(8,128)(2,1)}, bf16[2048,256]{1,0:T(8,128)(2,1)S(1)}, u32[]{:S(2)}, u32[]{:S(2)}) collective-permute-start(bf16[2048,256]{1,0:T(8,128)(2,1)} %collective-permute-done.10.refs_8_), channel_id=1, source_target_pairs={{0,8},{8,16},{16,24},{24,0},{32,40},{40,48},{48,56},{56,32},{64,72... | collective-permute-start | bytes 3145736 | tf_op jit(solution)/shard_map/ppermute | solution.py:309
  109.0 35.3 %collective-permute-start.25 = (bf16[2048,256]{1,0:T(8,128)(2,1)}, bf16[2048,256]{1,0:T(8,128)(2,1)S(1)}, u32[]{:S(2)}, u32[]{:S(2)}) collective-permute-start(bf16[2048,256]{1,0:T(8,128)(2,1)} %collective-permute-done.9.refs_7_), channel_id=1, source_target_pairs={{0,96},{8,104},{16,112},{24,120},{32,0},{40,8},{48,16},{56,24},{64... | collective-permute-start | bytes 3145736 | tf_op jit(solution)/shard_map/ppermute | solution.py:309
  166.0 61.2 %collective-permute-start.20 = (bf16[256,6144]{1,0:T(8,128)(2,1)}, bf16[256,6144]{1,0:T(8,128)(2,1)}, u32[]{:S(2)}, u32[]{:S(2)}) collective-permute-start(bf16[256,6144]{1,0:T(8,128)(2,1)} %get-tuple-element.30), channel_id=1, source_target_pairs={{0,1},{1,0},{2,3},{3,2},{4,5},{5,4},{6,7},{7,6},{8,9},{9,8},{10,11... | collective-permute-start | bytes 9437192 | tf_op jit(solution)/shard_map/ppermute | solution.py:314
  179.3 22.7 %collective-permute-start.37 = (bf16[168,1024]{1,0:T(8,128)(2,1)}, bf16[168,1024]{1,0:T(8,128)(2,1)S(1)}, u32[]{:S(2)}, u32[]{:S(2)}) collective-permute-start(bf16[168,1024]{1,0:T(8,128)(2,1)} %get-tuple-element.70), channel_id=1, source_target_pairs={{0,32},{8,40},{16,48},{24,56},{32,0},{40,8},{48,16},{56,24},{64,96... | collective-permute-start | bytes 1032200 | tf_op jit(solution)/shard_map/ppermute | solution.py:314
  193.5 30.1 %collective-permute-start.28 = (bf16[256,2048]{1,0:T(8,128)(2,1)}, bf16[256,2048]{1,0:T(8,128)(2,1)}, u32[]{:S(2)}, u32[]{:S(2)}) collective-permute-start(bf16[256,2048]{1,0:T(8,128)(2,1)} %get-tuple-element.32), channel_id=1, source_target_pairs={{0,1},{1,0},{2,3},{3,2},{4,5},{5,4},{6,7},{7,6},{8,9},{9,8},{10,11... | collective-permute-start | bytes 3145736 | tf_op jit(solution)/shard_map/ppermute | solution.py:314
  231.4 50.0 %collective-permute-start.21 = (bf16[64,6144]{1,0:T(8,128)(2,1)S(1)}, bf16[64,6144]{1,0:T(8,128)(2,1)S(1)}, u32[]{:S(2)}, u32[]{:S(2)}) collective-permute-start(bf16[64,6144]{1,0:T(8,128)(2,1)S(1)} %get-tuple-element.52), channel_id=1, source_target_pairs={{0,2},{1,3},{2,0},{3,1},{4,6},{5,7},{6,4},{7,5},{8,10},{9,11},{10,... | collective-permute-start | bytes 2359304 | tf_op jit(solution)/shard_map/ppermute | solution.py:314
  232.7 48.7 %collective-permute-start.22 = (bf16[64,6144]{1,0:T(8,128)(2,1)S(1)}, bf16[64,6144]{1,0:T(8,128)(2,1)}, u32[]{:S(2)}, u32[]{:S(2)}) collective-permute-start(bf16[64,6144]{1,0:T(8,128)(2,1)S(1)} %get-tuple-element.51), channel_id=1, source_target_pairs={{0,4},{1,5},{2,6},{3,7},{4,0},{5,1},{6,2},{7,3},{8,12},{9,13},{10,... | collective-permute-start | bytes 2359304 | tf_op jit(solution)/shard_map/ppermute | solution.py:314
  233.9 47.5 %collective-permute-start.23 = (bf16[64,6144]{1,0:T(8,128)(2,1)S(1)}, bf16[64,6144]{1,0:T(8,128)(2,1)}, u32[]{:S(2)}, u32[]{:S(2)}) collective-permute-start(bf16[64,6144]{1,0:T(8,128)(2,1)S(1)} %get-tuple-element.50), channel_id=1, source_target_pairs={{0,6},{1,7},{2,4},{3,5},{4,2},{5,3},{6,0},{7,1},{8,14},{9,15},{10,... | collective-permute-start | bytes 2359304 | tf_op jit(solution)/shard_map/ppermute | solution.py:314
  242.2 31.0 %collective-permute-start.30 = (bf16[64,2048]{1,0:T(8,128)(2,1)}, bf16[64,2048]{1,0:T(8,128)(2,1)S(1)}, u32[]{:S(2)}, u32[]{:S(2)}) collective-permute-start(bf16[64,2048]{1,0:T(8,128)(2,1)} %get-tuple-element.60), channel_id=1, source_target_pairs={{0,4},{1,5},{2,6},{3,7},{4,0},{5,1},{6,2},{7,3},{8,12},{9,13},{10,... | collective-permute-start | bytes 786440 | tf_op jit(solution)/shard_map/ppermute | solution.py:314
  242.4 39.0 %collective-permute-start.31 = (bf16[64,2048]{1,0:T(8,128)(2,1)}, bf16[64,2048]{1,0:T(8,128)(2,1)}, u32[]{:S(2)}, u32[]{:S(2)}) collective-permute-start(bf16[64,2048]{1,0:T(8,128)(2,1)} %get-tuple-element.59), channel_id=1, source_target_pairs={{0,6},{1,7},{2,4},{3,5},{4,2},{5,3},{6,0},{7,1},{8,14},{9,15},{10,... | collective-permute-start | bytes 786440 | tf_op jit(solution)/shard_map/ppermute | solution.py:314
  (33 other events, 344.4 us)

commit v2 on v1

--- a/solution.py
+++ b/solution.py
@@ -98,9 +98,9 @@
             gated[pl.ds(start, BLK // 2)] = gate[half * (BLK // 2) : (half + 1) * (BLK // 2)]
 
 
-def backward_kernel(place, acc, act0, act12, convh, mspec, fspec, skip, fwd, inv, invlag, *refs):
+def backward_kernel(place, acc, act0, mspec, fspec, skip, fwd, inv, invlag, *refs):
     og, refs = refs[: 2 * SIDE], refs[2 * SIDE :]
-    weights, (bg, pay0, pay1, pay2, pay3, gmix, lagbuf) = refs[:4], refs[4:]
+    weights, (bg, long0, long1, long2, long3, gmix, lagbuf) = refs[:4], refs[4:]
     rows = bg.shape[0]
     nb = rows // BLK
     fmat, imat = fwd[...], inv[...]
@@ -128,20 +128,31 @@
     for b in range(nb):
         gm = out[:, b * wide : (b + 1) * wide] + skip[...] * grads[b].astype(f32)
         gmix[b * BLK : (b + 1) * BLK] = gm
-        if b == 0:
-            head = gm[:PAD]
-            ga0 = bg[:PAD] * convh[...]
-            ga1 = head * act12[1]
-            ga2 = head * act12[0]
-            edge = jnp.concatenate(
-                [ga0[:2], ga1[:2], ga2[:2], jnp.zeros((2, gm.shape[1]), f32)], 0
-            ).astype(bf16)
     quarter = BLK // SIDE
-    for k, pay in enumerate((pay0, pay1, pay2, pay3)):
-        pay[:BLK] = grads[0]
-        pay[BLK : BLK + PAD] = edge
+    for k, part in enumerate((long0, long1, long2, long3)):
         start = pl.multiple_of((place[0] ^ k) * quarter, quarter)
-        pay[BLK + PAD :] = lagbuf[pl.ds(start, quarter)].astype(bf16)
+        part[...] = lagbuf[pl.ds(start, quarter)].astype(bf16)
+
+
+def head_kernel(place, acc, act0, act12, convh, lf, skip, *refs):
+    del place
+    og, refs = refs[: 2 * SIDE], refs[2 * SIDE :]
+    weights, (pay, ext) = refs[:4], refs[4:]
+    bg = acc[...] + lax.dot_general(
+        jnp.concatenate([o[...] for o in og], 1),
+        jnp.concatenate([w[n] for w in weights for n in range(2)], 1),
+        (((1,), (1,)), ((), ())),
+        preferred_element_type=f32,
+    )
+    g = (bg * act0[0]).astype(bf16)
+    ext[...] = g.astype(f32)
+    taps = lf[...].astype(f32)
+    gm0 = jnp.sum(taps * ext[:BLK], axis=0, keepdims=True) + skip[...] * ext[0:1]
+    gm1 = jnp.sum(taps * ext[1 : BLK + 1], axis=0, keepdims=True) + skip[...] * ext[1:2]
+    gm = jnp.concatenate([gm0, gm1], 0)
+    edge = [bg[:2] * convh[:2], gm * act12[1, :2], gm * act12[0, :2], jnp.zeros_like(gm)]
+    pay[:BLK] = g[:BLK]
+    pay[BLK:] = jnp.concatenate(edge, 0).astype(bf16)
 
 
 def finish_body(bg, conv, gmix, act, proj, sf, extra, gp, ext):
@@ -184,10 +195,13 @@
     short[...] = short_in[...] + finish_body(bg, conv, gfull, act, proj, sf, extra, gp, ext)
 
 
-def pieces_kernel(steps, back, *refs):
+def pieces_kernel(steps, back, more, *refs):
     weights, refs = refs[: 2 * steps], refs[2 * steps :]
     if back:
-        gated, og, (mine, other, acc, buf, sems) = refs[0], refs[1 : 1 + SIDE], refs[1 + SIDE :]
+        gated, og, refs = refs[0], refs[1 : 1 + SIDE], refs[1 + SIDE :]
+        if more:
+            acc_in, refs = refs[0], refs[3:]
+        mine, other, acc, buf, sems = refs
     else:
         gated, mine, other, buf, sems = refs
     step = pl.program_id(0)
@@ -209,7 +223,7 @@
         for c in copies(0):
             c.start()
         if back:
-            acc[...] = jnp.zeros_like(acc)
+            acc[...] = acc_in[...] if more else jnp.zeros_like(acc)
 
     for i in range(steps):
 
@@ -234,24 +248,32 @@
         )
 
 
-def multiply_pieces(weights, cols, gated, out_grad, back):
+def multiply_pieces(weights, cols, gated, out_grad=None, total=None, before=None):
     rows, chans = gated.shape
     width = weights[0].shape[1]
     steps = len(weights) // 2
+    back, more = out_grad is not None, before is not None
+    total = total or steps
+    offset = before[0] if more else 0
     whole = pl.BlockSpec((rows, chans), lambda i, c: (0, 0), pipeline_mode=pl.Buffered(1))
     in_specs = [pl.BlockSpec(memory_space=pl.ANY)] * len(weights) + [whole]
     operands = [*weights, gated]
+    aliases = {}
     if back:
         in_specs += [
             pl.BlockSpec((rows, width), lambda i, c, j=j: (0, c[SIDE * i + j])) for j in range(SIDE)
         ]
         operands += [out_grad] * SIDE
-    half_shape = jax.ShapeDtypeStruct((rows // 2, steps * SIDE * width), bf16)
-    half_spec = pl.BlockSpec((rows // 2, SIDE * width), lambda i, c: (0, i))
+        if more:
+            in_specs += [whole] + [pl.BlockSpec(memory_space=pl.ANY)] * 2
+            operands += [before[3], before[1], before[2]]
+            aliases = {len(operands) - 1: 0, len(operands): 1}
+    half_shape = jax.ShapeDtypeStruct((rows // 2, total * SIDE * width), bf16)
+    half_spec = pl.BlockSpec((rows // 2, SIDE * width), lambda i, c: (0, i + offset))
 
     def kernel(cols_ref, *refs):
         del cols_ref
-        pieces_kernel(steps, back, *refs)
+        pieces_kernel(steps, back, more, *refs)
 
     return pl.pallas_call(
         kernel,
@@ -266,6 +288,7 @@
             ],
         ),
         out_shape=[half_shape, half_shape] + [jax.ShapeDtypeStruct((rows, chans), f32)] * back,
+        input_output_aliases=aliases,
         cost_estimate=pl.CostEstimate(
             flops=(2 + 2 * back) * rows * chans * width * SIDE * steps,
             bytes_accessed=SIDE * steps * (2 * chans * width + 4 * rows * width) + 6 * rows * chans,
@@ -313,10 +336,11 @@
         name = "ctx" if axis in "xz" else "tp"
         return lax.ppermute(value, name, [(d, d ^ shift) for d in range(lax.axis_size(name))])
 
-    def gather(piece, first, second, turn):
+    def gather(piece, first, second):
+        h = piece.shape[0] // 2
         p, q = ring(piece, first, 1), ring(piece, first, -1)
-        r = ring(p if turn > 0 else q, first, turn)
-        one, two = jnp.concatenate([piece, p], 0), jnp.concatenate([q, r], 0)
+        t, b = ring(p[:h], first, 1), ring(q[h:], first, -1)
+        one, two = jnp.concatenate([piece, p], 0), jnp.concatenate([q, t, b], 0)
         op, oq = ring(one, second, 1), ring(one, second, -1)
         tp_, tq = ring(two, second, 1), ring(two, second, -1)
         far_one = ring(op, second, 1)
@@ -332,10 +356,8 @@
         return out
 
     order4 = (0, -1, 1, 2)
-    cols1 = jnp.stack(
-        blocks(0, order4, (0,)) + blocks(1, order4, (0,))
-        + blocks(0, order4, (-1, 1)) + blocks(1, order4, (-1, 1))
-    )
+    cols1 = jnp.stack(blocks(0, order4, (0,)) + blocks(1, order4, (0,)))
+    cols2 = jnp.stack(blocks(0, order4, (-1, 1)) + blocks(1, order4, (-1, 1)))
     cols3 = jnp.stack(blocks(0, order4, (2,)) + blocks(1, order4, (2,)))
 
     positions = jnp.arange(ctx_count, dtype=jnp.int32)
@@ -383,9 +405,8 @@
     got = along_z(to_z)
     left = landed(got, left_source)
 
-    wa, wb, _ = lax.optimization_barrier((out_weight[:, :width], out_weight[:, width:], sent))
-    near_a, mid_a, far_a = gather(wa, "x", "z", 1)
-    near_b, mid_b, far_b = gather(wb, "z", "x", -1)
+    near_a, mid_a, far_a = gather(out_weight[:, :width], "x", "z")
+    near_b, mid_b, far_b = gather(out_weight[:, width:], "z", "x")
 
     fwd = jnp.asarray(forward_matrix())
     inv_late, inv_now, inv_lag = (jnp.asarray(inverse_matrix(s)) for s in (BLK, 0, -BLK))
@@ -434,27 +455,61 @@
 
     def scatter(mine, other):
         got = swap(other, "core", 1)
-        total = (mine.astype(f32) + got.astype(f32)).astype(bf16)
-        parts = [total[k * share : (k + 1) * share] for k in range(SIDE)]
+        parts = [
+            (mine[k * share : (k + 1) * share].astype(f32) + got[k * share : (k + 1) * share].astype(f32)).astype(bf16)
+            for k in range(SIDE)
+        ]
         return [parts[0]] + [swap(parts[k], "y", k) for k in (1, 2, 3)]
 
+    early = multiply_pieces(near_a + near_b, cols1, gated, out_grad, 6)
     mine1, other1, acc = multiply_pieces(
-        near_a + near_b + mid_a + mid_b, cols1, gated, out_grad, True
+        mid_a + mid_b, cols2, gated, out_grad, 6, (2, *early)
     )
     out1 = scatter(mine1, other1)
 
     quarter = BLK // SIDE
-    place = jnp.concatenate([jnp.reshape(xi, (1,)), cols3]).astype(jnp.int32)
-
-    def third(w):
-        count = w.shape[0] // chans
-        return w.reshape(count, chans, width), pl.BlockSpec(
-            (count, tile, width), lambda i, c: (0, i, 0)
-        )
-
-    lasts, last_specs = zip(*[third(w) for w in far_a + far_b])
-    pay_shape = jax.ShapeDtypeStruct((BLK + PAD + quarter, chans), bf16)
-    pay_spec = col(BLK + PAD + quarter)
+    place = jnp.concatenate([jnp.reshape(zi, (1,)), cols3]).astype(jnp.int32)
+    lasts = [w.reshape(2, chans, width) for w in far_a + far_b]
+    last_spec = pl.BlockSpec((2, tile, width), lambda i, c: (0, i, 0))
+
+    def out_grad_rows(n):
+        return [pl.BlockSpec((n, width), lambda i, c, j=j: (0, c[1 + j])) for j in range(2 * SIDE)]
+
+    def first_rows(n, *lead):
+        zeros = [0] * len(lead)
+        return pl.BlockSpec((*lead, n, tile), lambda i, c: (*zeros, 0, i))
+
+    head = pl.pallas_call(
+        head_kernel,
+        grid_spec=pltpu.PrefetchScalarGridSpec(
+            num_scalar_prefetch=1,
+            grid=grid,
+            in_specs=[
+                first_rows(BLK + PAD),
+                first_rows(BLK + PAD, 1),
+                pl.BlockSpec(
+                    (pl.Element(2), pl.Element(PAD), pl.Element(tile)),
+                    lambda i, c: (1, 0, i * tile),
+                ),
+                first_rows(PAD),
+                col(BLK),
+                col(1),
+                *out_grad_rows(BLK + PAD),
+                *[last_spec] * 4,
+            ],
+            out_specs=col(BLK + PAD),
+            scratch_shapes=[pltpu.VMEM((BLK + PAD, tile), f32)],
+        ),
+        out_shape=jax.ShapeDtypeStruct((BLK + PAD, chans), bf16),
+        cost_estimate=pl.CostEstimate(
+            flops=600_000_000, bytes_accessed=6 << 20, transcendentals=0
+        ),
+        name="head",
+    )
+    pay = head(place, acc, act, act, conv, long_filter, skip_row, *[out_grad] * (2 * SIDE), *lasts)
+    got = along_x([pay] * SIDE)
+
+    long_shape = jax.ShapeDtypeStruct((quarter, chans), bf16)
     backward = pl.pallas_call(
         backward_kernel,
         grid_spec=pltpu.PrefetchScalarGridSpec(
@@ -462,52 +517,39 @@
             grid=grid,
             in_specs=[
                 col(rows),
-                pl.BlockSpec((1, rows, tile), lambda i, c: (0, 0, i)),
-                pl.BlockSpec(
-                    (pl.Element(2), pl.Element(PAD), pl.Element(tile)),
-                    lambda i, c: (1, 0, i * tile),
-                ),
-                col(PAD),
+                first_rows(rows, 1),
                 col(nb, 2 * BLK),
                 col(2 * BLK),
                 col(1),
                 const,
                 const,
                 const,
-                *[
-                    pl.BlockSpec((rows, width), lambda i, c, j=j: (0, c[1 + j]))
-                    for j in range(2 * SIDE)
-                ],
-                *last_specs,
+                *out_grad_rows(rows),
+                *[last_spec] * 4,
             ],
-            out_specs=[col(rows), pay_spec, pay_spec, pay_spec, pay_spec, col(rows)],
+            out_specs=[col(rows)] + [col(quarter)] * 4 + [col(rows)],
             scratch_shapes=[pltpu.VMEM((BLK, tile), f32)],
         ),
-        out_shape=[
-            jax.ShapeDtypeStruct((rows, chans), f32),
-            pay_shape, pay_shape, pay_shape, pay_shape,
-            jax.ShapeDtypeStruct((rows, chans), f32),
-        ],
+        out_shape=[jax.ShapeDtypeStruct((rows, chans), f32)]
+        + [long_shape] * 4
+        + [jax.ShapeDtypeStruct((rows, chans), f32)],
         cost_estimate=pl.CostEstimate(
             flops=8_000_000_000, bytes_accessed=20 << 20, transcendentals=0
         ),
         name="backward",
     )
-    bg, pay0, pay1, pay2, pay3, gmix = backward(
-        place, acc, act, act, conv, mspec, fspec, skip_row, fwd, inv_now, inv_lag,
+    bg, *longs, gmix = backward(
+        place, acc, act, mspec, fspec, skip_row, fwd, inv_now, inv_lag,
         *[out_grad] * (2 * SIDE), *lasts,
     )
 
-    got = along_x([pay0, pay1, pay2, pay3])
-    sums = [g[BLK + PAD :].astype(f32) for g in got]
-    quarter_sum = ((sums[0] + sums[1]) + (sums[2] + sums[3])).astype(bf16)
-    to_z = chosen([g[: BLK + PAD] for g in got], readers)
-    got = along_z([jnp.concatenate([v, quarter_sum], 0) for v in to_z])
+    to_z = chosen(got, readers)
+    got = along_z([jnp.concatenate([v, part], 0) for v, part in zip(to_z, longs)])
     right = landed([g[: BLK + PAD] for g in got], readers)
     sums = [g[BLK + PAD :].astype(f32) for g in got]
     my_quarter = (sums[0] + sums[1]) + (sums[2] + sums[3])
 
-    mine3, other3 = multiply_pieces(far_a + far_b, cols3, gated, None, False)
+    mine3, other3 = multiply_pieces(far_a + far_b, cols3, gated)
     out3 = scatter(mine3, other3)
 
     low = rows - BLK - PAD
@@ -563,12 +605,13 @@
         bg, conv, gmix, act, right, projected, short_filter, fspec, fwd, inv_now, short, gp
     )
 
-    got = along_x([jnp.concatenate([my_quarter, short], 0).astype(bf16)] * SIDE)
-    long_total = jnp.concatenate([pick(got, xi ^ q)[:quarter] for q in range(SIDE)], 0)
-    sums = [g[quarter:].astype(f32) for g in got]
-    sums = (sums[0] + sums[1]) + (sums[2] + sums[3])
-    sums = along_z([sums] * SIDE)
-    short_total = ((sums[0] + sums[1]) + (sums[2] + sums[3]))[:9].reshape(3, 3, chans)
+    message = jnp.concatenate([my_quarter, short], 0)
+    for along in (along_x, along_z):
+        got = along([message.astype(bf16)] * SIDE)
+        wide = [g.astype(f32) for g in got]
+        message = (wide[0] + wide[1]) + (wide[2] + wide[3])
+    long_total = jnp.concatenate([pick(got, zi ^ q)[:quarter] for q in range(SIDE)], 0)
+    short_total = message[quarter : quarter + 9].reshape(3, 3, chans)
 
     counts = tuple(o[0].shape[1] // width for o in (out1, out3))
     collect = pl.pallas_call(
@@ -587,7 +630,7 @@
         cost_estimate=pl.CostEstimate(flops=10_000_000, bytes_accessed=5 << 20, transcendentals=0),
         name="collect",
     )
-    mixed = collect(jnp.concatenate([cols1, cols3]), *out1, *out3)
+    mixed = collect(jnp.concatenate([cols1, cols2, cols3]), *out1, *out3)
 
     scale = 1.0 / math.sqrt(rows * ctx_count)
     return mixed, gp, long_total.astype(f32) * scale, short_total * scale

time: 291 us -> 294 us (1.010)
  waiting for transfers between devices: 109 us -> 95.6 us
  Pallas kernels: 69.9 us -> 81.9 us
  starting transfers between devices: 59.1 us -> 66.4 us
    ppermute x18 -> x20, waiting for transfers between devices: 49.3 us -> 33.8 us  [ring(): return lax.ppermute(value, 'ctx', pairs)]
    ppermute x18 -> x20, starting transfers between devices: 24.6 us -> 31.2 us  [ring(): return lax.ppermute(value, 'ctx', pairs)]
    pallas_call x2 -> x3, Pallas kernels: 18.3 us -> 24.5 us  [the longest x1 13.7 us: on_device(): backward(place, acc, act, mspec, fspec, skip_row, fwd, inv_now, inv_lag,...]
    pallas_call x2 -> x3, Pallas kernels: 27 us -> 32.9 us  [multiply_pieces(): pl.pallas_call(kernel, grid_spec=pltpu.PrefetchScalarGridSpec(num_scalar_...]
    concatenate x6 -> x4, local copies, waits for them, and re-layouts: 5.73 us -> 2 us  [the longest x2 0.74 us: gather(): one, two = (jnp.concatenate([piece, p], 0), jnp.concatenate([q, t, b], 0))]
    select_n x5 -> x4, other arithmetic: 4.95 us -> 1.29 us  [pick(): return jnp.where(index >= 2, high, low)]
    unnamed x32 -> x62, local copies, waits for them, and re-layouts: 6.15 us -> 7.52 us
  transfers between devices with their start and end apart: 44 -> 46, of which waited for: 17 -> 13; matrix products, arithmetic and copies ran while one was open for 12% -> 11% of each run, Pallas kernels for 18% -> 27%
where the time goes in v2:
time: 294 us; the launch traced here: 291 us
  waiting for transfers between devices  95.6 us (33%)
  Pallas kernels  81.9 us (28%)
  starting transfers between devices  66.4 us (23%)
  other arithmetic  19.4 us (7%)
  local copies, waits for them, and re-layouts  18.9 us (6%)
  between operations  8.96 us (3%)
    ppermute x26, waiting for transfers between devices, swap(): lax.ppermute(value, name, [(d, d ^ shift) for d in range(lax.axis_size(na...  61.8 us
    ppermute x26, starting transfers between devices, swap(): lax.ppermute(value, name, [(d, d ^ shift) for d in range(lax.axis_size(na...  35.2 us
    ppermute x20, waiting for transfers between devices, ring(): return lax.ppermute(value, 'ctx', pairs)  33.8 us
    pallas_call x3, Pallas kernels, multiply_pieces(): pl.pallas_call(kernel, grid_spec=pltpu.PrefetchScalarGridSpec(num_scalar_...  32.9 us
    ppermute x20, starting transfers between devices, ring(): return lax.ppermute(value, 'ctx', pairs)  31.2 us
    pallas_call x1, Pallas kernels, on_device(): backward(place, acc, act, mspec, fspec, skip_row, fwd, inv_now, inv_lag,...  13.7 us
    pallas_call x1, Pallas kernels, on_device(): forward(order, projected, left, short_filter, long_filter, skip_row, fwd,...  10.2 us
    pallas_call x1, Pallas kernels, on_device(): top(bg, conv, gmix, act, bg, conv, gmix, act, projected, short_filter)  8.33 us
  transfers between devices with their start and end apart: 46, of which 13 were waited for; matrix products, arithmetic and copies ran while one was open for 11% of the time, Pallas kernels for 27%

profile of v2, /device:TPU:24, one launch (start us, length us, event | category | flops | bytes accessed | tf_op | source)
XLA Modules:
  0.0 291.1 jit_solution(15002151100712551100)
XLA Ops:
  16.8 5.6 %collective-permute-done.16 = bf16[136,1024]{1,0:T(8,128)(2,1)S(1)} collective-permute-done((bf16[136,1024]{1,0:T(8,128)(2,1)S(1)}, bf16[136,1024]{1,0:T(8,128)(2,1)S(1)}, u32[]{:S(2)}, u32[]{:S(2)}) %collective-permute-start.16) | collective-permute-done | bytes 278560 | tf_op jit(solution)/shard_map/ppermute | solution.py:337
  22.5 4.0 %collective-permute-start.10 = (bf16[1024,256]{1,0:T(8,128)(2,1)S(1)}, bf16[1024,256]{1,0:T(8,128)(2,1)S(1)}, u32[]{:S(2)}, u32[]{:S(2)}) collective-permute-start(bf16[1024,256]{1,0:T(8,128)(2,1)S(1)} %get-tuple-element.64), channel_id=1, source_target_pairs={{0,96},{8,104},{16,112},{24,120},{32,0},{40,8},{48,16},{56,24},{64... | collective-permute-start | bytes 1572872 | tf_op jit(solution)/shard_map/ppermute | solution.py:332
  27.7 4.6 %collective-permute-done = bf16[1024,256]{1,0:T(8,128)(2,1)S(1)} collective-permute-done((bf16[1024,256]{1,0:T(8,128)(2,1)S(1)}, bf16[1024,256]{1,0:T(8,128)(2,1)S(1)}, u32[]{:S(2)}, u32[]{:S(2)}) %collective-permute-start) | collective-permute-done | bytes 524320 | tf_op jit(solution)/shard_map/ppermute | solution.py:332
  32.3 4.1 %collective-permute-start.19 = (bf16[136,1024]{1,0:T(8,128)(2,1)}, bf16[136,1024]{1,0:T(8,128)(2,1)}, u32[]{:S(2)}, u32[]{:S(2)}) collective-permute-start(bf16[136,1024]{1,0:T(8,128)(2,1)} %get-tuple-element.63), channel_id=1, source_target_pairs={{0,96},{8,104},{16,112},{24,120},{32,64},{40,72},{48,80},{56,88},{... | collective-permute-start | bytes 835592 | tf_op jit(solution)/shard_map/ppermute | solution.py:337
  55.3 11.2 %collective-permute-done.20 = bf16[136,1024]{1,0:T(8,128)(2,1)} collective-permute-done((bf16[136,1024]{1,0:T(8,128)(2,1)}, bf16[136,1024]{1,0:T(8,128)(2,1)}, u32[]{:S(2)}, u32[]{:S(2)}) %collective-permute-start.20) | collective-permute-done | bytes 278560 | tf_op jit(solution)/shard_map/ppermute | solution.py:337
  67.3 4.4 %collective-permute-done.3 = bf16[512,256]{1,0:T(8,128)(2,1)} collective-permute-done((bf16[512,256]{1,0:T(8,128)(2,1)}, bf16[512,256]{1,0:T(8,128)(2,1)}, u32[]{:S(2)}, u32[]{:S(2)}) %collective-permute-start.3) | collective-permute-done | bytes 262176 | tf_op jit(solution)/shard_map/ppermute | solution.py:332
  89.7 10.2 %forward.1 = (bf16[512,1024]{1,0:T(8,128)(2,1)}, f32[512,1024]{1,0:T(8,128)}, f32[3,512,1024]{2,1,0:T(8,128)}, f32[4,256,1024]{2,1,0:T(8,128)}, f32[256,1024]{1,0:T(8,128)}) custom-call(s32[8]{0:T(128)} %stack.173.order, bf16[3,512,1024]{2,1,0:T(8,128)(2,1)} %proj.5, bf16[136,1024]{1,0:T(8,128)(2,1)} %select_select_fusion.3.halo, f32[3,3,1024]{2,1,0:T(4,128)} %sf.5, ...), custom_call_target="tpu_custom_call" | custom-call | flops 12000000000 | bytes 20971520 | tf_op jit(solution)/shard_map/forward/pallas_call | solution.py:452
  99.9 5.5 %collective-permute-done.14.refs_6_ = bf16[2048,256]{1,0:T(8,128)(2,1)} collective-permute-done((bf16[2048,256]{1,0:T(8,128)(2,1)S(1)}, bf16[2048,256]{1,0:T(8,128)(2,1)}, u32[]{:S(2)}, u32[]{:S(2)}) %collective-permute-start.14) | collective-permute-done | bytes 1048608 | tf_op jit(solution)/shard_map/ppermute | solution.py:332
  105.4 4.1 %collective-permute-done.5.refs_1_ = bf16[2048,256]{1,0:T(8,128)(2,1)} collective-permute-done((bf16[2048,256]{1,0:T(8,128)(2,1)S(1)}, bf16[2048,256]{1,0:T(8,128)(2,1)}, u32[]{:S(2)}, u32[]{:S(2)}) %collective-permute-start.5) | collective-permute-done | bytes 1048608 | tf_op jit(solution)/shard_map/ppermute | solution.py:332
  110.8 13.9 %collective-permute-done.15.refs_7_ = bf16[2048,256]{1,0:T(8,128)(2,1)} collective-permute-done((bf16[2048,256]{1,0:T(8,128)(2,1)}, bf16[2048,256]{1,0:T(8,128)(2,1)}, u32[]{:S(2)}, u32[]{:S(2)}) %collective-permute-start.15) | collective-permute-done | bytes 1048608 | tf_op jit(solution)/shard_map/ppermute | solution.py:332
  124.6 3.7 %collective-permute-start.29 = (bf16[2048,256]{1,0:T(8,128)(2,1)}, bf16[2048,256]{1,0:T(8,128)(2,1)}, u32[]{:S(2)}, u32[]{:S(2)}) collective-permute-start(bf16[2048,256]{1,0:T(8,128)(2,1)} %collective-permute-done.15.refs_7_), channel_id=1, source_target_pairs={{0,24},{8,0},{16,8},{24,16},{32,56},{40,32},{48,40},{56,48},{64,88... | collective-permute-start | bytes 3145736 | tf_op jit(solution)/shard_map/ppermute | solution.py:332
  128.3 10.1 %pieces.3 = (bf16[256,6144]{1,0:T(8,128)(2,1)}, bf16[256,6144]{1,0:T(8,128)(2,1)}, f32[512,1024]{1,0:T(8,128)}) custom-call(s32[8]{0:T(128)} %stack.174.cols_ref, bf16[2048,256]{1,0:T(8,128)(2,1)} %copy-done.4, bf16[2048,256]{1,0:T(8,128)(2,1)} %copy-done.7, bf16[2048,256]{1,0:T(8,128)(2,1)} %copy-done.5, ...), custom_call_target="tpu_custom_call" | custom-call | flops 4294967296 | bytes 11534336 | tf_op jit(solution)/shard_map/pieces/pallas_call | solution.py:278
  138.4 15.8 %pieces.4 = (bf16[256,6144]{1,0:T(8,128)(2,1)}, bf16[256,6144]{1,0:T(8,128)(2,1)}, f32[512,1024]{1,0:T(8,128)}) custom-call(s32[16]{0:T(128)} %stack.164.cols_ref, bf16[2048,256]{1,0:T(8,128)(2,1)} %collective-permute-done.1.refs_0_, bf16[2048,256]{1,0:T(8,128)(2,1)} %collective-permute-done.5.refs_1_, ...), custom_call_target="tpu_custom_call", output_to_operand_aliasing={{0}: (15, {}), {1}: (16, {})} | custom-call | flops 8589934592 | bytes 19922944 | tf_op jit(solution)/shard_map/pieces/pallas_call | solution.py:278
  156.0 6.3 %head.1 = bf16[136,1024]{1,0:T(8,128)(2,1)} custom-call(s32[9]{0:T(128)} %concatenate.45.place, f32[512,1024]{1,0:T(8,128)} %get-tuple-element.35.acc, f32[3,512,1024]{2,1,0:T(8,128)} %get-tuple-element.36.act0.act12.act.actn, f32[3,512,1024]{2,1,0:T(8,128)} %get-tuple-element.36.act0.act12.act.actn, f32[512,1024]{1,0:T(8,128)} %get-tuple-element.40.convh.conv.convn, ...), custom_call_target="tpu_custom_call" | custom-call | flops 600000000 | bytes 6291456 | tf_op jit(solution)/shard_map/head/pallas_call | solution.py:509
  162.4 4.0 %collective-permute-start.35 = (bf16[136,1024]{1,0:T(8,128)(2,1)}, bf16[136,1024]{1,0:T(8,128)(2,1)S(1)}, u32[]{:S(2)}, u32[]{:S(2)}) collective-permute-start(bf16[136,1024]{1,0:T(8,128)(2,1)} %head.1), channel_id=1, source_target_pairs={{0,16},{8,24},{16,0},{24,8},{32,48},{40,56},{48,32},{56,40},{64,80... | collective-permute-start | bytes 835592 | tf_op jit(solution)/shard_map/ppermute | solution.py:337
  166.4 13.7 %backward.1 = (f32[512,1024]{1,0:T(8,128)}, bf16[32,1024]{1,0:T(8,128)(2,1)}, bf16[32,1024]{1,0:T(8,128)(2,1)}, bf16[32,1024]{1,0:T(8,128)(2,1)}, bf16[32,1024]{1,0:T(8,128)(2,1)}, /*index=5*/f32[512,1024]{1,0:T(8,128)}) custom-call(s32[9]{0:T(128)} %concatenate.45.place, f32[512,1024]{1,0:T(8,128)} %get-tuple-element.35.acc, ...), custom_call_target="tpu_custom_call" | custom-call | flops 8000000000 | bytes 20971520 | tf_op jit(solution)/shard_map/backward/pallas_call | solution.py:541
  188.6 7.0 %pieces.5 = (bf16[256,2048]{1,0:T(8,128)(2,1)}, bf16[256,2048]{1,0:T(8,128)(2,1)}) custom-call(s32[8]{0:T(128)} %stack.175.cols_ref, bf16[2048,256]{1,0:T(8,128)(2,1)} %copy-done.1, bf16[2048,256]{1,0:T(8,128)(2,1)} %copy-done.3, bf16[2048,256]{1,0:T(8,128)(2,1)} %copy-done.2, bf16[2048,256]{1,0:T(8,128)(2,1)} %collective-permute-done.29.refs_3_, ...), custom_call_target="tpu_custom_call" | custom-call | flops 2147483648 | bytes 11534336 | tf_op jit(solution)/shard_map/pieces/pallas_call | solution.py:278
  195.9 8.3 %top.1 = (bf16[3,512,1024]{2,1,0:T(8,128)(2,1)}, f32[16,1024]{1,0:T(8,128)}) custom-call(f32[512,1024]{1,0:T(8,128)} %get-tuple-element.39.bg.bgn, f32[512,1024]{1,0:T(8,128)} %get-tuple-element.40.convh.conv.convn, f32[512,1024]{1,0:T(8,128)} %get-tuple-element.41.gmix.gmixn, f32[3,512,1024]{2,1,0:T(8,128)} %get-tuple-element.36.act0.act12.act.actn, ...), custom_call_target="tpu_custom_call" | custom-call | flops 200000000 | bytes 10485760 | tf_op jit(solution)/shard_map/top/pallas_call | solution.py:585
  205.3 6.0 %bottom.1 = (bf16[3,512,1024]{2,1,0:T(8,128)(2,1)}, f32[16,1024]{1,0:T(8,128)}) custom-call(f32[512,1024]{1,0:T(8,128)} %get-tuple-element.39.bg.bgn, f32[512,1024]{1,0:T(8,128)} %get-tuple-element.40.convh.conv.convn, f32[512,1024]{1,0:T(8,128)} %get-tuple-element.41.gmix.gmixn, ...), custom_call_target="tpu_custom_call", output_to_operand_aliasing={{0}: (11, {})} | custom-call | flops 2000000000 | bytes 5242880 | tf_op jit(solution)/shard_map/bottom/pallas_call | solution.py:604
  218.2 3.7 %collective-permute-done.42 = bf16[48,1024]{1,0:T(8,128)(2,1)S(1)} collective-permute-done((bf16[48,1024]{1,0:T(8,128)(2,1)S(1)}, bf16[48,1024]{1,0:T(8,128)(2,1)S(1)}, u32[]{:S(2)}, u32[]{:S(2)}) %collective-permute-start.42) | collective-permute-done | bytes 98336 | tf_op jit(solution)/shard_map/ppermute | solution.py:337
  231.8 4.2 %add_convert_fusion = (bf16[64,6144]{1,0:T(8,128)(2,1)}, bf16[64,6144]{1,0:T(8,128)(2,1)}, bf16[64,6144]{1,0:T(8,128)(2,1)}, bf16[64,6144]{1,0:T(8,128)(2,1)}) fusion(bf16[256,6144]{1,0:T(8,128)(2,1)} %collective-permute-done.22, bf16[256,6144]{1,0:T(8,128)(2,1)S(1)} %copy-done), kind=kLoop, calls=%fused_computation | loop fusion | flops 6291456 | bytes 9437184 | tf_op jit(solution)/shard_map/convert_element_type | solution.py:459
  245.1 31.9 %collective-permute-done.32.refs_6_ = bf16[64,2048]{1,0:T(8,128)(2,1)S(1)} collective-permute-done((bf16[64,2048]{1,0:T(8,128)(2,1)}, bf16[64,2048]{1,0:T(8,128)(2,1)S(1)}, u32[]{:S(2)}, u32[]{:S(2)}) %collective-permute-start.32) | collective-permute-done | bytes 262176 | tf_op jit(solution)/shard_map/ppermute | solution.py:337
  277.0 8.1 %collective-permute-done.33.refs_7_ = bf16[64,2048]{1,0:T(8,128)(2,1)S(1)} collective-permute-done((bf16[64,2048]{1,0:T(8,128)(2,1)}, bf16[64,2048]{1,0:T(8,128)(2,1)S(1)}, u32[]{:S(2)}, u32[]{:S(2)}) %collective-permute-start.33) | collective-permute-done | bytes 262176 | tf_op jit(solution)/shard_map/ppermute | solution.py:337
  286.6 4.5 %collect.1 = bf16[64,8192]{1,0:T(8,128)(2,1)} custom-call(s32[32]{0:T(128)} %concatenate.39.cols, bf16[64,6144]{1,0:T(8,128)(2,1)} %get-tuple-element.53.refs_0_, bf16[64,6144]{1,0:T(8,128)(2,1)} %copy-done.16, bf16[64,6144]{1,0:T(8,128)(2,1)} %copy-done.17, bf16[64,6144]{1,0:T(8,128)(2,1)} %copy-done.18, bf16[64,2048]{1,0:T(8,128)(2,1)} %get-tuple-element.57.refs_4_, ...), custom_call_target="tpu_custom_call" | custom-call | flops 10000000 | bytes 5242880 | tf_op jit(solution)/shard_map/collect/pallas_call | solution.py:633
  (185 shorter events, 87.1 us)
Async XLA Ops:
  8.6 23.7 %collective-permute-start = (bf16[1024,256]{1,0:T(8,128)(2,1)S(1)}, bf16[1024,256]{1,0:T(8,128)(2,1)S(1)}, u32[]{:S(2)}, u32[]{:S(2)}) collective-permute-start(bf16[1024,256]{1,0:T(8,128)(2,1)S(1)} %get-tuple-element.65), channel_id=1, source_target_pairs={{0,8},{8,16},{16,24},{24,0},{32,40},{40,48},{48,56},{56,32},{64,72... | collective-permute-start | bytes 1572872 | tf_op jit(solution)/shard_map/ppermute | solution.py:332
  10.0 26.5 %collective-permute-start.8 = (bf16[1024,256]{1,0:T(8,128)(2,1)S(1)}, bf16[1024,256]{1,0:T(8,128)(2,1)}, u32[]{:S(2)}, u32[]{:S(2)}) collective-permute-start(bf16[1024,256]{1,0:T(8,128)(2,1)S(1)} %get-tuple-element.64), channel_id=1, source_target_pairs={{0,32},{8,40},{16,48},{24,56},{32,64},{40,72},{48,80},{56,88},{64,... | collective-permute-start | bytes 1572872 | tf_op jit(solution)/shard_map/ppermute | solution.py:332
  14.9 23.1 %collective-permute-start.2 = (bf16[1024,256]{1,0:T(8,128)(2,1)S(1)}, bf16[1024,256]{1,0:T(8,128)(2,1)}, u32[]{:S(2)}, u32[]{:S(2)}) collective-permute-start(bf16[1024,256]{1,0:T(8,128)(2,1)S(1)} %get-tuple-element.65), channel_id=1, source_target_pairs={{0,24},{8,0},{16,8},{24,16},{32,56},{40,32},{48,40},{56,48},{64,88... | collective-permute-start | bytes 1572872 | tf_op jit(solution)/shard_map/ppermute | solution.py:332
  36.5 47.2 %collective-permute-start.1 = (bf16[2048,256]{1,0:T(8,128)(2,1)S(1)}, bf16[2048,256]{1,0:T(8,128)(2,1)}, u32[]{:S(2)}, u32[]{:S(2)}) collective-permute-start(bf16[2048,256]{1,0:T(8,128)(2,1)S(1)} %pad_maximum_fusion.refs_0_), channel_id=1, source_target_pairs={{0,32},{8,40},{16,48},{24,56},{32,64},{40,72},{48,80},{56,88},{64,... | collective-permute-start | bytes 3145736 | tf_op jit(solution)/shard_map/ppermute | solution.py:332
  38.0 48.4 %collective-permute-start.6 = (bf16[2048,256]{1,0:T(8,128)(2,1)S(1)}, bf16[2048,256]{1,0:T(8,128)(2,1)}, u32[]{:S(2)}, u32[]{:S(2)}) collective-permute-start(bf16[2048,256]{1,0:T(8,128)(2,1)S(1)} %pad_maximum_fusion.refs_0_), channel_id=1, source_target_pairs={{0,96},{8,104},{16,112},{24,120},{32,0},{40,8},{48,16},{56,24},{64... | collective-permute-start | bytes 3145736 | tf_op jit(solution)/shard_map/ppermute | solution.py:332
  41.8 44.6 %collective-permute-start.9 = (bf16[2048,256]{1,0:T(8,128)(2,1)S(1)}, bf16[2048,256]{1,0:T(8,128)(2,1)}, u32[]{:S(2)}, u32[]{:S(2)}) collective-permute-start(bf16[2048,256]{1,0:T(8,128)(2,1)S(1)} %pad_maximum_fusion.1.refs_2_), channel_id=1, source_target_pairs={{0,8},{8,16},{16,24},{24,0},{32,40},{40,48},{48,56},{56,32},{64,72... | collective-permute-start | bytes 3145736 | tf_op jit(solution)/shard_map/ppermute | solution.py:332
  41.8 24.7 %collective-permute-start.20 = (bf16[136,1024]{1,0:T(8,128)(2,1)}, bf16[136,1024]{1,0:T(8,128)(2,1)}, u32[]{:S(2)}, u32[]{:S(2)}) collective-permute-start(bf16[136,1024]{1,0:T(8,128)(2,1)} %get-tuple-element.61), channel_id=1, source_target_pairs={{0,64},{8,72},{16,80},{24,88},{32,96},{40,104},{48,112},{56,120},{... | collective-permute-start | bytes 835592 | tf_op jit(solution)/shard_map/ppermute | solution.py:337
  44.2 27.4 %collective-permute-start.3 = (bf16[512,256]{1,0:T(8,128)(2,1)}, bf16[512,256]{1,0:T(8,128)(2,1)}, u32[]{:S(2)}, u32[]{:S(2)}) collective-permute-start(bf16[512,256]{1,0:T(8,128)(2,1)} %slice.172), channel_id=1, source_target_pairs={{0,8},{8,16},{16,24},{24,0},{32,40},{40,48},{48,56},{56,32},{64,72... | collective-permute-start | bytes 786440 | tf_op jit(solution)/shard_map/ppermute | solution.py:332
  79.3 26.1 %collective-permute-start.14 = (bf16[2048,256]{1,0:T(8,128)(2,1)S(1)}, bf16[2048,256]{1,0:T(8,128)(2,1)}, u32[]{:S(2)}, u32[]{:S(2)}) collective-permute-start(bf16[2048,256]{1,0:T(8,128)(2,1)S(1)} %pad_maximum_fusion.1.refs_2_), channel_id=1, source_target_pairs={{0,24},{8,0},{16,8},{24,16},{32,56},{40,32},{48,40},{56,48},{64,88... | collective-permute-start | bytes 3145736 | tf_op jit(solution)/shard_map/ppermute | solution.py:332
  82.5 27.1 %collective-permute-start.5 = (bf16[2048,256]{1,0:T(8,128)(2,1)S(1)}, bf16[2048,256]{1,0:T(8,128)(2,1)}, u32[]{:S(2)}, u32[]{:S(2)}) collective-permute-start(bf16[2048,256]{1,0:T(8,128)(2,1)S(1)} %constant_dynamic-update-slice_fusion.refs_1_), channel_id=1, source_target_pairs={{0,32},{8,40},{16,48},{24,56},{32,64},{40,72},{48,80},{56,88},{64,... | collective-permute-start | bytes 3145736 | tf_op jit(solution)/shard_map/ppermute | solution.py:332
  83.7 25.8 %collective-permute-start.7 = (bf16[2048,256]{1,0:T(8,128)(2,1)S(1)}, bf16[2048,256]{1,0:T(8,128)(2,1)}, u32[]{:S(2)}, u32[]{:S(2)}) collective-permute-start(bf16[2048,256]{1,0:T(8,128)(2,1)S(1)} %constant_dynamic-update-slice_fusion.refs_1_), channel_id=1, source_target_pairs={{0,96},{8,104},{16,112},{24,120},{32,0},{40,8},{48,16},{56,24},{64... | collective-permute-start | bytes 3145736 | tf_op jit(solution)/shard_map/ppermute | solution.py:332
  86.4 52.0 %collective-permute-start.13 = (bf16[2048,256]{1,0:T(8,128)(2,1)}, bf16[2048,256]{1,0:T(8,128)(2,1)}, u32[]{:S(2)}, u32[]{:S(2)}) collective-permute-start(bf16[2048,256]{1,0:T(8,128)(2,1)} %constant_dynamic-update-slice_fusion.3.refs_3_), channel_id=1, source_target_pairs={{0,8},{8,16},{16,24},{24,0},{32,40},{40,48},{48,56},{56,32},{64,72... | collective-permute-start | bytes 3145736 | tf_op jit(solution)/shard_map/ppermute | solution.py:332
  86.5 38.2 %collective-permute-start.15 = (bf16[2048,256]{1,0:T(8,128)(2,1)}, bf16[2048,256]{1,0:T(8,128)(2,1)}, u32[]{:S(2)}, u32[]{:S(2)}) collective-permute-start(bf16[2048,256]{1,0:T(8,128)(2,1)} %constant_dynamic-update-slice_fusion.3.refs_3_), channel_id=1, source_target_pairs={{0,24},{8,0},{16,8},{24,16},{32,56},{40,32},{48,40},{56,48},{64,88... | collective-permute-start | bytes 3145736 | tf_op jit(solution)/shard_map/ppermute | solution.py:332
  105.4 48.9 %collective-permute-start.26 = (bf16[2048,256]{1,0:T(8,128)(2,1)}, bf16[2048,256]{1,0:T(8,128)(2,1)S(1)}, u32[]{:S(2)}, u32[]{:S(2)}) collective-permute-start(bf16[2048,256]{1,0:T(8,128)(2,1)} %collective-permute-done.1.refs_0_), channel_id=1, source_target_pairs={{0,32},{8,40},{16,48},{24,56},{32,64},{40,72},{48,80},{56,88},{64,... | collective-permute-start | bytes 3145736 | tf_op jit(solution)/shard_map/ppermute | solution.py:332
  109.6 44.8 %collective-permute-start.28 = (bf16[2048,256]{1,0:T(8,128)(2,1)}, bf16[2048,256]{1,0:T(8,128)(2,1)S(1)}, u32[]{:S(2)}, u32[]{:S(2)}) collective-permute-start(bf16[2048,256]{1,0:T(8,128)(2,1)} %collective-permute-done.9.refs_4_), channel_id=1, source_target_pairs={{0,8},{8,16},{16,24},{24,0},{32,40},{40,48},{48,56},{56,32},{64,72... | collective-permute-start | bytes 3145736 | tf_op jit(solution)/shard_map/ppermute | solution.py:332
  109.6 44.8 %collective-permute-start.27 = (bf16[2048,256]{1,0:T(8,128)(2,1)}, bf16[2048,256]{1,0:T(8,128)(2,1)S(1)}, u32[]{:S(2)}, u32[]{:S(2)}) collective-permute-start(bf16[2048,256]{1,0:T(8,128)(2,1)} %collective-permute-done.7.refs_3_), channel_id=1, source_target_pairs={{0,96},{8,104},{16,112},{24,120},{32,0},{40,8},{48,16},{56,24},{64... | collective-permute-start | bytes 3145736 | tf_op jit(solution)/shard_map/ppermute | solution.py:332
  124.6 29.8 %collective-permute-start.29 = (bf16[2048,256]{1,0:T(8,128)(2,1)}, bf16[2048,256]{1,0:T(8,128)(2,1)}, u32[]{:S(2)}, u32[]{:S(2)}) collective-permute-start(bf16[2048,256]{1,0:T(8,128)(2,1)} %collective-permute-done.15.refs_7_), channel_id=1, source_target_pairs={{0,24},{8,0},{16,8},{24,16},{32,56},{40,32},{48,40},{56,48},{64,88... | collective-permute-start | bytes 3145736 | tf_op jit(solution)/shard_map/ppermute | solution.py:332
  154.2 77.6 %collective-permute-start.22 = (bf16[256,6144]{1,0:T(8,128)(2,1)}, bf16[256,6144]{1,0:T(8,128)(2,1)}, u32[]{:S(2)}, u32[]{:S(2)}) collective-permute-start(bf16[256,6144]{1,0:T(8,128)(2,1)} %get-tuple-element.32), channel_id=1, source_target_pairs={{0,1},{1,0},{2,3},{3,2},{4,5},{5,4},{6,7},{7,6},{8,9},{9,8},{10,11... | collective-permute-start | bytes 9437192 | tf_op jit(solution)/shard_map/ppermute | solution.py:337
  195.6 32.7 %collective-permute-start.30 = (bf16[256,2048]{1,0:T(8,128)(2,1)}, bf16[256,2048]{1,0:T(8,128)(2,1)}, u32[]{:S(2)}, u32[]{:S(2)}) collective-permute-start(bf16[256,2048]{1,0:T(8,128)(2,1)} %get-tuple-element.34), channel_id=1, source_target_pairs={{0,1},{1,0},{2,3},{3,2},{4,5},{5,4},{6,7},{7,6},{8,9},{9,8},{10,11... | collective-permute-start | bytes 3145736 | tf_op jit(solution)/shard_map/ppermute | solution.py:337
  236.0 49.2 %collective-permute-start.23 = (bf16[64,6144]{1,0:T(8,128)(2,1)}, bf16[64,6144]{1,0:T(8,128)(2,1)S(1)}, u32[]{:S(2)}, u32[]{:S(2)}) collective-permute-start(bf16[64,6144]{1,0:T(8,128)(2,1)} %get-tuple-element.52), channel_id=1, source_target_pairs={{0,2},{1,3},{2,0},{3,1},{4,6},{5,7},{6,4},{7,5},{8,10},{9,11},{10,... | collective-permute-start | bytes 2359304 | tf_op jit(solution)/shard_map/ppermute | solution.py:337
  237.3 47.9 %collective-permute-start.24 = (bf16[64,6144]{1,0:T(8,128)(2,1)}, bf16[64,6144]{1,0:T(8,128)(2,1)S(1)}, u32[]{:S(2)}, u32[]{:S(2)}) collective-permute-start(bf16[64,6144]{1,0:T(8,128)(2,1)} %get-tuple-element.51), channel_id=1, source_target_pairs={{0,4},{1,5},{2,6},{3,7},{4,0},{5,1},{6,2},{7,3},{8,12},{9,13},{10,... | collective-permute-start | bytes 2359304 | tf_op jit(solution)/shard_map/ppermute | solution.py:337
  238.5 46.6 %collective-permute-start.25 = (bf16[64,6144]{1,0:T(8,128)(2,1)}, bf16[64,6144]{1,0:T(8,128)(2,1)S(1)}, u32[]{:S(2)}, u32[]{:S(2)}) collective-permute-start(bf16[64,6144]{1,0:T(8,128)(2,1)} %get-tuple-element.50), channel_id=1, source_target_pairs={{0,6},{1,7},{2,4},{3,5},{4,2},{5,3},{6,0},{7,1},{8,14},{9,15},{10,... | collective-permute-start | bytes 2359304 | tf_op jit(solution)/shard_map/ppermute | solution.py:337
  241.4 35.6 %collective-permute-start.32 = (bf16[64,2048]{1,0:T(8,128)(2,1)}, bf16[64,2048]{1,0:T(8,128)(2,1)S(1)}, u32[]{:S(2)}, u32[]{:S(2)}) collective-permute-start(bf16[64,2048]{1,0:T(8,128)(2,1)} %get-tuple-element.55), channel_id=1, source_target_pairs={{0,4},{1,5},{2,6},{3,7},{4,0},{5,1},{6,2},{7,3},{8,12},{9,13},{10,... | collective-permute-start | bytes 786440 | tf_op jit(solution)/shard_map/ppermute | solution.py:337
  241.6 43.5 %collective-permute-start.33 = (bf16[64,2048]{1,0:T(8,128)(2,1)}, bf16[64,2048]{1,0:T(8,128)(2,1)S(1)}, u32[]{:S(2)}, u32[]{:S(2)}) collective-permute-start(bf16[64,2048]{1,0:T(8,128)(2,1)} %get-tuple-element.54), channel_id=1, source_target_pairs={{0,6},{1,7},{2,4},{3,5},{4,2},{5,3},{6,0},{7,1},{8,14},{9,15},{10,... | collective-permute-start | bytes 786440 | tf_op jit(solution)/shard_map/ppermute | solution.py:337
  (50 other events, 544.7 us)

commit v3 on v2

--- a/solution.py
+++ b/solution.py
@@ -33,9 +33,9 @@
 
 
 def inverse_matrix(start):
-    th = angles(np.arange(start, start + BLK, dtype=np.float64)).T / 1.0
+    th = angles(np.arange(start, start + BLK, dtype=np.float64)).T
     hi, lo = split_hi_lo(np.concatenate([np.cos(th), -np.sin(th)], 1) / BLK)
-    return np.concatenate([hi, lo], 0)
+    return np.concatenate([hi, lo], 1)
 
 
 def spectrum(fwd, rows):
@@ -48,90 +48,143 @@
     return jnp.concatenate([im[:h], -im[h:], -re[:h], re[h:]], 0)
 
 
-def product(a, b):
-    ar, ai, br, bi = a[:BLK], a[BLK:], b[:BLK], b[BLK:]
-    return jnp.concatenate([ar * br - ai * bi, ar * bi + ai * br], 0)
-
-
 def product_conj(a, b):
     ar, ai, br, bi = a[:BLK], a[BLK:], b[:BLK], b[BLK:]
     return jnp.concatenate([ar * br + ai * bi, ai * br - ar * bi], 0)
 
 
+def two_parts(y):
+    hi = y.astype(bf16)
+    return hi, (y - hi.astype(f32)).astype(bf16)
+
+
+def from_parts(inv, parts):
+    matrix = jnp.concatenate([inv[...], inv[:, : 2 * BLK]], 1)
+    return jnp.dot(matrix, parts, preferred_element_type=f32)
+
+
 def invert(inv, y):
-    hi = y.astype(bf16)
-    lo = (y - hi.astype(f32)).astype(bf16)
-    both = jnp.dot(inv, hi, preferred_element_type=f32)
-    return both[:BLK] + both[BLK:] + jnp.dot(inv[:BLK], lo, preferred_element_type=f32)
-
-
-def forward_kernel(order, proj, halo, sf, lf, skip, fwd, inv, gated, conv, act, mspec, fspec, ext):
+    hi, lo = two_parts(y)
+    return from_parts(inv, jnp.concatenate([hi, hi, lo], 0))
+
+
+def put_spectrum(buf, row, lanes, y):
+    hi, lo = two_parts(y)
+    n = y.shape[0]
+    buf[row : row + n, lanes] = hi
+    buf[2 * BLK + row : 2 * BLK + row + n, lanes] = hi
+    buf[4 * BLK + row : 4 * BLK + row + n, lanes] = lo
+
+
+def chunks(total, size):
+    return [(r, min(size, total - r)) for r in range(0, total, size)]
+
+
+ROWS = 32
+FREQS = 16
+
+
+def window_rows(spec, c, here, after):
+    sr, si = slice(c, c + FREQS), slice(BLK + c, BLK + c + FREQS)
+    wr, wi = spec[sr, here], spec[si, here]
+    if after is None:
+        return wr, wi
+    ar, ai = spec[sr, after], spec[si, after]
+    if c < BLK // 2:
+        return wr + ai, wi - ar
+    return wr - ai, wi + ar
+
+
+def forward_kernel(
+    proj, halo, sf, lf, skip, fwd, inv, gated, conv, act, mspec, fspec, ext, mix, spec, ybuf, out
+):
     rows = proj.shape[1]
-    fmat, imat = fwd[...], inv[...]
+    nb, wide = rows // BLK, proj.shape[2]
+    fmat = fwd[...]
+    edge = halo[BLK : BLK + PAD].astype(f32)
     for m in range(3):
-        ext[PAD : PAD + rows] = proj[m].astype(f32)
-        edge = halo[BLK : BLK + PAD].astype(f32)
-        ext[PAD - 2 : PAD] = edge[2 * m : 2 * m + 2]
-        total = sf[m, 0:1] * ext[PAD : PAD + rows]
-        for s in (1, 2):
-            total = total + sf[m, s : s + 1] * ext[PAD - s : PAD - s + rows]
-        act[m] = total
+        ext[m, PAD - 2 : PAD] = edge[2 * m : 2 * m + 2]
+        for r, n in chunks(rows, ROWS):
+            ext[m, PAD + r : PAD + r + n] = proj[m, r : r + n].astype(f32)
+    for h in range(2):
+        mix[h * BLK : (h + 1) * BLK, :wide] = halo[:BLK]
+    for r, n in chunks(rows, ROWS):
+        acts = []
+        for m in range(3):
+            total = sf[m, 0:1] * ext[m, PAD + r : PAD + r + n]
+            for s in (1, 2):
+                total = total + sf[m, s : s + 1] * ext[m, PAD - s + r : PAD - s + r + n]
+            act[m, r : r + n] = total
+            acts.append(total)
+        mixin = (acts[1] * acts[2]).astype(bf16)
+        at, lane = r % BLK, (r // BLK + 1) * wide
+        for h in range(2):
+            mix[h * BLK + at : h * BLK + at + n, lane : lane + wide] = mixin
     filt = spectrum(fmat, lf[...])
     fspec[...] = filt
-    nb, wide = rows // BLK, filt.shape[1]
-    mixins = [
-        (act[1, b * BLK : (b + 1) * BLK] * act[2, b * BLK : (b + 1) * BLK]).astype(bf16)
-        for b in range(nb)
-    ]
-    spec = spectrum(fmat, jnp.concatenate([halo[:BLK]] + mixins, 1))
-    window = spec[:, : nb * wide] + delay(spec[:, wide:])
-    out = invert(imat, product(window, jnp.concatenate([filt] * nb, 1)))
-    for b in range(nb):
-        span = slice(b * BLK, (b + 1) * BLK)
-        lanes = slice(b * wide, (b + 1) * wide)
-        mspec[b] = window[:, lanes]
-        full = out[:, lanes] + skip[...] * mixins[b].astype(f32)
-        conv[span] = full
-        gate = (act[0, span] * full).astype(bf16)
-        for half in range(2):
-            start = pl.multiple_of(order[2 * b + half], BLK // 2)
-            gated[pl.ds(start, BLK // 2)] = gate[half * (BLK // 2) : (half + 1) * (BLK // 2)]
+    spec[...] = jnp.dot(fmat, mix[...], preferred_element_type=f32)
+    for c in range(0, BLK, FREQS):
+        fr, fi = fspec[c : c + FREQS], fspec[BLK + c : BLK + c + FREQS]
+        for b in range(nb):
+            lanes = slice(b * wide, (b + 1) * wide)
+            wr, wi = window_rows(spec, c, lanes, slice((b + 1) * wide, (b + 2) * wide))
+            mspec[b, c : c + FREQS] = wr
+            mspec[b, BLK + c : BLK + c + FREQS] = wi
+            put_spectrum(ybuf, c, lanes, fr * wr - fi * wi)
+            put_spectrum(ybuf, BLK + c, lanes, fr * wi + fi * wr)
+    out[...] = from_parts(inv, ybuf[...])
+    for r, n in chunks(rows, ROWS):
+        at, lane = r % BLK, r // BLK * wide
+        mixin = mix[at : at + n, lane + wide : lane + 2 * wide].astype(f32)
+        full = out[at : at + n, lane : lane + wide] + skip[...] * mixin
+        conv[r : r + n] = full
+        gated[r : r + n] = (act[0, r : r + n] * full).astype(bf16)
 
 
 def backward_kernel(place, acc, act0, mspec, fspec, skip, fwd, inv, invlag, *refs):
     og, refs = refs[: 2 * SIDE], refs[2 * SIDE :]
-    weights, (bg, long0, long1, long2, long3, gmix, lagbuf) = refs[:4], refs[4:]
-    rows = bg.shape[0]
+    weights, refs = refs[:4], refs[4:]
+    bg, long0, long1, long2, long3, gmix, lagbuf, gbuf, spec, ybuf, lagy, out = refs
+    rows, wide = bg.shape
     nb = rows // BLK
-    fmat, imat = fwd[...], inv[...]
-    filt = fspec[...]
-    blocks = [w[n] for w in weights for n in range(2)]
     bg[...] = acc[...] + lax.dot_general(
         jnp.concatenate([o[...] for o in og], 1),
-        jnp.concatenate(blocks, 1),
+        jnp.concatenate([w[n] for w in weights for n in range(2)], 1),
         (((1,), (1,)), ((), ())),
         preferred_element_type=f32,
     )
-    wide = filt.shape[1]
-    grads = [
-        (bg[b * BLK : (b + 1) * BLK] * act0[0, b * BLK : (b + 1) * BLK]).astype(bf16)
-        for b in range(nb)
-    ]
-    spec = spectrum(fmat, jnp.concatenate(grads, 1))
-    lag = product_conj(spec[:, :wide], mspec[0])
-    for b in range(1, nb):
-        lag = lag + product_conj(spec[:, b * wide : (b + 1) * wide], mspec[b])
-    lagbuf[...] = invert(invlag[...], lag)
-    following = jnp.concatenate([spec[:, wide:], jnp.zeros(filt.shape, f32)], 1)
-    window = spec + delay(following)
-    out = invert(imat, product_conj(window, jnp.concatenate([filt] * nb, 1)))
-    for b in range(nb):
-        gm = out[:, b * wide : (b + 1) * wide] + skip[...] * grads[b].astype(f32)
-        gmix[b * BLK : (b + 1) * BLK] = gm
+    for r, n in chunks(rows, ROWS):
+        g = (bg[r : r + n] * act0[0, r : r + n]).astype(bf16)
+        at, lane = r % BLK, r // BLK * wide
+        for h in range(2):
+            gbuf[h * BLK + at : h * BLK + at + n, lane : lane + wide] = g
+    spec[...] = jnp.dot(fwd[...], gbuf[...], preferred_element_type=f32)
+    whole = slice(0, wide)
+    for c in range(0, BLK, FREQS):
+        sr, si = slice(c, c + FREQS), slice(BLK + c, BLK + c + FREQS)
+        fr, fi = fspec[sr], fspec[si]
+        lag_r = lag_i = None
+        for b in range(nb):
+            lanes = slice(b * wide, (b + 1) * wide)
+            after = slice((b + 1) * wide, (b + 2) * wide) if b + 1 < nb else None
+            gr, gi, mr, mi = spec[sr, lanes], spec[si, lanes], mspec[b, sr], mspec[b, si]
+            pr, pi = gr * mr + gi * mi, gi * mr - gr * mi
+            lag_r, lag_i = (pr, pi) if b == 0 else (lag_r + pr, lag_i + pi)
+            wr, wi = window_rows(spec, c, lanes, after)
+            put_spectrum(ybuf, c, lanes, wr * fr + wi * fi)
+            put_spectrum(ybuf, BLK + c, lanes, wi * fr - wr * fi)
+        put_spectrum(lagy, c, whole, lag_r)
+        put_spectrum(lagy, BLK + c, whole, lag_i)
+    lagbuf[...] = from_parts(invlag, lagy[...])
     quarter = BLK // SIDE
     for k, part in enumerate((long0, long1, long2, long3)):
         start = pl.multiple_of((place[0] ^ k) * quarter, quarter)
         part[...] = lagbuf[pl.ds(start, quarter)].astype(bf16)
+    out[...] = from_parts(inv, ybuf[...])
+    for r, n in chunks(rows, ROWS):
+        at, lane = r % BLK, r // BLK * wide
+        g = gbuf[at : at + n, lane : lane + wide].astype(f32)
+        gmix[r : r + n] = out[at : at + n, lane : lane + wide] + skip[...] * g
 
 
 def head_kernel(place, acc, act0, act12, convh, lf, skip, *refs):
@@ -156,24 +209,27 @@
 
 
 def finish_body(bg, conv, gmix, act, proj, sf, extra, gp, ext):
-    rows = bg.shape[0]
+    rows, wide = bg.shape
     sums = []
     for m in range(3):
-        if m == 0:
-            ga = bg[...] * conv[...]
-        else:
-            ga = gmix[...] * act[2 - m]
-        ext[:rows] = ga
-        ext[rows : rows + PAD] = extra[m]
-        x = proj[m].astype(f32)
-        total = sf[m, 0:1] * ga
-        sums.append(jnp.sum(x * ga, axis=0, keepdims=True))
-        for s in (1, 2):
-            moved = ext[s : s + rows]
-            total = total + sf[m, s : s + 1] * moved
-            sums.append(jnp.sum(x * moved, axis=0, keepdims=True))
-        gp[m] = total.astype(bf16)
-    return jnp.concatenate(sums + [jnp.zeros((7, bg.shape[1]), f32)], 0)
+        for r, n in chunks(rows, ROWS):
+            if m == 0:
+                ext[m, r : r + n] = bg[r : r + n] * conv[r : r + n]
+            else:
+                ext[m, r : r + n] = gmix[r : r + n] * act[2 - m, r : r + n]
+        ext[m, rows : rows + PAD] = extra[m]
+        parts = [jnp.zeros((8, wide), f32)] * 3
+        for r, n in chunks(rows, ROWS):
+            x = proj[m, r : r + n].astype(f32)
+            total = None
+            for s in range(3):
+                moved = ext[m, r + s : r + s + n]
+                term = sf[m, s : s + 1] * moved
+                total = term if s == 0 else total + term
+                parts[s] = parts[s] + jnp.sum((x * moved).reshape(n // 8, 8, wide), axis=0)
+            gp[m, r : r + n] = total.astype(bf16)
+        sums += [jnp.sum(p, axis=0, keepdims=True) for p in parts]
+    return jnp.concatenate(sums + [jnp.zeros((7, wide), f32)], 0)
 
 
 def top_kernel(bg, conv, gmix, act, bgn, convn, gmixn, actn, proj, sf, gp, short, ext):
@@ -188,7 +244,7 @@
     rows = bg.shape[0]
     late = delay(spectrum(fwd[...], halo[:BLK]))
     gfull[: rows - BLK] = gmix[: rows - BLK]
-    gfull[rows - BLK :] = gmix[rows - BLK :] + invert(inv[...], product_conj(late, fspec[...]))
+    gfull[rows - BLK :] = gmix[rows - BLK :] + invert(inv, product_conj(late, fspec[...]))
     edge = halo[BLK : BLK + PAD].astype(f32)
     zeros = jnp.zeros((PAD - 2, edge.shape[1]), f32)
     extra = [jnp.concatenate([edge[2 * m : 2 * m + 2], zeros], 0) for m in range(3)]
@@ -200,12 +256,12 @@
     if back:
         gated, og, refs = refs[0], refs[1 : 1 + SIDE], refs[1 + SIDE :]
         if more:
-            acc_in, refs = refs[0], refs[3:]
-        mine, other, acc, buf, sems = refs
+            acc_in, refs = refs[0], refs[2:]
+        result, acc, buf, sems = refs
     else:
-        gated, mine, other, buf, sems = refs
+        gated, result, buf, sems = refs
     step = pl.program_id(0)
-    chans, half = gated.shape[1], gated.shape[0] // 2
+    chans = gated.shape[1]
     width = buf.shape[2] // SIDE
 
     def copies(i):
@@ -236,9 +292,7 @@
                 c.wait()
 
     w = buf[step % 2]
-    out = jnp.dot(gated[...], w, preferred_element_type=f32).astype(bf16)
-    mine[...] = out[:half]
-    other[...] = out[half:]
+    result[...] = jnp.dot(gated[...], w, preferred_element_type=f32).astype(bf16)
     if back:
         acc[...] += lax.dot_general(
             jnp.concatenate([o[...] for o in og], 1),
@@ -265,11 +319,11 @@
         ]
         operands += [out_grad] * SIDE
         if more:
-            in_specs += [whole] + [pl.BlockSpec(memory_space=pl.ANY)] * 2
-            operands += [before[3], before[1], before[2]]
-            aliases = {len(operands) - 1: 0, len(operands): 1}
-    half_shape = jax.ShapeDtypeStruct((rows // 2, total * SIDE * width), bf16)
-    half_spec = pl.BlockSpec((rows // 2, SIDE * width), lambda i, c: (0, i + offset))
+            in_specs += [whole, pl.BlockSpec(memory_space=pl.ANY)]
+            operands += [before[2], before[1]]
+            aliases = {len(operands): 0}
+    result_shape = jax.ShapeDtypeStruct((rows, total * SIDE * width), bf16)
+    result_spec = pl.BlockSpec((rows, SIDE * width), lambda i, c: (0, i + offset))
 
     def kernel(cols_ref, *refs):
         del cols_ref
@@ -281,13 +335,13 @@
             num_scalar_prefetch=1,
             grid=(steps,),
             in_specs=in_specs,
-            out_specs=[half_spec, half_spec] + [whole] * back,
+            out_specs=[result_spec] + [whole] * back,
             scratch_shapes=[
                 pltpu.VMEM((2, chans, SIDE * width), bf16),
                 pltpu.SemaphoreType.DMA((2, SIDE)),
             ],
         ),
-        out_shape=[half_shape, half_shape] + [jax.ShapeDtypeStruct((rows, chans), f32)] * back,
+        out_shape=[result_shape] + [jax.ShapeDtypeStruct((rows, chans), f32)] * back,
         input_output_aliases=aliases,
         cost_estimate=pl.CostEstimate(
             flops=(2 + 2 * back) * rows * chans * width * SIDE * steps,
@@ -302,17 +356,13 @@
     mixed = refs[-1]
     width = mixed.shape[1] // sum(counts)
     begin = 0
-    for i, count in enumerate(counts):
-        parts = refs[4 * i : 4 * i + 4]
+    for ref, count in zip(refs, counts):
 
         @pl.loop(0, count)
-        def _(p, parts=parts, begin=begin):
+        def _(p, ref=ref, begin=begin):
             lanes = pl.ds(pl.multiple_of(p * width, width), width)
-            vals = [r[:, lanes].astype(f32) for r in parts]
             start = pl.multiple_of(cols[begin + p] * width, width)
-            mixed[:, pl.ds(start, width)] = (
-                (vals[0] + vals[1]) + (vals[2] + vals[3])
-            ).astype(bf16)
+            mixed[:, pl.ds(start, width)] = ref[:, lanes]
 
         begin += count
 
@@ -321,8 +371,8 @@
     rows, chans = projected.shape[1:]
     width = out_weight.shape[1] // 2
     ctx_count, tp_count = lax.axis_size("ctx"), lax.axis_size("tp")
-    me, tp = lax.axis_index("ctx"), lax.axis_index("tp")
-    zi, xi, yi, ci = me // SIDE, me % SIDE, tp // 2, tp % 2
+    me = lax.axis_index("ctx")
+    zi, xi = me // SIDE, me % SIDE
 
     def ring(value, axis, step):
         if axis == "x":
@@ -332,9 +382,8 @@
         return lax.ppermute(value, "ctx", pairs)
 
     def swap(value, axis, k):
-        shift = {"x": k, "z": k * SIDE, "core": k, "y": 2 * k}[axis]
-        name = "ctx" if axis in "xz" else "tp"
-        return lax.ppermute(value, name, [(d, d ^ shift) for d in range(lax.axis_size(name))])
+        shift = {"x": k, "z": k * SIDE}[axis]
+        return lax.ppermute(value, "ctx", [(d, d ^ shift) for d in range(ctx_count)])
 
     def gather(piece, first, second):
         h = piece.shape[0] // 2
@@ -411,13 +460,6 @@
     fwd = jnp.asarray(forward_matrix())
     inv_late, inv_now, inv_lag = (jnp.asarray(inverse_matrix(s)) for s in (BLK, 0, -BLK))
     skip_row = skip_gain[None, :]
-    share = rows // tp_count
-    order = jnp.stack(
-        [
-            (((t % 2) ^ ci) * SIDE + ((t // 2) ^ yi)) * share
-            for t in range(tp_count)
-        ]
-    ).astype(jnp.int32)
     tile = 256
     grid = (chans // tile,)
     nb = rows // BLK
@@ -426,17 +468,21 @@
         return pl.BlockSpec((*lead, tile), lambda i, *_: (*([0] * len(lead)), i))
 
     const = pl.BlockSpec((2 * BLK, 2 * BLK), lambda i, *_: (0, 0))
+    const_inv = pl.BlockSpec((BLK, 4 * BLK), lambda i, *_: (0, 0))
     forward = pl.pallas_call(
         forward_kernel,
-        grid_spec=pltpu.PrefetchScalarGridSpec(
-            num_scalar_prefetch=1,
-            grid=grid,
-            in_specs=[
-                col(3, rows), col(BLK + PAD), col(3, 3), col(BLK), col(1), const, const,
-            ],
-            out_specs=[col(rows), col(rows), col(3, rows), col(nb, 2 * BLK), col(2 * BLK)],
-            scratch_shapes=[pltpu.VMEM((rows + PAD, tile), f32)],
-        ),
+        grid=grid,
+        in_specs=[
+            col(3, rows), col(BLK + PAD), col(3, 3), col(BLK), col(1), const, const_inv,
+        ],
+        out_specs=[col(rows), col(rows), col(3, rows), col(nb, 2 * BLK), col(2 * BLK)],
+        scratch_shapes=[
+            pltpu.VMEM((3, rows + PAD, tile), f32),
+            pltpu.VMEM((2 * BLK, (nb + 1) * tile), bf16),
+            pltpu.VMEM((2 * BLK, (nb + 1) * tile), f32),
+            pltpu.VMEM((6 * BLK, nb * tile), bf16),
+            pltpu.VMEM((BLK, nb * tile), f32),
+        ],
         out_shape=[
             jax.ShapeDtypeStruct((rows, chans), bf16),
             jax.ShapeDtypeStruct((rows, chans), f32),
@@ -445,27 +491,22 @@
             jax.ShapeDtypeStruct((2 * BLK, chans), f32),
         ],
         cost_estimate=pl.CostEstimate(
-            flops=12_000_000_000, bytes_accessed=20 << 20, transcendentals=0
+            flops=8_000_000_000, bytes_accessed=20 << 20, transcendentals=0
         ),
         name="forward",
     )
     gated, conv, act, mspec, fspec = forward(
-        order, projected, left, short_filter, long_filter, skip_row, fwd, inv_late
-    )
-
-    def scatter(mine, other):
-        got = swap(other, "core", 1)
-        parts = [
-            (mine[k * share : (k + 1) * share].astype(f32) + got[k * share : (k + 1) * share].astype(f32)).astype(bf16)
-            for k in range(SIDE)
-        ]
-        return [parts[0]] + [swap(parts[k], "y", k) for k in (1, 2, 3)]
+        projected, left, short_filter, long_filter, skip_row, fwd, inv_late
+    )
+
+    def scatter(value):
+        return lax.psum_scatter(value, "tp", scatter_dimension=0, tiled=True)
 
     early = multiply_pieces(near_a + near_b, cols1, gated, out_grad, 6)
-    mine1, other1, acc = multiply_pieces(
+    out1, acc = multiply_pieces(
         mid_a + mid_b, cols2, gated, out_grad, 6, (2, *early)
     )
-    out1 = scatter(mine1, other1)
+    out1 = scatter(out1)
 
     quarter = BLK // SIDE
     place = jnp.concatenate([jnp.reshape(zi, (1,)), cols3]).astype(jnp.int32)
@@ -522,13 +563,20 @@
                 col(2 * BLK),
                 col(1),
                 const,
-                const,
-                const,
+                const_inv,
+                const_inv,
                 *out_grad_rows(rows),
                 *[last_spec] * 4,
             ],
             out_specs=[col(rows)] + [col(quarter)] * 4 + [col(rows)],
-            scratch_shapes=[pltpu.VMEM((BLK, tile), f32)],
+            scratch_shapes=[
+                pltpu.VMEM((BLK, tile), f32),
+                pltpu.VMEM((2 * BLK, nb * tile), bf16),
+                pltpu.VMEM((2 * BLK, nb * tile), f32),
+                pltpu.VMEM((6 * BLK, nb * tile), bf16),
+                pltpu.VMEM((6 * BLK, tile), bf16),
+                pltpu.VMEM((BLK, nb * tile), f32),
+            ],
         ),
         out_shape=[jax.ShapeDtypeStruct((rows, chans), f32)]
         + [long_shape] * 4
@@ -549,8 +597,8 @@
     sums = [g[BLK + PAD :].astype(f32) for g in got]
     my_quarter = (sums[0] + sums[1]) + (sums[2] + sums[3])
 
-    mine3, other3 = multiply_pieces(far_a + far_b, cols3, gated)
-    out3 = scatter(mine3, other3)
+    (out3,) = multiply_pieces(far_a + far_b, cols3, gated)
+    out3 = scatter(out3)
 
     low = rows - BLK - PAD
 
@@ -576,7 +624,7 @@
         ],
         out_specs=[rows_at(0, low, 3), col(16)],
         out_shape=[gp_shape, short_shape],
-        scratch_shapes=[pltpu.VMEM((low + PAD, tile), f32)],
+        scratch_shapes=[pltpu.VMEM((3, low + PAD, tile), f32)],
         cost_estimate=pl.CostEstimate(
             flops=200_000_000, bytes_accessed=10 << 20, transcendentals=0
         ),
@@ -589,12 +637,12 @@
         grid=grid,
         in_specs=[
             rows_at(low, rest), rows_at(low, rest), rows_at(low, rest), acts_at(low, rest),
-            col(BLK + PAD), rows_at(low, rest, 3), col(3, 3), col(2 * BLK), const, const, col(16),
+            col(BLK + PAD), rows_at(low, rest, 3), col(3, 3), col(2 * BLK), const, const_inv, col(16),
             pl.BlockSpec(memory_space=pl.ANY),
         ],
         out_specs=[rows_at(low, rest, 3), col(16)],
         out_shape=[gp_shape, short_shape],
-        scratch_shapes=[pltpu.VMEM((rest + PAD, tile), f32), pltpu.VMEM((rest, tile), f32)],
+        scratch_shapes=[pltpu.VMEM((3, rest + PAD, tile), f32), pltpu.VMEM((rest, tile), f32)],
         input_output_aliases={11: 0},
         cost_estimate=pl.CostEstimate(
             flops=2_000_000_000, bytes_accessed=5 << 20, transcendentals=0
@@ -613,24 +661,21 @@
     long_total = jnp.concatenate([pick(got, zi ^ q)[:quarter] for q in range(SIDE)], 0)
     short_total = message[quarter : quarter + 9].reshape(3, 3, chans)
 
-    counts = tuple(o[0].shape[1] // width for o in (out1, out3))
+    share = rows // tp_count
+    counts = tuple(o.shape[1] // width for o in (out1, out3))
     collect = pl.pallas_call(
         lambda cols, *refs: collect_kernel(counts, cols, *refs),
         grid_spec=pltpu.PrefetchScalarGridSpec(
             num_scalar_prefetch=1,
             grid=(1,),
-            in_specs=[
-                pl.BlockSpec(o[0].shape, lambda i, c: (0, 0))
-                for o in (out1, out3)
-                for _ in range(SIDE)
-            ],
+            in_specs=[pl.BlockSpec(o.shape, lambda i, c: (0, 0)) for o in (out1, out3)],
             out_specs=pl.BlockSpec((share, 2 * width * ctx_count), lambda i, c: (0, 0)),
         ),
         out_shape=jax.ShapeDtypeStruct((share, 2 * width * ctx_count), bf16),
         cost_estimate=pl.CostEstimate(flops=10_000_000, bytes_accessed=5 << 20, transcendentals=0),
         name="collect",
     )
-    mixed = collect(jnp.concatenate([cols1, cols2, cols3]), *out1, *out3)
+    mixed = collect(jnp.concatenate([cols1, cols2, cols3]), out1, out3)
 
     scale = 1.0 / math.sqrt(rows * ctx_count)
     return mixed, gp, long_total.astype(f32) * scale, short_total * scale

time: 294 us -> 242 us (0.82)
  waiting for transfers between devices: 95.6 us -> 54.6 us
  between operations: 8.96 us -> 22.3 us
  other arithmetic: 19.4 us -> 11 us
  local copies, waits for them, and re-layouts: 18.9 us -> 11.8 us
  starting transfers between devices: 66.4 us -> 61.3 us
    ppermute x26 -> x18, waiting for transfers between devices: 61.8 us -> 38.1 us  [swap(): lax.ppermute(value, 'ctx', [(d, d ^ shift) for d in range(ctx_count)])]
    ppermute x20, waiting for transfers between devices: 33.8 us -> 16.4 us  [ring(): return lax.ppermute(value, 'ctx', pairs)]
    ppermute x26 -> x18, starting transfers between devices: 35.2 us -> 25.4 us  [swap(): lax.ppermute(value, 'ctx', [(d, d ^ shift) for d in range(ctx_count)])]
    convert_element_type x2 -> x0, other arithmetic: 6.92 us -> none  [scatter(): (mine[k * share:(k + 1) * share].astype(f32) + got[k * share:(k + 1) * sh...]
    ppermute x20, starting transfers between devices: 31.2 us -> 35.9 us  [ring(): return lax.ppermute(value, 'ctx', pairs)]
    unnamed x62 -> x48, local copies, waits for them, and re-layouts: 7.52 us -> 2.94 us
  transfers between devices with their start and end apart: 46 -> 40, of which waited for: 13 -> 16; matrix products, arithmetic and copies ran while one was open for 11% -> 8% of each run, Pallas kernels for 27% -> 29%
where the time goes in v3:
time: 242 us; the launch traced here: 241 us
  Pallas kernels  79.5 us (33%)
  starting transfers between devices  61.3 us (25%)
  waiting for transfers between devices  54.6 us (23%)
  between operations  22.3 us (9%)
  local copies, waits for them, and re-layouts  11.8 us (5%)
  other arithmetic  11 us (5%)
    ppermute x18, waiting for transfers between devices, swap(): lax.ppermute(value, 'ctx', [(d, d ^ shift) for d in range(ctx_count)])  38.1 us
    ppermute x20, starting transfers between devices, ring(): return lax.ppermute(value, 'ctx', pairs)  35.9 us
    pallas_call x3, Pallas kernels, multiply_pieces(): pl.pallas_call(kernel, grid_spec=pltpu.PrefetchScalarGridSpec(num_scalar_...  33.3 us
    ppermute x18, starting transfers between devices, swap(): lax.ppermute(value, 'ctx', [(d, d ^ shift) for d in range(ctx_count)])  25.4 us
    ppermute x20, waiting for transfers between devices, ring(): return lax.ppermute(value, 'ctx', pairs)  16.4 us
    pallas_call x1, Pallas kernels, on_device(): backward(place, acc, act, mspec, fspec, skip_row, fwd, inv_now, inv_lag,...  14 us
    pallas_call x1, Pallas kernels, on_device(): forward(projected, left, short_filter, long_filter, skip_row, fwd, inv_late)  8.9 us
    pallas_call x1, Pallas kernels, on_device(): top(bg, conv, gmix, act, bg, conv, gmix, act, projected, short_filter)  7.8 us
  transfers between devices with their start and end apart: 40, of which 16 were waited for; matrix products, arithmetic and copies ran while one was open for 8% of the time, Pallas kernels for 29%

profile of v3, /device:TPU:24, one launch (start us, length us, event | category | flops | bytes accessed | tf_op | source)
XLA Modules:
  0.0 240.6 jit_solution(10658569751436263641)
XLA Ops:
  23.5 2.7 %collective-permute-start.16 = (bf16[136,1024]{1,0:T(8,128)(2,1)S(1)}, bf16[136,1024]{1,0:T(8,128)(2,1)S(1)}, u32[]{:S(2)}, u32[]{:S(2)}) collective-permute-start(bf16[136,1024]{1,0:T(8,128)(2,1)S(1)} %maximum_maximum_fusion), channel_id=1, source_target_pairs={{0,24},{8,16},{16,8},{24,0},{32,56},{40,48},{48,40},{56,32},{64,88... | collective-permute-start | bytes 835592 | tf_op jit(solution)/shard_map/ppermute | solution.py:386
  28.4 3.3 %collective-permute-start.4 = (bf16[512,256]{1,0:T(8,128)(2,1)S(1)}, bf16[512,256]{1,0:T(8,128)(2,1)S(1)}, u32[]{:S(2)}, u32[]{:S(2)}) collective-permute-start(bf16[512,256]{1,0:T(8,128)(2,1)S(1)} %slice.109), channel_id=1, source_target_pairs={{0,24},{8,0},{16,8},{24,16},{32,56},{40,32},{48,40},{56,48},{64,88... | collective-permute-start | bytes 786440 | tf_op jit(solution)/shard_map/ppermute | solution.py:382
  37.9 4.0 %collective-permute-start.12 = (bf16[512,256]{1,0:T(8,128)(2,1)S(1)}, bf16[512,256]{1,0:T(8,128)(2,1)S(1)}, u32[]{:S(2)}, u32[]{:S(2)}) collective-permute-start(bf16[512,256]{1,0:T(8,128)(2,1)S(1)} %slice.111), channel_id=1, source_target_pairs={{0,96},{8,104},{16,112},{24,120},{32,0},{40,8},{48,16},{56,24},{64... | collective-permute-start | bytes 786440 | tf_op jit(solution)/shard_map/ppermute | solution.py:382
  43.1 2.7 %collective-permute-done.12 = bf16[512,256]{1,0:T(8,128)(2,1)S(1)} collective-permute-done((bf16[512,256]{1,0:T(8,128)(2,1)S(1)}, bf16[512,256]{1,0:T(8,128)(2,1)S(1)}, u32[]{:S(2)}, u32[]{:S(2)}) %collective-permute-start.12) | collective-permute-done | bytes 262176 | tf_op jit(solution)/shard_map/ppermute | solution.py:382
  45.9 3.8 %collective-permute-start.7 = (bf16[2048,256]{1,0:T(8,128)(2,1)S(1)}, bf16[2048,256]{1,0:T(8,128)(2,1)}, u32[]{:S(2)}, u32[]{:S(2)}) collective-permute-start(bf16[2048,256]{1,0:T(8,128)(2,1)S(1)} %constant_dynamic-update-slice_fusion.refs_1_), channel_id=1, source_target_pairs={{0,96},{8,104},{16,112},{24,120},{32,0},{40,8},{48,16},{56,24},{64... | collective-permute-start | bytes 3145736 | tf_op jit(solution)/shard_map/ppermute | solution.py:382
  49.7 3.2 %collective-permute-start.15 = (bf16[2048,256]{1,0:T(8,128)(2,1)S(1)}, bf16[2048,256]{1,0:T(8,128)(2,1)}, u32[]{:S(2)}, u32[]{:S(2)}) collective-permute-start(bf16[2048,256]{1,0:T(8,128)(2,1)S(1)} %constant_dynamic-update-slice_fusion.3.refs_3_), channel_id=1, source_target_pairs={{0,24},{8,0},{16,8},{24,16},{32,56},{40,32},{48,40},{56,48},{64,88... | collective-permute-start | bytes 3145736 | tf_op jit(solution)/shard_map/ppermute | solution.py:382
  54.2 20.1 %collective-permute-done.21 = bf16[136,1024]{1,0:T(8,128)(2,1)S(1)} collective-permute-done((bf16[136,1024]{1,0:T(8,128)(2,1)S(1)}, bf16[136,1024]{1,0:T(8,128)(2,1)S(1)}, u32[]{:S(2)}, u32[]{:S(2)}) %collective-permute-start.21) | collective-permute-done | bytes 278560 | tf_op jit(solution)/shard_map/ppermute | solution.py:386
  75.5 9.8 %collective-permute-done.19 = bf16[136,1024]{1,0:T(8,128)(2,1)S(1)} collective-permute-done((bf16[136,1024]{1,0:T(8,128)(2,1)S(1)}, bf16[136,1024]{1,0:T(8,128)(2,1)S(1)}, u32[]{:S(2)}, u32[]{:S(2)}) %collective-permute-start.19) | collective-permute-done | bytes 278560 | tf_op jit(solution)/shard_map/ppermute | solution.py:386
  88.1 3.2 %collective-permute-start.23 = (bf16[2048,256]{1,0:T(8,128)(2,1)}, bf16[2048,256]{1,0:T(8,128)(2,1)S(1)}, u32[]{:S(2)}, u32[]{:S(2)}) collective-permute-start(bf16[2048,256]{1,0:T(8,128)(2,1)} %collective-permute-done.7.refs_3_), channel_id=1, source_target_pairs={{0,96},{8,104},{16,112},{24,120},{32,0},{40,8},{48,16},{56,24},{64... | collective-permute-start | bytes 3145736 | tf_op jit(solution)/shard_map/ppermute | solution.py:382
  91.3 2.9 %collective-permute-start.25 = (bf16[2048,256]{1,0:T(8,128)(2,1)}, bf16[2048,256]{1,0:T(8,128)(2,1)}, u32[]{:S(2)}, u32[]{:S(2)}) collective-permute-start(bf16[2048,256]{1,0:T(8,128)(2,1)} %collective-permute-done.15.refs_7_), channel_id=1, source_target_pairs={{0,24},{8,0},{16,8},{24,16},{32,56},{40,32},{48,40},{56,48},{64,88... | collective-permute-start | bytes 3145736 | tf_op jit(solution)/shard_map/ppermute | solution.py:382
  99.1 8.9 %forward.1 = (bf16[512,1024]{1,0:T(8,128)(2,1)}, f32[512,1024]{1,0:T(8,128)}, f32[3,512,1024]{2,1,0:T(8,128)}, f32[4,256,1024]{2,1,0:T(8,128)}, f32[256,1024]{1,0:T(8,128)}) custom-call(bf16[3,512,1024]{2,1,0:T(8,128)(2,1)} %proj.5, bf16[136,1024]{1,0:T(8,128)(2,1)} %select_select_fusion.3.halo, f32[3,3,1024]{2,1,0:T(4,128)} %sf.5, bf16[128,1024]{1,0:T(8,128)(2,1)} %lf.3, ...), custom_call_target="tpu_custom_call" | custom-call | flops 8000000000 | bytes 20971520 | tf_op jit(solution)/shard_map/forward/pallas_call | solution.py:498
  112.1 7.1 %pieces.5 = bf16[512,2048]{1,0:T(8,128)(2,1)} custom-call(s32[8]{0:T(128)} %stack.139.cols_ref, bf16[2048,256]{1,0:T(8,128)(2,1)} %copy-done, bf16[2048,256]{1,0:T(8,128)(2,1)} %copy-done.2, bf16[2048,256]{1,0:T(8,128)(2,1)} %copy-done.1, bf16[2048,256]{1,0:T(8,128)(2,1)} %collective-permute-done.25.refs_3_, bf16[512,1024]{1,0:T(8,128)(2,1)} %get-tuple-element.23.refs_4_.refs_8_), custom_call_target="tpu_custom_call" | custom-call | flops 2147483648 | bytes 11534336 | tf_op jit(solution)/shard_map/pieces/pallas_call | solution.py:332
  121.0 3.0 %collective-permute-start.14 = (bf16[2048,256]{1,0:T(8,128)(2,1)S(1)}, bf16[2048,256]{1,0:T(8,128)(2,1)}, u32[]{:S(2)}, u32[]{:S(2)}) collective-permute-start(bf16[2048,256]{1,0:T(8,128)(2,1)S(1)} %copy-done.6), channel_id=1, source_target_pairs={{0,24},{8,0},{16,8},{24,16},{32,56},{40,32},{48,40},{56,48},{64,88... | collective-permute-start | bytes 3145736 | tf_op jit(solution)/shard_map/ppermute | solution.py:382
  126.7 10.2 %pieces.3 = (bf16[512,6144]{1,0:T(8,128)(2,1)}, f32[512,1024]{1,0:T(8,128)}) custom-call(s32[8]{0:T(128)} %stack.138.cols_ref, bf16[2048,256]{1,0:T(8,128)(2,1)} %copy-done.3, bf16[2048,256]{1,0:T(8,128)(2,1)} %copy-done.9, bf16[2048,256]{1,0:T(8,128)(2,1)} %copy-done.5, bf16[2048,256]{1,0:T(8,128)(2,1)} %copy-done.8, ...), custom_call_target="tpu_custom_call" | custom-call | flops 4294967296 | bytes 11534336 | tf_op jit(solution)/shard_map/pieces/pallas_call | solution.py:332
  139.8 3.7 %collective-permute-done.5.refs_1_ = bf16[2048,256]{1,0:T(8,128)(2,1)} collective-permute-done((bf16[2048,256]{1,0:T(8,128)(2,1)}, bf16[2048,256]{1,0:T(8,128)(2,1)}, u32[]{:S(2)}, u32[]{:S(2)}) %collective-permute-start.5) | collective-permute-done | bytes 1048608 | tf_op jit(solution)/shard_map/ppermute | solution.py:382
  144.7 16.0 %pieces.4 = (bf16[512,6144]{1,0:T(8,128)(2,1)}, f32[512,1024]{1,0:T(8,128)}) custom-call(s32[16]{0:T(128)} %stack.137.cols_ref, bf16[2048,256]{1,0:T(8,128)(2,1)} %collective-permute-done.1.refs_0_, bf16[2048,256]{1,0:T(8,128)(2,1)} %collective-permute-done.5.refs_1_, bf16[2048,256]{1,0:T(8,128)(2,1)} %copy-done.13, ...), custom_call_target="tpu_custom_call", output_to_operand_aliasing={{0}: (15, {})} | custom-call | flops 8589934592 | bytes 19922944 | tf_op jit(solution)/shard_map/pieces/pallas_call | solution.py:332
  163.1 6.4 %head.1 = bf16[136,1024]{1,0:T(8,128)(2,1)} custom-call(s32[9]{0:T(128)} %concatenate.45.place, f32[512,1024]{1,0:T(8,128)} %get-tuple-element.27.acc, f32[3,512,1024]{2,1,0:T(8,128)} %get-tuple-element.28.act0.act12.act.actn, f32[3,512,1024]{2,1,0:T(8,128)} %get-tuple-element.28.act0.act12.act.actn, f32[512,1024]{1,0:T(8,128)} %get-tuple-element.32.convh.conv.convn, ...), custom_call_target="tpu_custom_call" | custom-call | flops 600000000 | bytes 6291456 | tf_op jit(solution)/shard_map/head/pallas_call | solution.py:550
  169.7 4.0 %collective-permute-start.27 = (bf16[136,1024]{1,0:T(8,128)(2,1)}, bf16[136,1024]{1,0:T(8,128)(2,1)S(1)}, u32[]{:S(2)}, u32[]{:S(2)}) collective-permute-start(bf16[136,1024]{1,0:T(8,128)(2,1)} %head.1), channel_id=1, source_target_pairs={{0,16},{8,24},{16,0},{24,8},{32,48},{40,56},{48,32},{56,40},{64,80... | collective-permute-start | bytes 835592 | tf_op jit(solution)/shard_map/ppermute | solution.py:386
  173.7 14.0 %backward.1 = (f32[512,1024]{1,0:T(8,128)}, bf16[32,1024]{1,0:T(8,128)(2,1)}, bf16[32,1024]{1,0:T(8,128)(2,1)}, bf16[32,1024]{1,0:T(8,128)(2,1)}, bf16[32,1024]{1,0:T(8,128)(2,1)}, /*index=5*/f32[512,1024]{1,0:T(8,128)}) custom-call(s32[9]{0:T(128)} %concatenate.45.place, f32[512,1024]{1,0:T(8,128)} %get-tuple-element.27.acc, ...), custom_call_target="tpu_custom_call" | custom-call | flops 8000000000 | bytes 20971520 | tf_op jit(solution)/shard_map/backward/pallas_call | solution.py:589
  195.8 7.8 %top.1 = (bf16[3,512,1024]{2,1,0:T(8,128)(2,1)}, f32[16,1024]{1,0:T(8,128)}) custom-call(f32[512,1024]{1,0:T(8,128)} %get-tuple-element.31.bg.bgn, f32[512,1024]{1,0:T(8,128)} %get-tuple-element.32.convh.conv.convn, f32[512,1024]{1,0:T(8,128)} %get-tuple-element.33.gmix.gmixn, f32[3,512,1024]{2,1,0:T(8,128)} %get-tuple-element.28.act0.act12.act.actn, ...), custom_call_target="tpu_custom_call" | custom-call | flops 200000000 | bytes 10485760 | tf_op jit(solution)/shard_map/top/pallas_call | solution.py:633
  205.4 6.1 %bottom.1 = (bf16[3,512,1024]{2,1,0:T(8,128)(2,1)}, f32[16,1024]{1,0:T(8,128)}) custom-call(f32[512,1024]{1,0:T(8,128)} %get-tuple-element.31.bg.bgn, f32[512,1024]{1,0:T(8,128)} %get-tuple-element.32.convh.conv.convn, f32[512,1024]{1,0:T(8,128)} %get-tuple-element.33.gmix.gmixn, ...), custom_call_target="tpu_custom_call", output_to_operand_aliasing={{0}: (11, {})} | custom-call | flops 2000000000 | bytes 5242880 | tf_op jit(solution)/shard_map/bottom/pallas_call | solution.py:652
  216.6 2.8 %collective-permute-done.34 = bf16[48,1024]{1,0:T(8,128)(2,1)S(1)} collective-permute-done((bf16[48,1024]{1,0:T(8,128)(2,1)S(1)}, bf16[48,1024]{1,0:T(8,128)(2,1)S(1)}, u32[]{:S(2)}, u32[]{:S(2)}) %collective-permute-start.34) | collective-permute-done | bytes 98336 | tf_op jit(solution)/shard_map/ppermute | solution.py:386
  220.4 2.9 %collective-permute-start.36 = (bf16[48,1024]{1,0:T(8,128)(2,1)S(1)}, bf16[48,1024]{1,0:T(8,128)(2,1)S(1)}, u32[]{:S(2)}, u32[]{:S(2)}) collective-permute-start(bf16[48,1024]{1,0:T(8,128)(2,1)S(1)} %add_convert_fusion), channel_id=1, source_target_pairs={{0,64},{8,72},{16,80},{24,88},{32,96},{40,104},{48,112},{56,120},{... | collective-permute-start | bytes 294920 | tf_op jit(solution)/shard_map/ppermute | solution.py:386
  230.7 3.1 %collect.1 = bf16[64,8192]{1,0:T(8,128)(2,1)} custom-call(s32[32]{0:T(128)} %concatenate.39.cols, bf16[64,6144]{1,0:T(8,128)(2,1)} %reduce-scatter.3.cloned.1.call-done.refs_0_, bf16[64,2048]{1,0:T(8,128)(2,1)} %reduce-scatter.5.cloned.1.call-done.refs_1_), custom_call_target="tpu_custom_call" | custom-call | flops 10000000 | bytes 5242880 | tf_op jit(solution)/shard_map/collect/pallas_call | solution.py:678
  (158 shorter events, 66.6 us)
Async XLA Ops:
  7.2 223.5 %reduce-scatter.5.cloned.1.call-start = ((), (), s32[]{:S(2)}) async-start(), calls=%async_computation.3 | async-start | bytes 2359296 | tf_op jit(solution)/shard_map/reduce_scatter | solution.py:503
  8.5 15.0 %collective-permute-start = (bf16[1024,256]{1,0:T(8,128)(2,1)S(1)}, bf16[1024,256]{1,0:T(8,128)(2,1)}, u32[]{:S(2)}, u32[]{:S(2)}) collective-permute-start(bf16[1024,256]{1,0:T(8,128)(2,1)S(1)} %get-tuple-element.49), channel_id=1, source_target_pairs={{0,8},{8,16},{16,24},{24,0},{32,40},{40,48},{48,56},{56,32},{64,72... | collective-permute-start | bytes 1572872 | tf_op jit(solution)/shard_map/ppermute | solution.py:382
  10.1 17.1 %collective-permute-start.2 = (bf16[1024,256]{1,0:T(8,128)(2,1)S(1)}, bf16[1024,256]{1,0:T(8,128)(2,1)S(1)}, u32[]{:S(2)}, u32[]{:S(2)}) collective-permute-start(bf16[1024,256]{1,0:T(8,128)(2,1)S(1)} %get-tuple-element.49), channel_id=1, source_target_pairs={{0,24},{8,0},{16,8},{24,16},{32,56},{40,32},{48,40},{56,48},{64,88... | collective-permute-start | bytes 1572872 | tf_op jit(solution)/shard_map/ppermute | solution.py:382
  11.8 16.6 %collective-permute-start.8 = (bf16[1024,256]{1,0:T(8,128)(2,1)S(1)}, bf16[1024,256]{1,0:T(8,128)(2,1)}, u32[]{:S(2)}, u32[]{:S(2)}) collective-permute-start(bf16[1024,256]{1,0:T(8,128)(2,1)S(1)} %get-tuple-element.48), channel_id=1, source_target_pairs={{0,32},{8,40},{16,48},{24,56},{32,64},{40,72},{48,80},{56,88},{64,... | collective-permute-start | bytes 1572872 | tf_op jit(solution)/shard_map/ppermute | solution.py:382
  13.7 20.4 %collective-permute-start.10 = (bf16[1024,256]{1,0:T(8,128)(2,1)S(1)}, bf16[1024,256]{1,0:T(8,128)(2,1)S(1)}, u32[]{:S(2)}, u32[]{:S(2)}) collective-permute-start(bf16[1024,256]{1,0:T(8,128)(2,1)S(1)} %get-tuple-element.48), channel_id=1, source_target_pairs={{0,96},{8,104},{16,112},{24,120},{32,0},{40,8},{48,16},{56,24},{64... | collective-permute-start | bytes 1572872 | tf_op jit(solution)/shard_map/ppermute | solution.py:382
  18.5 27.4 %collective-permute-start.18 = (bf16[136,1024]{1,0:T(8,128)(2,1)S(1)}, bf16[136,1024]{1,0:T(8,128)(2,1)S(1)}, u32[]{:S(2)}, u32[]{:S(2)}) collective-permute-start(bf16[136,1024]{1,0:T(8,128)(2,1)S(1)} %maximum_maximum_fusion), channel_id=1, source_target_pairs={{0,8},{8,0},{16,24},{24,16},{32,40},{40,32},{48,56},{56,48},{64,72... | collective-permute-start | bytes 835592 | tf_op jit(solution)/shard_map/ppermute | solution.py:386
  23.5 26.1 %collective-permute-start.16 = (bf16[136,1024]{1,0:T(8,128)(2,1)S(1)}, bf16[136,1024]{1,0:T(8,128)(2,1)S(1)}, u32[]{:S(2)}, u32[]{:S(2)}) collective-permute-start(bf16[136,1024]{1,0:T(8,128)(2,1)S(1)} %maximum_maximum_fusion), channel_id=1, source_target_pairs={{0,24},{8,16},{16,8},{24,0},{32,56},{40,48},{48,40},{56,32},{64,88... | collective-permute-start | bytes 835592 | tf_op jit(solution)/shard_map/ppermute | solution.py:386
  42.7 44.7 %collective-permute-start.1 = (bf16[2048,256]{1,0:T(8,128)(2,1)S(1)}, bf16[2048,256]{1,0:T(8,128)(2,1)}, u32[]{:S(2)}, u32[]{:S(2)}) collective-permute-start(bf16[2048,256]{1,0:T(8,128)(2,1)S(1)} %pad_maximum_fusion.refs_0_), channel_id=1, source_target_pairs={{0,32},{8,40},{16,48},{24,56},{32,64},{40,72},{48,80},{56,88},{64,... | collective-permute-start | bytes 3145736 | tf_op jit(solution)/shard_map/ppermute | solution.py:382
  45.8 41.6 %collective-permute-start.9 = (bf16[2048,256]{1,0:T(8,128)(2,1)S(1)}, bf16[2048,256]{1,0:T(8,128)(2,1)}, u32[]{:S(2)}, u32[]{:S(2)}) collective-permute-start(bf16[2048,256]{1,0:T(8,128)(2,1)S(1)} %pad_maximum_fusion.1.refs_2_), channel_id=1, source_target_pairs={{0,8},{8,16},{16,24},{24,0},{32,40},{40,48},{48,56},{56,32},{64,72... | collective-permute-start | bytes 3145736 | tf_op jit(solution)/shard_map/ppermute | solution.py:382
  45.9 42.2 %collective-permute-start.7 = (bf16[2048,256]{1,0:T(8,128)(2,1)S(1)}, bf16[2048,256]{1,0:T(8,128)(2,1)}, u32[]{:S(2)}, u32[]{:S(2)}) collective-permute-start(bf16[2048,256]{1,0:T(8,128)(2,1)S(1)} %constant_dynamic-update-slice_fusion.refs_1_), channel_id=1, source_target_pairs={{0,96},{8,104},{16,112},{24,120},{32,0},{40,8},{48,16},{56,24},{64... | collective-permute-start | bytes 3145736 | tf_op jit(solution)/shard_map/ppermute | solution.py:382
  49.7 41.6 %collective-permute-start.15 = (bf16[2048,256]{1,0:T(8,128)(2,1)S(1)}, bf16[2048,256]{1,0:T(8,128)(2,1)}, u32[]{:S(2)}, u32[]{:S(2)}) collective-permute-start(bf16[2048,256]{1,0:T(8,128)(2,1)S(1)} %constant_dynamic-update-slice_fusion.3.refs_3_), channel_id=1, source_target_pairs={{0,24},{8,0},{16,8},{24,16},{32,56},{40,32},{48,40},{56,48},{64,88... | collective-permute-start | bytes 3145736 | tf_op jit(solution)/shard_map/ppermute | solution.py:382
  54.2 20.1 %collective-permute-start.21 = (bf16[136,1024]{1,0:T(8,128)(2,1)S(1)}, bf16[136,1024]{1,0:T(8,128)(2,1)S(1)}, u32[]{:S(2)}, u32[]{:S(2)}) collective-permute-start(bf16[136,1024]{1,0:T(8,128)(2,1)S(1)} %get-tuple-element.46), channel_id=1, source_target_pairs={{0,32},{8,40},{16,48},{24,56},{32,0},{40,8},{48,16},{56,24},{64,96... | collective-permute-start | bytes 835592 | tf_op jit(solution)/shard_map/ppermute | solution.py:386
  87.4 23.1 %collective-permute-start.22 = (bf16[2048,256]{1,0:T(8,128)(2,1)}, bf16[2048,256]{1,0:T(8,128)(2,1)S(1)}, u32[]{:S(2)}, u32[]{:S(2)}) collective-permute-start(bf16[2048,256]{1,0:T(8,128)(2,1)} %collective-permute-done.1.refs_0_), channel_id=1, source_target_pairs={{0,32},{8,40},{16,48},{24,56},{32,64},{40,72},{48,80},{56,88},{64,... | collective-permute-start | bytes 3145736 | tf_op jit(solution)/shard_map/ppermute | solution.py:382
  87.4 23.1 %collective-permute-start.24 = (bf16[2048,256]{1,0:T(8,128)(2,1)}, bf16[2048,256]{1,0:T(8,128)(2,1)S(1)}, u32[]{:S(2)}, u32[]{:S(2)}) collective-permute-start(bf16[2048,256]{1,0:T(8,128)(2,1)} %collective-permute-done.9.refs_4_), channel_id=1, source_target_pairs={{0,8},{8,16},{16,24},{24,0},{32,40},{40,48},{48,56},{56,32},{64,72... | collective-permute-start | bytes 3145736 | tf_op jit(solution)/shard_map/ppermute | solution.py:382
  88.1 22.4 %collective-permute-start.23 = (bf16[2048,256]{1,0:T(8,128)(2,1)}, bf16[2048,256]{1,0:T(8,128)(2,1)S(1)}, u32[]{:S(2)}, u32[]{:S(2)}) collective-permute-start(bf16[2048,256]{1,0:T(8,128)(2,1)} %collective-permute-done.7.refs_3_), channel_id=1, source_target_pairs={{0,96},{8,104},{16,112},{24,120},{32,0},{40,8},{48,16},{56,24},{64... | collective-permute-start | bytes 3145736 | tf_op jit(solution)/shard_map/ppermute | solution.py:382
  91.3 19.2 %collective-permute-start.25 = (bf16[2048,256]{1,0:T(8,128)(2,1)}, bf16[2048,256]{1,0:T(8,128)(2,1)}, u32[]{:S(2)}, u32[]{:S(2)}) collective-permute-start(bf16[2048,256]{1,0:T(8,128)(2,1)} %collective-permute-done.15.refs_7_), channel_id=1, source_target_pairs={{0,24},{8,0},{16,8},{24,16},{32,56},{40,32},{48,40},{56,48},{64,88... | collective-permute-start | bytes 3145736 | tf_op jit(solution)/shard_map/ppermute | solution.py:382
  119.2 111.5 %reduce-scatter.3.cloned.1.call-start = ((), (), s32[]{:S(2)}) async-start(), calls=%async_computation.2 | async-start | bytes 7077888 | tf_op jit(solution)/shard_map/reduce_scatter | solution.py:503
  120.4 18.7 %collective-permute-start.6 = (bf16[2048,256]{1,0:T(8,128)(2,1)S(1)}, bf16[2048,256]{1,0:T(8,128)(2,1)S(1)}, u32[]{:S(2)}, u32[]{:S(2)}) collective-permute-start(bf16[2048,256]{1,0:T(8,128)(2,1)S(1)} %copy-done.4), channel_id=1, source_target_pairs={{0,96},{8,104},{16,112},{24,120},{32,0},{40,8},{48,16},{56,24},{64... | collective-permute-start | bytes 3145736 | tf_op jit(solution)/shard_map/ppermute | solution.py:382
  121.0 18.8 %collective-permute-start.14 = (bf16[2048,256]{1,0:T(8,128)(2,1)S(1)}, bf16[2048,256]{1,0:T(8,128)(2,1)}, u32[]{:S(2)}, u32[]{:S(2)}) collective-permute-start(bf16[2048,256]{1,0:T(8,128)(2,1)S(1)} %copy-done.6), channel_id=1, source_target_pairs={{0,24},{8,0},{16,8},{24,16},{32,56},{40,32},{48,40},{56,48},{64,88... | collective-permute-start | bytes 3145736 | tf_op jit(solution)/shard_map/ppermute | solution.py:382
  124.0 19.6 %collective-permute-start.5 = (bf16[2048,256]{1,0:T(8,128)(2,1)}, bf16[2048,256]{1,0:T(8,128)(2,1)}, u32[]{:S(2)}, u32[]{:S(2)}) collective-permute-start(bf16[2048,256]{1,0:T(8,128)(2,1)} %copy-done.9), channel_id=1, source_target_pairs={{0,32},{8,40},{16,48},{24,56},{32,64},{40,72},{48,80},{56,88},{64,... | collective-permute-start | bytes 3145736 | tf_op jit(solution)/shard_map/ppermute | solution.py:382
  125.4 19.2 %collective-permute-start.13 = (bf16[2048,256]{1,0:T(8,128)(2,1)}, bf16[2048,256]{1,0:T(8,128)(2,1)}, u32[]{:S(2)}, u32[]{:S(2)}) collective-permute-start(bf16[2048,256]{1,0:T(8,128)(2,1)} %copy-done.8), channel_id=1, source_target_pairs={{0,8},{8,16},{16,24},{24,0},{32,40},{40,48},{48,56},{56,32},{64,72... | collective-permute-start | bytes 3145736 | tf_op jit(solution)/shard_map/ppermute | solution.py:382
  169.5 18.2 %collective-permute-start.28 = (bf16[136,1024]{1,0:T(8,128)(2,1)}, bf16[136,1024]{1,0:T(8,128)(2,1)S(1)}, u32[]{:S(2)}, u32[]{:S(2)}) collective-permute-start(bf16[136,1024]{1,0:T(8,128)(2,1)} %head.1), channel_id=1, source_target_pairs={{0,8},{8,0},{16,24},{24,16},{32,40},{40,32},{48,56},{56,48},{64,72... | collective-permute-start | bytes 835592 | tf_op jit(solution)/shard_map/ppermute | solution.py:386
  169.6 18.1 %collective-permute-start.26 = (bf16[136,1024]{1,0:T(8,128)(2,1)}, bf16[136,1024]{1,0:T(8,128)(2,1)S(1)}, u32[]{:S(2)}, u32[]{:S(2)}) collective-permute-start(bf16[136,1024]{1,0:T(8,128)(2,1)} %head.1), channel_id=1, source_target_pairs={{0,24},{8,16},{16,8},{24,0},{32,56},{40,48},{48,40},{56,32},{64,88... | collective-permute-start | bytes 835592 | tf_op jit(solution)/shard_map/ppermute | solution.py:386
  169.7 18.0 %collective-permute-start.27 = (bf16[136,1024]{1,0:T(8,128)(2,1)}, bf16[136,1024]{1,0:T(8,128)(2,1)S(1)}, u32[]{:S(2)}, u32[]{:S(2)}) collective-permute-start(bf16[136,1024]{1,0:T(8,128)(2,1)} %head.1), channel_id=1, source_target_pairs={{0,16},{8,24},{16,0},{24,8},{32,48},{40,56},{48,32},{56,40},{64,80... | collective-permute-start | bytes 835592 | tf_op jit(solution)/shard_map/ppermute | solution.py:386
  (37 other events, 467.2 us)
Sparse Core Ops, SparseCore 0:
  119.4 31.0 reduce-scatter.4
  160.8 38.9 reduce-scatter.2

commit v4 on v3

--- a/solution.py
+++ b/solution.py
@@ -34,8 +34,7 @@
 
 def inverse_matrix(start):
     th = angles(np.arange(start, start + BLK, dtype=np.float64)).T
-    hi, lo = split_hi_lo(np.concatenate([np.cos(th), -np.sin(th)], 1) / BLK)
-    return np.concatenate([hi, lo], 1)
+    return (np.concatenate([np.cos(th), -np.sin(th)], 1) / BLK).astype(np.float32).astype(bf16)
 
 
 def spectrum(fwd, rows):
@@ -53,27 +52,8 @@
     return jnp.concatenate([ar * br + ai * bi, ai * br - ar * bi], 0)
 
 
-def two_parts(y):
-    hi = y.astype(bf16)
-    return hi, (y - hi.astype(f32)).astype(bf16)
-
-
-def from_parts(inv, parts):
-    matrix = jnp.concatenate([inv[...], inv[:, : 2 * BLK]], 1)
-    return jnp.dot(matrix, parts, preferred_element_type=f32)
-
-
-def invert(inv, y):
-    hi, lo = two_parts(y)
-    return from_parts(inv, jnp.concatenate([hi, hi, lo], 0))
-
-
-def put_spectrum(buf, row, lanes, y):
-    hi, lo = two_parts(y)
-    n = y.shape[0]
-    buf[row : row + n, lanes] = hi
-    buf[2 * BLK + row : 2 * BLK + row + n, lanes] = hi
-    buf[4 * BLK + row : 4 * BLK + row + n, lanes] = lo
+def invert(inv, spec):
+    return jnp.dot(inv[...], spec, preferred_element_type=f32)
 
 
 def chunks(total, size):
@@ -130,9 +110,9 @@
             wr, wi = window_rows(spec, c, lanes, slice((b + 1) * wide, (b + 2) * wide))
             mspec[b, c : c + FREQS] = wr
             mspec[b, BLK + c : BLK + c + FREQS] = wi
-            put_spectrum(ybuf, c, lanes, fr * wr - fi * wi)
-            put_spectrum(ybuf, BLK + c, lanes, fr * wi + fi * wr)
-    out[...] = from_parts(inv, ybuf[...])
+            ybuf[c : c + FREQS, lanes] = (fr * wr - fi * wi).astype(bf16)
+            ybuf[BLK + c : BLK + c + FREQS, lanes] = (fr * wi + fi * wr).astype(bf16)
+    out[...] = invert(inv, ybuf[...])
     for r, n in chunks(rows, ROWS):
         at, lane = r % BLK, r // BLK * wide
         mixin = mix[at : at + n, lane + wide : lane + 2 * wide].astype(f32)
@@ -159,7 +139,6 @@
         for h in range(2):
             gbuf[h * BLK + at : h * BLK + at + n, lane : lane + wide] = g
     spec[...] = jnp.dot(fwd[...], gbuf[...], preferred_element_type=f32)
-    whole = slice(0, wide)
     for c in range(0, BLK, FREQS):
         sr, si = slice(c, c + FREQS), slice(BLK + c, BLK + c + FREQS)
         fr, fi = fspec[sr], fspec[si]
@@ -171,16 +150,16 @@
             pr, pi = gr * mr + gi * mi, gi * mr - gr * mi
             lag_r, lag_i = (pr, pi) if b == 0 else (lag_r + pr, lag_i + pi)
             wr, wi = window_rows(spec, c, lanes, after)
-            put_spectrum(ybuf, c, lanes, wr * fr + wi * fi)
-            put_spectrum(ybuf, BLK + c, lanes, wi * fr - wr * fi)
-        put_spectrum(lagy, c, whole, lag_r)
-        put_spectrum(lagy, BLK + c, whole, lag_i)
-    lagbuf[...] = from_parts(invlag, lagy[...])
+            ybuf[sr, lanes] = (wr * fr + wi * fi).astype(bf16)
+            ybuf[si, lanes] = (wi * fr - wr * fi).astype(bf16)
+        lagy[sr] = lag_r.astype(bf16)
+        lagy[si] = lag_i.astype(bf16)
+    lagbuf[...] = invert(invlag, lagy[...])
     quarter = BLK // SIDE
     for k, part in enumerate((long0, long1, long2, long3)):
         start = pl.multiple_of((place[0] ^ k) * quarter, quarter)
         part[...] = lagbuf[pl.ds(start, quarter)].astype(bf16)
-    out[...] = from_parts(inv, ybuf[...])
+    out[...] = invert(inv, ybuf[...])
     for r, n in chunks(rows, ROWS):
         at, lane = r % BLK, r // BLK * wide
         g = gbuf[at : at + n, lane : lane + wide].astype(f32)
@@ -244,17 +223,18 @@
     rows = bg.shape[0]
     late = delay(spectrum(fwd[...], halo[:BLK]))
     gfull[: rows - BLK] = gmix[: rows - BLK]
-    gfull[rows - BLK :] = gmix[rows - BLK :] + invert(inv, product_conj(late, fspec[...]))
+    gfull[rows - BLK :] = gmix[rows - BLK :] + invert(inv, product_conj(late, fspec[...]).astype(bf16))
     edge = halo[BLK : BLK + PAD].astype(f32)
     zeros = jnp.zeros((PAD - 2, edge.shape[1]), f32)
     extra = [jnp.concatenate([edge[2 * m : 2 * m + 2], zeros], 0) for m in range(3)]
     short[...] = short_in[...] + finish_body(bg, conv, gfull, act, proj, sf, extra, gp, ext)
 
 
-def pieces_kernel(steps, back, more, *refs):
-    weights, refs = refs[: 2 * steps], refs[2 * steps :]
+def pieces_kernel(steps, per, back, more, *refs):
+    count = steps * per // 2
+    weights, refs = refs[:count], refs[count:]
     if back:
-        gated, og, refs = refs[0], refs[1 : 1 + SIDE], refs[1 + SIDE :]
+        gated, og, refs = refs[0], refs[1 : 1 + per], refs[1 + per :]
         if more:
             acc_in, refs = refs[0], refs[2:]
         result, acc, buf, sems = refs
@@ -262,16 +242,16 @@
         gated, result, buf, sems = refs
     step = pl.program_id(0)
     chans = gated.shape[1]
-    width = buf.shape[2] // SIDE
+    width = buf.shape[2] // per
 
     def copies(i):
         return [
             pltpu.make_async_copy(
-                weights[2 * i + j // 2].at[pl.ds((j % 2) * chans, chans)],
+                weights[(per * i + j) // 2].at[pl.ds((per * i + j) % 2 * chans, chans)],
                 buf.at[i % 2, :, pl.ds(j * width, width)],
                 sems.at[i % 2, j],
             )
-            for j in range(SIDE)
+            for j in range(per)
         ]
 
     @pl.when(step == 0)
@@ -302,10 +282,10 @@
         )
 
 
-def multiply_pieces(weights, cols, gated, out_grad=None, total=None, before=None):
+def multiply_pieces(weights, table, gated, out_grad=None, total=None, before=None, per=SIDE):
     rows, chans = gated.shape
     width = weights[0].shape[1]
-    steps = len(weights) // 2
+    steps = 2 * len(weights) // per
     back, more = out_grad is not None, before is not None
     total = total or steps
     offset = before[0] if more else 0
@@ -315,19 +295,19 @@
     aliases = {}
     if back:
         in_specs += [
-            pl.BlockSpec((rows, width), lambda i, c, j=j: (0, c[SIDE * i + j])) for j in range(SIDE)
+            pl.BlockSpec((rows, width), lambda i, c, j=j: (0, c[1 + per * (i + offset) + j])) for j in range(per)
         ]
-        operands += [out_grad] * SIDE
+        operands += [out_grad] * per
         if more:
             in_specs += [whole, pl.BlockSpec(memory_space=pl.ANY)]
             operands += [before[2], before[1]]
             aliases = {len(operands): 0}
-    result_shape = jax.ShapeDtypeStruct((rows, total * SIDE * width), bf16)
-    result_spec = pl.BlockSpec((rows, SIDE * width), lambda i, c: (0, i + offset))
+    result_shape = jax.ShapeDtypeStruct((rows, total * per * width), bf16)
+    result_spec = pl.BlockSpec((rows, per * width), lambda i, c: (0, i + offset))
 
     def kernel(cols_ref, *refs):
         del cols_ref
-        pieces_kernel(steps, back, more, *refs)
+        pieces_kernel(steps, per, back, more, *refs)
 
     return pl.pallas_call(
         kernel,
@@ -337,19 +317,19 @@
             in_specs=in_specs,
             out_specs=[result_spec] + [whole] * back,
             scratch_shapes=[
-                pltpu.VMEM((2, chans, SIDE * width), bf16),
-                pltpu.SemaphoreType.DMA((2, SIDE)),
+                pltpu.VMEM((2, chans, per * width), bf16),
+                pltpu.SemaphoreType.DMA((2, per)),
             ],
         ),
         out_shape=[result_shape] + [jax.ShapeDtypeStruct((rows, chans), f32)] * back,
         input_output_aliases=aliases,
         cost_estimate=pl.CostEstimate(
-            flops=(2 + 2 * back) * rows * chans * width * SIDE * steps,
-            bytes_accessed=SIDE * steps * (2 * chans * width + 4 * rows * width) + 6 * rows * chans,
+            flops=(2 + 2 * back) * rows * chans * width * per * steps,
+            bytes_accessed=per * steps * (2 * chans * width + 4 * rows * width) + 6 * rows * chans,
             transcendentals=0,
         ),
         name="pieces",
-    )(cols, *operands)
+    )(table, *operands)
 
 
 def collect_kernel(counts, cols, *refs):
@@ -361,7 +341,7 @@
         @pl.loop(0, count)
         def _(p, ref=ref, begin=begin):
             lanes = pl.ds(pl.multiple_of(p * width, width), width)
-            start = pl.multiple_of(cols[begin + p] * width, width)
+            start = pl.multiple_of(cols[1 + begin + p] * width, width)
             mixed[:, pl.ds(start, width)] = ref[:, lanes]
 
         begin += count
@@ -397,17 +377,15 @@
         return [one, two], [op, tp_, oq, tq], [far_one, far_two]
 
     def blocks(half, near, far_steps):
-        out = []
-        for f in far_steps:
-            for n in near:
-                z, x = (f, n) if half == 0 else (n, f)
-                out.append(2 * ((zi + z) % SIDE * SIDE + (xi + x) % SIDE) + half)
-        return out
+        steps = [(f, n) if half == 0 else (n, f) for f in far_steps for n in near]
+        return [(half, z, x) for z, x in steps]
 
     order4 = (0, -1, 1, 2)
-    cols1 = jnp.stack(blocks(0, order4, (0,)) + blocks(1, order4, (0,)))
-    cols2 = jnp.stack(blocks(0, order4, (-1, 1)) + blocks(1, order4, (-1, 1)))
-    cols3 = jnp.stack(blocks(0, order4, (2,)) + blocks(1, order4, (2,)))
+    halves, dz, dx = np.array(
+        [b for far in ((0,), (-1, 1), (2,)) for half in (0, 1) for b in blocks(half, order4, far)]
+    ).T
+    table = 2 * ((zi + dz) % SIDE * SIDE + (xi + dx) % SIDE) + halves
+    table = jnp.concatenate([jnp.reshape(zi, (1,)), table]).astype(jnp.int32)
 
     positions = jnp.arange(ctx_count, dtype=jnp.int32)
     matches = left_source[None, :] == positions[:, None]
@@ -468,7 +446,7 @@
         return pl.BlockSpec((*lead, tile), lambda i, *_: (*([0] * len(lead)), i))
 
     const = pl.BlockSpec((2 * BLK, 2 * BLK), lambda i, *_: (0, 0))
-    const_inv = pl.BlockSpec((BLK, 4 * BLK), lambda i, *_: (0, 0))
+    const_inv = pl.BlockSpec((BLK, 2 * BLK), lambda i, *_: (0, 0))
     forward = pl.pallas_call(
         forward_kernel,
         grid=grid,
@@ -480,7 +458,7 @@
             pltpu.VMEM((3, rows + PAD, tile), f32),
             pltpu.VMEM((2 * BLK, (nb + 1) * tile), bf16),
             pltpu.VMEM((2 * BLK, (nb + 1) * tile), f32),
-            pltpu.VMEM((6 * BLK, nb * tile), bf16),
+            pltpu.VMEM((2 * BLK, nb * tile), bf16),
             pltpu.VMEM((BLK, nb * tile), f32),
         ],
         out_shape=[
@@ -502,19 +480,18 @@
     def scatter(value):
         return lax.psum_scatter(value, "tp", scatter_dimension=0, tiled=True)
 
-    early = multiply_pieces(near_a + near_b, cols1, gated, out_grad, 6)
+    early = multiply_pieces(near_a + near_b, table, gated, out_grad, 6)
     out1, acc = multiply_pieces(
-        mid_a + mid_b, cols2, gated, out_grad, 6, (2, *early)
+        mid_a + mid_b, table, gated, out_grad, 6, (2, *early)
     )
     out1 = scatter(out1)
 
     quarter = BLK // SIDE
-    place = jnp.concatenate([jnp.reshape(zi, (1,)), cols3]).astype(jnp.int32)
     lasts = [w.reshape(2, chans, width) for w in far_a + far_b]
     last_spec = pl.BlockSpec((2, tile, width), lambda i, c: (0, i, 0))
 
     def out_grad_rows(n):
-        return [pl.BlockSpec((n, width), lambda i, c, j=j: (0, c[1 + j])) for j in range(2 * SIDE)]
+        return [pl.BlockSpec((n, width), lambda i, c, j=j: (0, c[1 + 6 * SIDE + j])) for j in range(2 * SIDE)]
 
     def first_rows(n, *lead):
         zeros = [0] * len(lead)
@@ -547,7 +524,7 @@
         ),
         name="head",
     )
-    pay = head(place, acc, act, act, conv, long_filter, skip_row, *[out_grad] * (2 * SIDE), *lasts)
+    pay = head(table, acc, act, act, conv, long_filter, skip_row, *[out_grad] * (2 * SIDE), *lasts)
     got = along_x([pay] * SIDE)
 
     long_shape = jax.ShapeDtypeStruct((quarter, chans), bf16)
@@ -573,8 +550,8 @@
                 pltpu.VMEM((BLK, tile), f32),
                 pltpu.VMEM((2 * BLK, nb * tile), bf16),
                 pltpu.VMEM((2 * BLK, nb * tile), f32),
-                pltpu.VMEM((6 * BLK, nb * tile), bf16),
-                pltpu.VMEM((6 * BLK, tile), bf16),
+                pltpu.VMEM((2 * BLK, nb * tile), bf16),
+                pltpu.VMEM((2 * BLK, tile), bf16),
                 pltpu.VMEM((BLK, nb * tile), f32),
             ],
         ),
@@ -587,7 +564,7 @@
         name="backward",
     )
     bg, *longs, gmix = backward(
-        place, acc, act, mspec, fspec, skip_row, fwd, inv_now, inv_lag,
+        table, acc, act, mspec, fspec, skip_row, fwd, inv_now, inv_lag,
         *[out_grad] * (2 * SIDE), *lasts,
     )
 
@@ -597,7 +574,7 @@
     sums = [g[BLK + PAD :].astype(f32) for g in got]
     my_quarter = (sums[0] + sums[1]) + (sums[2] + sums[3])
 
-    (out3,) = multiply_pieces(far_a + far_b, cols3, gated)
+    (out3,) = multiply_pieces(far_a + far_b, table, gated, per=2)
     out3 = scatter(out3)
 
     low = rows - BLK - PAD
@@ -675,7 +652,7 @@
         cost_estimate=pl.CostEstimate(flops=10_000_000, bytes_accessed=5 << 20, transcendentals=0),
         name="collect",
     )
-    mixed = collect(jnp.concatenate([cols1, cols2, cols3]), out1, out3)
+    mixed = collect(table, out1, out3)
 
     scale = 1.0 / math.sqrt(rows * ctx_count)
     return mixed, gp, long_total.astype(f32) * scale, short_total * scale

time: 242 us -> 253 us (1.045)
  waiting for transfers between devices: 54.6 us -> 74.5 us
  starting transfers between devices: 61.3 us -> 54.5 us
    ppermute x20, waiting for transfers between devices: 16.4 us -> 30.2 us  [ring(): return lax.ppermute(value, 'ctx', pairs)]
    ppermute x18, waiting for transfers between devices: 38.1 us -> 44.2 us  [swap(): lax.ppermute(value, 'ctx', [(d, d ^ shift) for d in range(ctx_count)])]
    ppermute x20, starting transfers between devices: 35.9 us -> 31.7 us  [ring(): return lax.ppermute(value, 'ctx', pairs)]
    ppermute x18, starting transfers between devices: 25.4 us -> 22.5 us  [swap(): lax.ppermute(value, 'ctx', [(d, d ^ shift) for d in range(ctx_count)])]
  transfers between devices with their start and end apart: 40 -> 40, of which waited for: 16 -> 17; matrix products, arithmetic and copies ran while one was open for 8% -> 7% of each run, Pallas kernels for 29% -> 27%
where the time goes in v4:
time: 253 us; the launch traced here: 252 us
  Pallas kernels  78.7 us (31%)
  waiting for transfers between devices  74.5 us (29%)
  starting transfers between devices  54.5 us (22%)
  between operations  22 us (9%)
  other arithmetic  12.6 us (5%)
  local copies, waits for them, and re-layouts  9.65 us (4%)
    ppermute x18, waiting for transfers between devices, swap(): lax.ppermute(value, 'ctx', [(d, d ^ shift) for d in range(ctx_count)])  44.2 us
    pallas_call x3, Pallas kernels, multiply_pieces(): pl.pallas_call(kernel, grid_spec=pltpu.PrefetchScalarGridSpec(num_scalar_...  33.8 us
    ppermute x20, starting transfers between devices, ring(): return lax.ppermute(value, 'ctx', pairs)  31.7 us
    ppermute x20, waiting for transfers between devices, ring(): return lax.ppermute(value, 'ctx', pairs)  30.2 us
    ppermute x18, starting transfers between devices, swap(): lax.ppermute(value, 'ctx', [(d, d ^ shift) for d in range(ctx_count)])  22.5 us
    pallas_call x1, Pallas kernels, on_device(): backward(table, acc, act, mspec, fspec, skip_row, fwd, inv_now, inv_lag,...  12.5 us
    pallas_call x1, Pallas kernels, on_device(): forward(projected, left, short_filter, long_filter, skip_row, fwd, inv_late)  8.94 us
    pallas_call x1, Pallas kernels, on_device(): top(bg, conv, gmix, act, bg, conv, gmix, act, projected, short_filter)  7.77 us
  transfers between devices with their start and end apart: 40, of which 17 were waited for; matrix products, arithmetic and copies ran while one was open for 7% of the time, Pallas kernels for 27%

profile of v4, /device:TPU:24, one launch (start us, length us, event | category | flops | bytes accessed | tf_op | source)
XLA Modules:
  0.0 252.0 jit_solution(1611759987147063277)
XLA Ops:
  9.3 4.0 %collective-permute-start.10 = (bf16[1024,256]{1,0:T(8,128)(2,1)S(1)}, bf16[1024,256]{1,0:T(8,128)(2,1)S(1)}, u32[]{:S(2)}, u32[]{:S(2)}) collective-permute-start(bf16[1024,256]{1,0:T(8,128)(2,1)S(1)} %get-tuple-element.48), channel_id=1, source_target_pairs={{0,96},{8,104},{16,112},{24,120},{32,0},{40,8},{48,16},{56,24},{64... | collective-permute-start | bytes 1572872 | tf_op jit(solution)/shard_map/ppermute | solution.py:362
  23.6 4.3 %collective-permute-done.8 = bf16[1024,256]{1,0:T(8,128)(2,1)S(1)} collective-permute-done((bf16[1024,256]{1,0:T(8,128)(2,1)S(1)}, bf16[1024,256]{1,0:T(8,128)(2,1)S(1)}, u32[]{:S(2)}, u32[]{:S(2)}) %collective-permute-start.8) | collective-permute-done | bytes 524320 | tf_op jit(solution)/shard_map/ppermute | solution.py:362
  31.6 11.9 %collective-permute-done = bf16[1024,256]{1,0:T(8,128)(2,1)} collective-permute-done((bf16[1024,256]{1,0:T(8,128)(2,1)}, bf16[1024,256]{1,0:T(8,128)(2,1)}, u32[]{:S(2)}, u32[]{:S(2)}) %collective-permute-start) | collective-permute-done | bytes 524320 | tf_op jit(solution)/shard_map/ppermute | solution.py:362
  43.6 3.0 %collective-permute-start.12 = (bf16[512,256]{1,0:T(8,128)(2,1)S(1)}, bf16[512,256]{1,0:T(8,128)(2,1)S(1)}, u32[]{:S(2)}, u32[]{:S(2)}) collective-permute-start(bf16[512,256]{1,0:T(8,128)(2,1)S(1)} %slice.111), channel_id=1, source_target_pairs={{0,96},{8,104},{16,112},{24,120},{32,0},{40,8},{48,16},{56,24},{64... | collective-permute-start | bytes 786440 | tf_op jit(solution)/shard_map/ppermute | solution.py:362
  50.0 3.3 %collective-permute-start.4 = (bf16[512,256]{1,0:T(8,128)(2,1)S(1)}, bf16[512,256]{1,0:T(8,128)(2,1)S(1)}, u32[]{:S(2)}, u32[]{:S(2)}) collective-permute-start(bf16[512,256]{1,0:T(8,128)(2,1)S(1)} %slice.109), channel_id=1, source_target_pairs={{0,24},{8,0},{16,8},{24,16},{32,56},{40,32},{48,40},{56,48},{64,88... | collective-permute-start | bytes 786440 | tf_op jit(solution)/shard_map/ppermute | solution.py:362
  53.5 3.2 %collective-permute-done.3 = bf16[512,256]{1,0:T(8,128)(2,1)S(1)} collective-permute-done((bf16[512,256]{1,0:T(8,128)(2,1)S(1)}, bf16[512,256]{1,0:T(8,128)(2,1)S(1)}, u32[]{:S(2)}, u32[]{:S(2)}) %collective-permute-start.3) | collective-permute-done | bytes 262176 | tf_op jit(solution)/shard_map/ppermute | solution.py:362
  61.6 3.2 %collective-permute-start.7 = (bf16[2048,256]{1,0:T(8,128)(2,1)}, bf16[2048,256]{1,0:T(8,128)(2,1)}, u32[]{:S(2)}, u32[]{:S(2)}) collective-permute-start(bf16[2048,256]{1,0:T(8,128)(2,1)} %constant_dynamic-update-slice_fusion.refs_1_), channel_id=1, source_target_pairs={{0,96},{8,104},{16,112},{24,120},{32,0},{40,8},{48,16},{56,24},{64... | collective-permute-start | bytes 3145736 | tf_op jit(solution)/shard_map/ppermute | solution.py:362
  67.4 25.4 %collective-permute-done.19 = bf16[136,1024]{1,0:T(8,128)(2,1)} collective-permute-done((bf16[136,1024]{1,0:T(8,128)(2,1)S(1)}, bf16[136,1024]{1,0:T(8,128)(2,1)}, u32[]{:S(2)}, u32[]{:S(2)}) %collective-permute-start.19) | collective-permute-done | bytes 278560 | tf_op jit(solution)/shard_map/ppermute | solution.py:366
  92.8 10.8 %collective-permute-done.20 = bf16[136,1024]{1,0:T(8,128)(2,1)} collective-permute-done((bf16[136,1024]{1,0:T(8,128)(2,1)S(1)}, bf16[136,1024]{1,0:T(8,128)(2,1)}, u32[]{:S(2)}, u32[]{:S(2)}) %collective-permute-start.20) | collective-permute-done | bytes 278560 | tf_op jit(solution)/shard_map/ppermute | solution.py:366
  105.8 3.1 %collective-permute-start.25 = (bf16[2048,256]{1,0:T(8,128)(2,1)}, bf16[2048,256]{1,0:T(8,128)(2,1)S(1)}, u32[]{:S(2)}, u32[]{:S(2)}) collective-permute-start(bf16[2048,256]{1,0:T(8,128)(2,1)} %collective-permute-done.15.refs_7_), channel_id=1, source_target_pairs={{0,24},{8,0},{16,8},{24,16},{32,56},{40,32},{48,40},{56,48},{64,88... | collective-permute-start | bytes 3145736 | tf_op jit(solution)/shard_map/ppermute | solution.py:362
  116.2 8.9 %forward.1 = (bf16[512,1024]{1,0:T(8,128)(2,1)}, f32[512,1024]{1,0:T(8,128)}, f32[3,512,1024]{2,1,0:T(8,128)}, f32[4,256,1024]{2,1,0:T(8,128)}, f32[256,1024]{1,0:T(8,128)}) custom-call(bf16[3,512,1024]{2,1,0:T(8,128)(2,1)} %proj.5, bf16[136,1024]{1,0:T(8,128)(2,1)} %select_select_fusion.3.halo, f32[3,3,1024]{2,1,0:T(4,128)} %sf.5, bf16[128,1024]{1,0:T(8,128)(2,1)} %lf.3, ...), custom_call_target="tpu_custom_call" | custom-call | flops 8000000000 | bytes 20971520 | tf_op jit(solution)/shard_map/forward/pallas_call | solution.py:476
  127.5 7.6 %pieces.5 = bf16[512,2048]{1,0:T(8,128)(2,1)} custom-call(s32[33]{0:T(128)} %pad_add_fusion.cols_ref.cols.place, bf16[2048,256]{1,0:T(8,128)(2,1)} %copy-done.1, bf16[2048,256]{1,0:T(8,128)(2,1)} %collective-permute-done.23.refs_1_, bf16[2048,256]{1,0:T(8,128)(2,1)} %copy-done, bf16[2048,256]{1,0:T(8,128)(2,1)} %copy-done.2, ...), custom_call_target="tpu_custom_call" | custom-call | flops 2147483648 | bytes 11534336 | tf_op jit(solution)/shard_map/pieces/pallas_call | solution.py:312
  136.7 3.6 %collective-permute-start.6 = (bf16[2048,256]{1,0:T(8,128)(2,1)S(1)}, bf16[2048,256]{1,0:T(8,128)(2,1)}, u32[]{:S(2)}, u32[]{:S(2)}) collective-permute-start(bf16[2048,256]{1,0:T(8,128)(2,1)S(1)} %copy-done.6), channel_id=1, source_target_pairs={{0,96},{8,104},{16,112},{24,120},{32,0},{40,8},{48,16},{56,24},{64... | collective-permute-start | bytes 3145736 | tf_op jit(solution)/shard_map/ppermute | solution.py:362
  142.1 10.2 %pieces.3 = (bf16[512,6144]{1,0:T(8,128)(2,1)}, f32[512,1024]{1,0:T(8,128)}) custom-call(s32[33]{0:T(128)} %pad_add_fusion.cols_ref.cols.place, bf16[2048,256]{1,0:T(8,128)(2,1)} %copy-done.5, bf16[2048,256]{1,0:T(8,128)(2,1)} %constant_dynamic-update-slice_fusion.refs_1_, bf16[2048,256]{1,0:T(8,128)(2,1)} %copy-done.3, bf16[2048,256]{1,0:T(8,128)(2,1)} %copy-done.8, ...), custom_call_target="tpu_custom_call" | custom-call | flops 4294967296 | bytes 11534336 | tf_op jit(solution)/shard_map/pieces/pallas_call | solution.py:312
  154.9 3.7 %collective-permute-done.13.refs_5_ = bf16[2048,256]{1,0:T(8,128)(2,1)} collective-permute-done((bf16[2048,256]{1,0:T(8,128)(2,1)}, bf16[2048,256]{1,0:T(8,128)(2,1)}, u32[]{:S(2)}, u32[]{:S(2)}) %collective-permute-start.13) | collective-permute-done | bytes 1048608 | tf_op jit(solution)/shard_map/ppermute | solution.py:362
  159.7 16.0 %pieces.4 = (bf16[512,6144]{1,0:T(8,128)(2,1)}, f32[512,1024]{1,0:T(8,128)}) custom-call(s32[33]{0:T(128)} %pad_add_fusion.cols_ref.cols.place, bf16[2048,256]{1,0:T(8,128)(2,1)} %collective-permute-done.1.refs_0_, bf16[2048,256]{1,0:T(8,128)(2,1)} %collective-permute-done.5.refs_1_, ...), custom_call_target="tpu_custom_call", output_to_operand_aliasing={{0}: (15, {})} | custom-call | flops 8589934592 | bytes 19922944 | tf_op jit(solution)/shard_map/pieces/pallas_call | solution.py:312
  177.7 6.7 %head.1 = bf16[136,1024]{1,0:T(8,128)(2,1)} custom-call(s32[33]{0:T(128)} %pad_add_fusion.cols_ref.cols.place, f32[512,1024]{1,0:T(8,128)} %get-tuple-element.27.acc, f32[3,512,1024]{2,1,0:T(8,128)} %get-tuple-element.28.act0.act12.act.actn, f32[3,512,1024]{2,1,0:T(8,128)} %get-tuple-element.28.act0.act12.act.actn, ...), custom_call_target="tpu_custom_call" | custom-call | flops 600000000 | bytes 6291456 | tf_op jit(solution)/shard_map/head/pallas_call | solution.py:527
  188.6 12.5 %backward.1 = (f32[512,1024]{1,0:T(8,128)}, bf16[32,1024]{1,0:T(8,128)(2,1)}, bf16[32,1024]{1,0:T(8,128)(2,1)}, bf16[32,1024]{1,0:T(8,128)(2,1)}, bf16[32,1024]{1,0:T(8,128)(2,1)}, /*index=5*/f32[512,1024]{1,0:T(8,128)}) custom-call(s32[33]{0:T(128)} %pad_add_fusion.cols_ref.cols.place, f32[512,1024]{1,0:T(8,128)} %get-tuple-element.27.acc, ...), custom_call_target="tpu_custom_call" | custom-call | flops 8000000000 | bytes 20971520 | tf_op jit(solution)/shard_map/backward/pallas_call | solution.py:566
  203.1 3.4 %collective-permute-start.31 = (bf16[168,1024]{1,0:T(8,128)(2,1)S(1)}, bf16[168,1024]{1,0:T(8,128)(2,1)S(1)}, u32[]{:S(2)}, u32[]{:S(2)}) collective-permute-start(bf16[168,1024]{1,0:T(8,128)(2,1)S(1)} %pad_maximum_fusion.4), channel_id=1, source_target_pairs={{0,32},{8,40},{16,48},{24,56},{32,0},{40,8},{48,16},{56,24},{64,96... | collective-permute-start | bytes 1032200 | tf_op jit(solution)/shard_map/ppermute | solution.py:366
  208.3 7.8 %top.1 = (bf16[3,512,1024]{2,1,0:T(8,128)(2,1)}, f32[16,1024]{1,0:T(8,128)}) custom-call(f32[512,1024]{1,0:T(8,128)} %get-tuple-element.31.bg.bgn, f32[512,1024]{1,0:T(8,128)} %get-tuple-element.32.convh.conv.convn, f32[512,1024]{1,0:T(8,128)} %get-tuple-element.33.gmix.gmixn, f32[3,512,1024]{2,1,0:T(8,128)} %get-tuple-element.28.act0.act12.act.actn, ...), custom_call_target="tpu_custom_call" | custom-call | flops 200000000 | bytes 10485760 | tf_op jit(solution)/shard_map/top/pallas_call | solution.py:610
  216.9 5.9 %bottom.1 = (bf16[3,512,1024]{2,1,0:T(8,128)(2,1)}, f32[16,1024]{1,0:T(8,128)}) custom-call(f32[512,1024]{1,0:T(8,128)} %get-tuple-element.31.bg.bgn, f32[512,1024]{1,0:T(8,128)} %get-tuple-element.32.convh.conv.convn, f32[512,1024]{1,0:T(8,128)} %get-tuple-element.33.gmix.gmixn, ...), custom_call_target="tpu_custom_call", output_to_operand_aliasing={{0}: (11, {})} | custom-call | flops 2000000000 | bytes 5242880 | tf_op jit(solution)/shard_map/bottom/pallas_call | solution.py:629
  223.9 2.8 %collective-permute-start.33 = (bf16[48,1024]{1,0:T(8,128)(2,1)S(1)}, bf16[48,1024]{1,0:T(8,128)(2,1)S(1)}, u32[]{:S(2)}, u32[]{:S(2)}) collective-permute-start(bf16[48,1024]{1,0:T(8,128)(2,1)S(1)} %pad_maximum_fusion.5), channel_id=1, source_target_pairs={{0,16},{8,24},{16,0},{24,8},{32,48},{40,56},{48,32},{56,40},{64,80... | collective-permute-start | bytes 294920 | tf_op jit(solution)/shard_map/ppermute | solution.py:366
  236.8 2.8 %collective-permute-done.35 = bf16[48,1024]{1,0:T(8,128)(2,1)S(1)} collective-permute-done((bf16[48,1024]{1,0:T(8,128)(2,1)S(1)}, bf16[48,1024]{1,0:T(8,128)(2,1)S(1)}, u32[]{:S(2)}, u32[]{:S(2)}) %collective-permute-start.35) | collective-permute-done | bytes 98336 | tf_op jit(solution)/shard_map/ppermute | solution.py:366
  242.0 3.1 %collect.1 = bf16[64,8192]{1,0:T(8,128)(2,1)} custom-call(s32[33]{0:T(128)} %pad_add_fusion.cols_ref.cols.place, bf16[64,6144]{1,0:T(8,128)(2,1)} %reduce-scatter.3.cloned.1.call-done.refs_0_, bf16[64,2048]{1,0:T(8,128)(2,1)} %reduce-scatter.5.cloned.1.call-done.refs_1_), custom_call_target="tpu_custom_call" | custom-call | flops 10000000 | bytes 5242880 | tf_op jit(solution)/shard_map/collect/pallas_call | solution.py:655
  (153 shorter events, 62.5 us)
Async XLA Ops:
  7.2 234.9 %reduce-scatter.5.cloned.1.call-start = ((), (), s32[]{:S(2)}) async-start(), calls=%async_computation.3 | async-start | bytes 2359296 | tf_op jit(solution)/shard_map/reduce_scatter | solution.py:481
  9.3 21.4 %collective-permute-start.10 = (bf16[1024,256]{1,0:T(8,128)(2,1)S(1)}, bf16[1024,256]{1,0:T(8,128)(2,1)S(1)}, u32[]{:S(2)}, u32[]{:S(2)}) collective-permute-start(bf16[1024,256]{1,0:T(8,128)(2,1)S(1)} %get-tuple-element.48), channel_id=1, source_target_pairs={{0,96},{8,104},{16,112},{24,120},{32,0},{40,8},{48,16},{56,24},{64... | collective-permute-start | bytes 1572872 | tf_op jit(solution)/shard_map/ppermute | solution.py:362
  16.7 43.1 %collective-permute-start.16 = (bf16[136,1024]{1,0:T(8,128)(2,1)}, bf16[136,1024]{1,0:T(8,128)(2,1)}, u32[]{:S(2)}, u32[]{:S(2)}) collective-permute-start(bf16[136,1024]{1,0:T(8,128)(2,1)} %maximum_maximum_fusion), channel_id=1, source_target_pairs={{0,24},{8,16},{16,8},{24,0},{32,56},{40,48},{48,40},{56,32},{64,88... | collective-permute-start | bytes 835592 | tf_op jit(solution)/shard_map/ppermute | solution.py:366
  19.5 42.1 %collective-permute-start.17 = (bf16[136,1024]{1,0:T(8,128)(2,1)}, bf16[136,1024]{1,0:T(8,128)(2,1)}, u32[]{:S(2)}, u32[]{:S(2)}) collective-permute-start(bf16[136,1024]{1,0:T(8,128)(2,1)} %maximum_maximum_fusion), channel_id=1, source_target_pairs={{0,16},{8,24},{16,0},{24,8},{32,48},{40,56},{48,32},{56,40},{64,80... | collective-permute-start | bytes 835592 | tf_op jit(solution)/shard_map/ppermute | solution.py:366
  20.3 23.3 %collective-permute-start = (bf16[1024,256]{1,0:T(8,128)(2,1)}, bf16[1024,256]{1,0:T(8,128)(2,1)}, u32[]{:S(2)}, u32[]{:S(2)}) collective-permute-start(bf16[1024,256]{1,0:T(8,128)(2,1)} %get-tuple-element.49), channel_id=1, source_target_pairs={{0,8},{8,16},{16,24},{24,0},{32,40},{40,48},{48,56},{56,32},{64,72... | collective-permute-start | bytes 1572872 | tf_op jit(solution)/shard_map/ppermute | solution.py:362
  27.9 21.1 %collective-permute-start.2 = (bf16[1024,256]{1,0:T(8,128)(2,1)}, bf16[1024,256]{1,0:T(8,128)(2,1)S(1)}, u32[]{:S(2)}, u32[]{:S(2)}) collective-permute-start(bf16[1024,256]{1,0:T(8,128)(2,1)} %get-tuple-element.49), channel_id=1, source_target_pairs={{0,24},{8,0},{16,8},{24,16},{32,56},{40,32},{48,40},{56,48},{64,88... | collective-permute-start | bytes 1572872 | tf_op jit(solution)/shard_map/ppermute | solution.py:362
  30.7 19.3 %collective-permute-start.11 = (bf16[512,256]{1,0:T(8,128)(2,1)S(1)}, bf16[512,256]{1,0:T(8,128)(2,1)S(1)}, u32[]{:S(2)}, u32[]{:S(2)}) collective-permute-start(bf16[512,256]{1,0:T(8,128)(2,1)S(1)} %slice.110), channel_id=1, source_target_pairs={{0,32},{8,40},{16,48},{24,56},{32,64},{40,72},{48,80},{56,88},{64,... | collective-permute-start | bytes 786440 | tf_op jit(solution)/shard_map/ppermute | solution.py:362
  56.7 48.4 %collective-permute-start.9 = (bf16[2048,256]{1,0:T(8,128)(2,1)S(1)}, bf16[2048,256]{1,0:T(8,128)(2,1)}, u32[]{:S(2)}, u32[]{:S(2)}) collective-permute-start(bf16[2048,256]{1,0:T(8,128)(2,1)S(1)} %pad_maximum_fusion.1.refs_2_), channel_id=1, source_target_pairs={{0,8},{8,16},{16,24},{24,0},{32,40},{40,48},{48,56},{56,32},{64,72... | collective-permute-start | bytes 3145736 | tf_op jit(solution)/shard_map/ppermute | solution.py:362
  59.1 46.0 %collective-permute-start.1 = (bf16[2048,256]{1,0:T(8,128)(2,1)S(1)}, bf16[2048,256]{1,0:T(8,128)(2,1)}, u32[]{:S(2)}, u32[]{:S(2)}) collective-permute-start(bf16[2048,256]{1,0:T(8,128)(2,1)S(1)} %pad_maximum_fusion.refs_0_), channel_id=1, source_target_pairs={{0,32},{8,40},{16,48},{24,56},{32,64},{40,72},{48,80},{56,88},{64,... | collective-permute-start | bytes 3145736 | tf_op jit(solution)/shard_map/ppermute | solution.py:362
  59.8 46.0 %collective-permute-start.15 = (bf16[2048,256]{1,0:T(8,128)(2,1)S(1)}, bf16[2048,256]{1,0:T(8,128)(2,1)}, u32[]{:S(2)}, u32[]{:S(2)}) collective-permute-start(bf16[2048,256]{1,0:T(8,128)(2,1)S(1)} %constant_dynamic-update-slice_fusion.3.refs_3_), channel_id=1, source_target_pairs={{0,24},{8,0},{16,8},{24,16},{32,56},{40,32},{48,40},{56,48},{64,88... | collective-permute-start | bytes 3145736 | tf_op jit(solution)/shard_map/ppermute | solution.py:362
  61.6 47.3 %collective-permute-start.7 = (bf16[2048,256]{1,0:T(8,128)(2,1)}, bf16[2048,256]{1,0:T(8,128)(2,1)}, u32[]{:S(2)}, u32[]{:S(2)}) collective-permute-start(bf16[2048,256]{1,0:T(8,128)(2,1)} %constant_dynamic-update-slice_fusion.refs_1_), channel_id=1, source_target_pairs={{0,96},{8,104},{16,112},{24,120},{32,0},{40,8},{48,16},{56,24},{64... | collective-permute-start | bytes 3145736 | tf_op jit(solution)/shard_map/ppermute | solution.py:362
  67.4 25.4 %collective-permute-start.19 = (bf16[136,1024]{1,0:T(8,128)(2,1)S(1)}, bf16[136,1024]{1,0:T(8,128)(2,1)}, u32[]{:S(2)}, u32[]{:S(2)}) collective-permute-start(bf16[136,1024]{1,0:T(8,128)(2,1)S(1)} %get-tuple-element.47), channel_id=1, source_target_pairs={{0,96},{8,104},{16,112},{24,120},{32,64},{40,72},{48,80},{56,88},{... | collective-permute-start | bytes 835592 | tf_op jit(solution)/shard_map/ppermute | solution.py:366
  105.1 20.1 %collective-permute-start.24 = (bf16[2048,256]{1,0:T(8,128)(2,1)}, bf16[2048,256]{1,0:T(8,128)(2,1)S(1)}, u32[]{:S(2)}, u32[]{:S(2)}) collective-permute-start(bf16[2048,256]{1,0:T(8,128)(2,1)} %collective-permute-done.9.refs_4_), channel_id=1, source_target_pairs={{0,8},{8,16},{16,24},{24,0},{32,40},{40,48},{48,56},{56,32},{64,72... | collective-permute-start | bytes 3145736 | tf_op jit(solution)/shard_map/ppermute | solution.py:362
  105.2 20.2 %collective-permute-start.22 = (bf16[2048,256]{1,0:T(8,128)(2,1)}, bf16[2048,256]{1,0:T(8,128)(2,1)S(1)}, u32[]{:S(2)}, u32[]{:S(2)}) collective-permute-start(bf16[2048,256]{1,0:T(8,128)(2,1)} %collective-permute-done.1.refs_0_), channel_id=1, source_target_pairs={{0,32},{8,40},{16,48},{24,56},{32,64},{40,72},{48,80},{56,88},{64,... | collective-permute-start | bytes 3145736 | tf_op jit(solution)/shard_map/ppermute | solution.py:362
  105.8 19.5 %collective-permute-start.25 = (bf16[2048,256]{1,0:T(8,128)(2,1)}, bf16[2048,256]{1,0:T(8,128)(2,1)S(1)}, u32[]{:S(2)}, u32[]{:S(2)}) collective-permute-start(bf16[2048,256]{1,0:T(8,128)(2,1)} %collective-permute-done.15.refs_7_), channel_id=1, source_target_pairs={{0,24},{8,0},{16,8},{24,16},{32,56},{40,32},{48,40},{56,48},{64,88... | collective-permute-start | bytes 3145736 | tf_op jit(solution)/shard_map/ppermute | solution.py:362
  109.0 18.5 %collective-permute-start.23 = (bf16[2048,256]{1,0:T(8,128)(2,1)}, bf16[2048,256]{1,0:T(8,128)(2,1)}, u32[]{:S(2)}, u32[]{:S(2)}) collective-permute-start(bf16[2048,256]{1,0:T(8,128)(2,1)} %collective-permute-done.7.refs_3_), channel_id=1, source_target_pairs={{0,96},{8,104},{16,112},{24,120},{32,0},{40,8},{48,16},{56,24},{64... | collective-permute-start | bytes 3145736 | tf_op jit(solution)/shard_map/ppermute | solution.py:362
  135.2 106.9 %reduce-scatter.3.cloned.1.call-start = ((), (), s32[]{:S(2)}) async-start(), calls=%async_computation.2 | async-start | bytes 7077888 | tf_op jit(solution)/shard_map/reduce_scatter | solution.py:481
  136.4 16.8 %collective-permute-start.14 = (bf16[2048,256]{1,0:T(8,128)(2,1)S(1)}, bf16[2048,256]{1,0:T(8,128)(2,1)S(1)}, u32[]{:S(2)}, u32[]{:S(2)}) collective-permute-start(bf16[2048,256]{1,0:T(8,128)(2,1)S(1)} %copy-done.4), channel_id=1, source_target_pairs={{0,24},{8,0},{16,8},{24,16},{32,56},{40,32},{48,40},{56,48},{64,88... | collective-permute-start | bytes 3145736 | tf_op jit(solution)/shard_map/ppermute | solution.py:362
  136.7 18.1 %collective-permute-start.6 = (bf16[2048,256]{1,0:T(8,128)(2,1)S(1)}, bf16[2048,256]{1,0:T(8,128)(2,1)}, u32[]{:S(2)}, u32[]{:S(2)}) collective-permute-start(bf16[2048,256]{1,0:T(8,128)(2,1)S(1)} %copy-done.6), channel_id=1, source_target_pairs={{0,96},{8,104},{16,112},{24,120},{32,0},{40,8},{48,16},{56,24},{64... | collective-permute-start | bytes 3145736 | tf_op jit(solution)/shard_map/ppermute | solution.py:362
  140.4 18.2 %collective-permute-start.13 = (bf16[2048,256]{1,0:T(8,128)(2,1)}, bf16[2048,256]{1,0:T(8,128)(2,1)}, u32[]{:S(2)}, u32[]{:S(2)}) collective-permute-start(bf16[2048,256]{1,0:T(8,128)(2,1)} %copy-done.8), channel_id=1, source_target_pairs={{0,8},{8,16},{16,24},{24,0},{32,40},{40,48},{48,56},{56,32},{64,72... | collective-permute-start | bytes 3145736 | tf_op jit(solution)/shard_map/ppermute | solution.py:362
  142.1 17.6 %collective-permute-start.5 = (bf16[2048,256]{1,0:T(8,128)(2,1)}, bf16[2048,256]{1,0:T(8,128)(2,1)}, u32[]{:S(2)}, u32[]{:S(2)}) collective-permute-start(bf16[2048,256]{1,0:T(8,128)(2,1)} %constant_dynamic-update-slice_fusion.refs_1_), channel_id=1, source_target_pairs={{0,32},{8,40},{16,48},{24,56},{32,64},{40,72},{48,80},{56,88},{64,... | collective-permute-start | bytes 3145736 | tf_op jit(solution)/shard_map/ppermute | solution.py:362
  184.5 16.7 %collective-permute-start.26 = (bf16[136,1024]{1,0:T(8,128)(2,1)}, bf16[136,1024]{1,0:T(8,128)(2,1)S(1)}, u32[]{:S(2)}, u32[]{:S(2)}) collective-permute-start(bf16[136,1024]{1,0:T(8,128)(2,1)} %head.1), channel_id=1, source_target_pairs={{0,24},{8,16},{16,8},{24,0},{32,56},{40,48},{48,40},{56,32},{64,88... | collective-permute-start | bytes 835592 | tf_op jit(solution)/shard_map/ppermute | solution.py:366
  185.9 15.2 %collective-permute-start.27 = (bf16[136,1024]{1,0:T(8,128)(2,1)}, bf16[136,1024]{1,0:T(8,128)(2,1)S(1)}, u32[]{:S(2)}, u32[]{:S(2)}) collective-permute-start(bf16[136,1024]{1,0:T(8,128)(2,1)} %head.1), channel_id=1, source_target_pairs={{0,16},{8,24},{16,0},{24,8},{32,48},{40,56},{48,32},{56,40},{64,80... | collective-permute-start | bytes 835592 | tf_op jit(solution)/shard_map/ppermute | solution.py:366
  186.5 14.7 %collective-permute-start.28 = (bf16[136,1024]{1,0:T(8,128)(2,1)}, bf16[136,1024]{1,0:T(8,128)(2,1)S(1)}, u32[]{:S(2)}, u32[]{:S(2)}) collective-permute-start(bf16[136,1024]{1,0:T(8,128)(2,1)} %head.1), channel_id=1, source_target_pairs={{0,8},{8,0},{16,24},{24,16},{32,40},{40,32},{48,56},{56,48},{64,72... | collective-permute-start | bytes 835592 | tf_op jit(solution)/shard_map/ppermute | solution.py:366
  (36 other events, 474.6 us)
Sparse Core Ops, SparseCore 0:
  135.3 30.4 reduce-scatter.4
  175.9 38.0 reduce-scatter.2

commit v5 on v4

--- a/solution.py
+++ b/solution.py
@@ -239,7 +239,7 @@
             acc_in, refs = refs[0], refs[2:]
         result, acc, buf, sems = refs
     else:
-        gated, result, buf, sems = refs
+        gated, (result, buf, sems) = refs[0], refs[1 + more :]
     step = pl.program_id(0)
     chans = gated.shape[1]
     width = buf.shape[2] // per
@@ -299,9 +299,12 @@
         ]
         operands += [out_grad] * per
         if more:
-            in_specs += [whole, pl.BlockSpec(memory_space=pl.ANY)]
-            operands += [before[2], before[1]]
-            aliases = {len(operands): 0}
+            in_specs.append(whole)
+            operands.append(before[2])
+    if more:
+        in_specs.append(pl.BlockSpec(memory_space=pl.ANY))
+        operands.append(before[1])
+        aliases = {len(operands): 0}
     result_shape = jax.ShapeDtypeStruct((rows, total * per * width), bf16)
     result_spec = pl.BlockSpec((rows, per * width), lambda i, c: (0, i + offset))
 
@@ -351,8 +354,9 @@
     rows, chans = projected.shape[1:]
     width = out_weight.shape[1] // 2
     ctx_count, tp_count = lax.axis_size("ctx"), lax.axis_size("tp")
-    me = lax.axis_index("ctx")
-    zi, xi = me // SIDE, me % SIDE
+    me = lax.axis_index("ctx").astype(jnp.uint32)
+    zu, xu = me >> 2, me & 3
+    zi, xi = zu.astype(jnp.int32), xu.astype(jnp.int32)
 
     def ring(value, axis, step):
         if axis == "x":
@@ -384,7 +388,7 @@
     halves, dz, dx = np.array(
         [b for far in ((0,), (-1, 1), (2,)) for half in (0, 1) for b in blocks(half, order4, far)]
     ).T
-    table = 2 * ((zi + dz) % SIDE * SIDE + (xi + dx) % SIDE) + halves
+    table = 2 * (((zi + dz) & 3) * SIDE + ((xi + dx) & 3)) + halves
     table = jnp.concatenate([jnp.reshape(zi, (1,)), table]).astype(jnp.int32)
 
     positions = jnp.arange(ctx_count, dtype=jnp.int32)
@@ -407,16 +411,12 @@
     def along_z(payloads):
         return [payloads[0]] + [swap(payloads[k], "z", k) for k in (1, 2, 3)]
 
-    def chosen(got, table):
-        out = []
-        for k in range(SIDE):
-            source = jnp.maximum(at(table, (zi ^ k) * SIDE + xi), 0)
-            out.append(pick(got, (source % SIDE) ^ xi))
-        return out
-
-    def landed(got, table):
-        source = at(table, me)
-        value = pick(got, (jnp.maximum(source, 0) // SIDE) ^ zi)
+    def chosen(got, sources):
+        return [pick(got, (at(sources, me ^ (4 * k)) & 3) ^ xi) for k in range(SIDE)]
+
+    def landed(got, sources):
+        source = at(sources, me)
+        value = pick(got, ((source >> 2) & 3) ^ zi)
         return jnp.where(source >= 0, value, jnp.zeros_like(value))
 
     near = projected[1:, rows - BLK - PAD :].astype(f32)
@@ -480,12 +480,10 @@
     def scatter(value):
         return lax.psum_scatter(value, "tp", scatter_dimension=0, tiled=True)
 
-    early = multiply_pieces(near_a + near_b, table, gated, out_grad, 6)
+    early = multiply_pieces(near_a + near_b, table, gated, out_grad, 8)
     out1, acc = multiply_pieces(
-        mid_a + mid_b, table, gated, out_grad, 6, (2, *early)
-    )
-    out1 = scatter(out1)
-
+        mid_a + mid_b, table, gated, out_grad, 8, (2, *early)
+    )
     quarter = BLK // SIDE
     lasts = [w.reshape(2, chans, width) for w in far_a + far_b]
     last_spec = pl.BlockSpec((2, tile, width), lambda i, c: (0, i, 0))
@@ -574,8 +572,10 @@
     sums = [g[BLK + PAD :].astype(f32) for g in got]
     my_quarter = (sums[0] + sums[1]) + (sums[2] + sums[3])
 
-    (out3,) = multiply_pieces(far_a + far_b, table, gated, per=2)
-    out3 = scatter(out3)
+    (out1,) = multiply_pieces(
+        far_a + far_b, table, gated, None, 16, (12, out1), per=2
+    )
+    out1 = scatter(out1)
 
     low = rows - BLK - PAD
 
@@ -639,20 +639,20 @@
     short_total = message[quarter : quarter + 9].reshape(3, 3, chans)
 
     share = rows // tp_count
-    counts = tuple(o.shape[1] // width for o in (out1, out3))
+    counts = tuple(o.shape[1] // width for o in (out1,))
     collect = pl.pallas_call(
         lambda cols, *refs: collect_kernel(counts, cols, *refs),
         grid_spec=pltpu.PrefetchScalarGridSpec(
             num_scalar_prefetch=1,
             grid=(1,),
-            in_specs=[pl.BlockSpec(o.shape, lambda i, c: (0, 0)) for o in (out1, out3)],
+            in_specs=[pl.BlockSpec(o.shape, lambda i, c: (0, 0)) for o in (out1,)],
             out_specs=pl.BlockSpec((share, 2 * width * ctx_count), lambda i, c: (0, 0)),
         ),
         out_shape=jax.ShapeDtypeStruct((share, 2 * width * ctx_count), bf16),
         cost_estimate=pl.CostEstimate(flops=10_000_000, bytes_accessed=5 << 20, transcendentals=0),
         name="collect",
     )
-    mixed = collect(table, out1, out3)
+    mixed = collect(table, out1)
 
     scale = 1.0 / math.sqrt(rows * ctx_count)
     return mixed, gp, long_total.astype(f32) * scale, short_total * scale

time: 253 us -> 259 us (1.024)
  local copies, waits for them, and re-layouts: 9.65 us -> 17.7 us
  starting transfers between devices: 54.5 us -> 51.7 us
    ppermute x20, waiting for transfers between devices: 30.2 us -> 44.5 us  [ring(): return lax.ppermute(value, 'ctx', pairs)]
    ppermute x18, waiting for transfers between devices: 44.2 us -> 30.7 us  [swap(): lax.ppermute(value, 'ctx', [(d, d ^ shift) for d in range(ctx_count)])]
    unnamed x46 -> x50, local copies, waits for them, and re-layouts: 3.37 us -> 8.38 us
    ppermute x20, starting transfers between devices: 31.7 us -> 26.8 us  [ring(): return lax.ppermute(value, 'ctx', pairs)]
  transfers between devices with their start and end apart: 40 -> 39, of which waited for: 17 -> 14; matrix products, arithmetic and copies ran while one was open for 7% -> 10% of each run, Pallas kernels for 27% -> 26%
where the time goes in v5:
time: 259 us; the launch traced here: 258 us
  Pallas kernels  78.2 us (30%)
  waiting for transfers between devices  75.1 us (29%)
  starting transfers between devices  51.7 us (20%)
  between operations  22.2 us (9%)
  local copies, waits for them, and re-layouts  17.7 us (7%)
  other arithmetic  12.7 us (5%)
    ppermute x20, waiting for transfers between devices, ring(): return lax.ppermute(value, 'ctx', pairs)  44.5 us
    pallas_call x3, Pallas kernels, multiply_pieces(): pl.pallas_call(kernel, grid_spec=pltpu.PrefetchScalarGridSpec(num_scalar_...  33.7 us
    ppermute x18, waiting for transfers between devices, swap(): lax.ppermute(value, 'ctx', [(d, d ^ shift) for d in range(ctx_count)])  30.7 us
    ppermute x20, starting transfers between devices, ring(): return lax.ppermute(value, 'ctx', pairs)  26.8 us
    ppermute x18, starting transfers between devices, swap(): lax.ppermute(value, 'ctx', [(d, d ^ shift) for d in range(ctx_count)])  24.8 us
    pallas_call x1, Pallas kernels, on_device(): backward(table, acc, act, mspec, fspec, skip_row, fwd, inv_now, inv_lag,...  12.4 us
    pallas_call x1, Pallas kernels, on_device(): forward(projected, left, short_filter, long_filter, skip_row, fwd, inv_late)  8.91 us
    unnamed x50, local copies, waits for them, and re-layouts  8.38 us
  transfers between devices with their start and end apart: 39, of which 14 were waited for; matrix products, arithmetic and copies ran while one was open for 10% of the time, Pallas kernels for 26%

profile of v5, /device:TPU:24, one launch (start us, length us, event | category | flops | bytes accessed | tf_op | source)
XLA Modules:
  0.0 257.6 jit_solution(13700918511426957483)
XLA Ops:
  13.9 2.8 %collective-permute-start.16 = (bf16[136,1024]{1,0:T(8,128)(2,1)}, bf16[136,1024]{1,0:T(8,128)(2,1)}, u32[]{:S(2)}, u32[]{:S(2)}) collective-permute-start(bf16[136,1024]{1,0:T(8,128)(2,1)} %maximum_maximum_fusion), channel_id=1, source_target_pairs={{0,24},{8,16},{16,8},{24,0},{32,56},{40,48},{48,40},{56,32},{64,88... | collective-permute-start | bytes 835592 | tf_op jit(solution)/shard_map/ppermute | solution.py:370
  24.5 2.8 %collective-permute-start.3 = (bf16[1024,256]{1,0:T(8,128)(2,1)S(1)}, bf16[1024,256]{1,0:T(8,128)(2,1)S(1)}, u32[]{:S(2)}, u32[]{:S(2)}) collective-permute-start(bf16[1024,256]{1,0:T(8,128)(2,1)S(1)} %get-tuple-element.49), channel_id=1, source_target_pairs={{0,24},{8,0},{16,8},{24,16},{32,56},{40,32},{48,40},{56,48},{64,88... | collective-permute-start | bytes 1572872 | tf_op jit(solution)/shard_map/ppermute | solution.py:366
  27.4 13.2 %collective-permute-done = bf16[1024,256]{1,0:T(8,128)(2,1)S(1)} collective-permute-done((bf16[1024,256]{1,0:T(8,128)(2,1)S(1)}, bf16[1024,256]{1,0:T(8,128)(2,1)S(1)}, u32[]{:S(2)}, u32[]{:S(2)}) %collective-permute-start) | collective-permute-done | bytes 524320 | tf_op jit(solution)/shard_map/ppermute | solution.py:366
  49.6 3.2 %collective-permute-start.19 = (bf16[136,1024]{1,0:T(8,128)(2,1)}, bf16[136,1024]{1,0:T(8,128)(2,1)}, u32[]{:S(2)}, u32[]{:S(2)}) collective-permute-start(bf16[136,1024]{1,0:T(8,128)(2,1)} %get-tuple-element.47), channel_id=1, source_target_pairs={{0,96},{8,104},{16,112},{24,120},{32,64},{40,72},{48,80},{56,88},{... | collective-permute-start | bytes 835592 | tf_op jit(solution)/shard_map/ppermute | solution.py:370
  56.9 3.4 %collective-permute-start.5 = (bf16[512,256]{1,0:T(8,128)(2,1)}, bf16[512,256]{1,0:T(8,128)(2,1)}, u32[]{:S(2)}, u32[]{:S(2)}) collective-permute-start(bf16[512,256]{1,0:T(8,128)(2,1)} %slice.109), channel_id=1, source_target_pairs={{0,24},{8,0},{16,8},{24,16},{32,56},{40,32},{48,40},{56,48},{64,88... | collective-permute-start | bytes 786440 | tf_op jit(solution)/shard_map/ppermute | solution.py:366
  62.4 15.4 %collective-permute-done.19 = bf16[136,1024]{1,0:T(8,128)(2,1)} collective-permute-done((bf16[136,1024]{1,0:T(8,128)(2,1)}, bf16[136,1024]{1,0:T(8,128)(2,1)}, u32[]{:S(2)}, u32[]{:S(2)}) %collective-permute-start.19) | collective-permute-done | bytes 278560 | tf_op jit(solution)/shard_map/ppermute | solution.py:370
  79.4 3.2 %collective-permute-start.13 = (bf16[512,256]{1,0:T(8,128)(2,1)S(1)}, bf16[512,256]{1,0:T(8,128)(2,1)S(1)}, u32[]{:S(2)}, u32[]{:S(2)}) collective-permute-start(bf16[512,256]{1,0:T(8,128)(2,1)S(1)} %slice.111), channel_id=1, source_target_pairs={{0,96},{8,104},{16,112},{24,120},{32,0},{40,8},{48,16},{56,24},{64... | collective-permute-start | bytes 786440 | tf_op jit(solution)/shard_map/ppermute | solution.py:366
  87.0 3.2 %collective-permute-done.13 = bf16[512,256]{1,0:T(8,128)(2,1)S(1)} collective-permute-done((bf16[512,256]{1,0:T(8,128)(2,1)S(1)}, bf16[512,256]{1,0:T(8,128)(2,1)S(1)}, u32[]{:S(2)}, u32[]{:S(2)}) %collective-permute-start.13) | collective-permute-done | bytes 262176 | tf_op jit(solution)/shard_map/ppermute | solution.py:366
  93.4 3.7 %collective-permute-done.20 = bf16[136,1024]{1,0:T(8,128)(2,1)S(1)} collective-permute-done((bf16[136,1024]{1,0:T(8,128)(2,1)}, bf16[136,1024]{1,0:T(8,128)(2,1)S(1)}, u32[]{:S(2)}, u32[]{:S(2)}) %collective-permute-start.20) | collective-permute-done | bytes 278560 | tf_op jit(solution)/shard_map/ppermute | solution.py:370
  98.3 3.3 %collective-permute-done.21 = bf16[136,1024]{1,0:T(8,128)(2,1)S(1)} collective-permute-done((bf16[136,1024]{1,0:T(8,128)(2,1)S(1)}, bf16[136,1024]{1,0:T(8,128)(2,1)S(1)}, u32[]{:S(2)}, u32[]{:S(2)}) %collective-permute-start.21) | collective-permute-done | bytes 278560 | tf_op jit(solution)/shard_map/ppermute | solution.py:370
  110.1 8.9 %forward.1 = (bf16[512,1024]{1,0:T(8,128)(2,1)}, f32[512,1024]{1,0:T(8,128)}, f32[3,512,1024]{2,1,0:T(8,128)}, f32[4,256,1024]{2,1,0:T(8,128)}, f32[256,1024]{1,0:T(8,128)}) custom-call(bf16[3,512,1024]{2,1,0:T(8,128)(2,1)} %proj.5, bf16[136,1024]{1,0:T(8,128)(2,1)} %select_select_fusion.3.halo, f32[3,3,1024]{2,1,0:T(4,128)} %sf.5, bf16[128,1024]{1,0:T(8,128)(2,1)} %lf.3, ...), custom_call_target="tpu_custom_call" | custom-call | flops 8000000000 | bytes 20971520 | tf_op jit(solution)/shard_map/forward/pallas_call | solution.py:476
  119.0 5.2 %collective-permute-done.23.refs_2_ = bf16[2048,256]{1,0:T(8,128)(2,1)} collective-permute-done((bf16[2048,256]{1,0:T(8,128)(2,1)S(1)}, bf16[2048,256]{1,0:T(8,128)(2,1)}, u32[]{:S(2)}, u32[]{:S(2)}) %collective-permute-start.23) | collective-permute-done | bytes 1048608 | tf_op jit(solution)/shard_map/ppermute | solution.py:366
  124.6 19.1 %collective-permute-done.6.refs_3_ = bf16[2048,256]{1,0:T(8,128)(2,1)} collective-permute-done((bf16[2048,256]{1,0:T(8,128)(2,1)}, bf16[2048,256]{1,0:T(8,128)(2,1)}, u32[]{:S(2)}, u32[]{:S(2)}) %collective-permute-start.6) | collective-permute-done | bytes 1048608 | tf_op jit(solution)/shard_map/ppermute | solution.py:366
  145.5 10.1 %pieces.3 = (bf16[512,8192]{1,0:T(8,128)(2,1)}, f32[512,1024]{1,0:T(8,128)}) custom-call(s32[33]{0:T(128)} %pad_add_fusion.cols_ref.cols.place, bf16[2048,256]{1,0:T(8,128)(2,1)} %copy-done.4, bf16[2048,256]{1,0:T(8,128)(2,1)} %constant_dynamic-update-slice_fusion.refs_1_, bf16[2048,256]{1,0:T(8,128)(2,1)} %copy-done.3, ...), custom_call_target="tpu_custom_call" | custom-call | flops 4294967296 | bytes 11534336 | tf_op jit(solution)/shard_map/pieces/pallas_call | solution.py:315
  155.6 16.0 %pieces.4 = (bf16[512,8192]{1,0:T(8,128)(2,1)}, f32[512,1024]{1,0:T(8,128)}) custom-call(s32[33]{0:T(128)} %pad_add_fusion.cols_ref.cols.place, bf16[2048,256]{1,0:T(8,128)(2,1)} %collective-permute-done.1.refs_0_, bf16[2048,256]{1,0:T(8,128)(2,1)} %collective-permute-done.22.refs_1_, ...), custom_call_target="tpu_custom_call", output_to_operand_aliasing={{0}: (15, {})} | custom-call | flops 8589934592 | bytes 19922944 | tf_op jit(solution)/shard_map/pieces/pallas_call | solution.py:315
  173.2 7.6 %pieces.5 = bf16[512,8192]{1,0:T(8,128)(2,1)} custom-call(s32[33]{0:T(128)} %pad_add_fusion.cols_ref.cols.place, bf16[2048,256]{1,0:T(8,128)(2,1)} %copy-done.1, bf16[2048,256]{1,0:T(8,128)(2,1)} %copy-done.2, bf16[2048,256]{1,0:T(8,128)(2,1)} %copy-done, bf16[2048,256]{1,0:T(8,128)(2,1)} %collective-permute-done.15.refs_3_, ...), custom_call_target="tpu_custom_call", output_to_operand_aliasing={{}: (6, {})} | custom-call | flops 2147483648 | bytes 11534336 | tf_op jit(solution)/shard_map/pieces/pallas_call | solution.py:315
  182.8 6.3 %head.1 = bf16[136,1024]{1,0:T(8,128)(2,1)} custom-call(s32[33]{0:T(128)} %pad_add_fusion.cols_ref.cols.place, f32[512,1024]{1,0:T(8,128)} %get-tuple-element.27.acc, f32[3,512,1024]{2,1,0:T(8,128)} %get-tuple-element.28.act0.act12.act.actn, f32[3,512,1024]{2,1,0:T(8,128)} %get-tuple-element.28.act0.act12.act.actn, ...), custom_call_target="tpu_custom_call" | custom-call | flops 600000000 | bytes 6291456 | tf_op jit(solution)/shard_map/head/pallas_call | solution.py:525
  193.3 12.4 %backward.1 = (f32[512,1024]{1,0:T(8,128)}, bf16[32,1024]{1,0:T(8,128)(2,1)}, bf16[32,1024]{1,0:T(8,128)(2,1)}, bf16[32,1024]{1,0:T(8,128)(2,1)}, bf16[32,1024]{1,0:T(8,128)(2,1)}, /*index=5*/f32[512,1024]{1,0:T(8,128)}) custom-call(s32[33]{0:T(128)} %pad_add_fusion.cols_ref.cols.place, f32[512,1024]{1,0:T(8,128)} %get-tuple-element.27.acc, ...), custom_call_target="tpu_custom_call" | custom-call | flops 8000000000 | bytes 20971520 | tf_op jit(solution)/shard_map/backward/pallas_call | solution.py:564
  206.8 2.5 collective-permute-start.29
  213.3 7.8 %top.1 = (bf16[3,512,1024]{2,1,0:T(8,128)(2,1)}, f32[16,1024]{1,0:T(8,128)}) custom-call(f32[512,1024]{1,0:T(8,128)} %get-tuple-element.31.bg.bgn, f32[512,1024]{1,0:T(8,128)} %get-tuple-element.32.convh.conv.convn, f32[512,1024]{1,0:T(8,128)} %get-tuple-element.33.gmix.gmixn, f32[3,512,1024]{2,1,0:T(8,128)} %get-tuple-element.28.act0.act12.act.actn, ...), custom_call_target="tpu_custom_call" | custom-call | flops 200000000 | bytes 10485760 | tf_op jit(solution)/shard_map/top/pallas_call | solution.py:610
  221.9 6.0 %bottom.1 = (bf16[3,512,1024]{2,1,0:T(8,128)(2,1)}, f32[16,1024]{1,0:T(8,128)}) custom-call(f32[512,1024]{1,0:T(8,128)} %get-tuple-element.31.bg.bgn, f32[512,1024]{1,0:T(8,128)} %get-tuple-element.32.convh.conv.convn, f32[512,1024]{1,0:T(8,128)} %get-tuple-element.33.gmix.gmixn, ...), custom_call_target="tpu_custom_call", output_to_operand_aliasing={{0}: (11, {})} | custom-call | flops 2000000000 | bytes 5242880 | tf_op jit(solution)/shard_map/bottom/pallas_call | solution.py:629
  237.4 2.6 %collective-permute-start.35 = (bf16[48,1024]{1,0:T(8,128)(2,1)S(1)}, bf16[48,1024]{1,0:T(8,128)(2,1)S(1)}, u32[]{:S(2)}, u32[]{:S(2)}) collective-permute-start(bf16[48,1024]{1,0:T(8,128)(2,1)S(1)} %add_convert_fusion), channel_id=1, source_target_pairs={{0,96},{8,104},{16,112},{24,120},{32,64},{40,72},{48,80},{56,88},{... | collective-permute-start | bytes 294920 | tf_op jit(solution)/shard_map/ppermute | solution.py:370
  243.3 2.8 %collective-permute-done.36 = bf16[48,1024]{1,0:T(8,128)(2,1)S(1)} collective-permute-done((bf16[48,1024]{1,0:T(8,128)(2,1)S(1)}, bf16[48,1024]{1,0:T(8,128)(2,1)S(1)}, u32[]{:S(2)}, u32[]{:S(2)}) %collective-permute-start.36) | collective-permute-done | bytes 98336 | tf_op jit(solution)/shard_map/ppermute | solution.py:370
  247.7 3.1 %collect.1 = bf16[64,8192]{1,0:T(8,128)(2,1)} custom-call(s32[33]{0:T(128)} %pad_add_fusion.cols_ref.cols.place, bf16[64,8192]{1,0:T(8,128)(2,1)} %reduce-scatter.2.cloned.1.call-done.refs_0_), custom_call_target="tpu_custom_call" | custom-call | flops 10000000 | bytes 5242880 | tf_op jit(solution)/shard_map/collect/pallas_call | solution.py:655
  (154 shorter events, 70.9 us)
Async XLA Ops:
  7.2 240.5 %reduce-scatter.2.cloned.1.call-start = ((), (), s32[]{:S(2)}) async-start(), calls=%async_computation.1 | async-start | bytes 9437184 | tf_op jit(solution)/shard_map/reduce_scatter | solution.py:481
  8.5 16.0 %collective-permute-start.8 = (bf16[1024,256]{1,0:T(8,128)(2,1)S(1)}, bf16[1024,256]{1,0:T(8,128)(2,1)S(1)}, u32[]{:S(2)}, u32[]{:S(2)}) collective-permute-start(bf16[1024,256]{1,0:T(8,128)(2,1)S(1)} %get-tuple-element.48), channel_id=1, source_target_pairs={{0,32},{8,40},{16,48},{24,56},{32,64},{40,72},{48,80},{56,88},{64,... | collective-permute-start | bytes 1572872 | tf_op jit(solution)/shard_map/ppermute | solution.py:366
  13.9 31.2 %collective-permute-start.16 = (bf16[136,1024]{1,0:T(8,128)(2,1)}, bf16[136,1024]{1,0:T(8,128)(2,1)}, u32[]{:S(2)}, u32[]{:S(2)}) collective-permute-start(bf16[136,1024]{1,0:T(8,128)(2,1)} %maximum_maximum_fusion), channel_id=1, source_target_pairs={{0,24},{8,16},{16,8},{24,0},{32,56},{40,48},{48,40},{56,32},{64,88... | collective-permute-start | bytes 835592 | tf_op jit(solution)/shard_map/ppermute | solution.py:370
  16.6 30.6 %collective-permute-start.17 = (bf16[136,1024]{1,0:T(8,128)(2,1)}, bf16[136,1024]{1,0:T(8,128)(2,1)}, u32[]{:S(2)}, u32[]{:S(2)}) collective-permute-start(bf16[136,1024]{1,0:T(8,128)(2,1)} %maximum_maximum_fusion), channel_id=1, source_target_pairs={{0,16},{8,24},{16,0},{24,8},{32,48},{40,56},{48,32},{56,40},{64,80... | collective-permute-start | bytes 835592 | tf_op jit(solution)/shard_map/ppermute | solution.py:370
  17.4 29.8 %collective-permute-start.18 = (bf16[136,1024]{1,0:T(8,128)(2,1)}, bf16[136,1024]{1,0:T(8,128)(2,1)}, u32[]{:S(2)}, u32[]{:S(2)}) collective-permute-start(bf16[136,1024]{1,0:T(8,128)(2,1)} %maximum_maximum_fusion), channel_id=1, source_target_pairs={{0,8},{8,0},{16,24},{24,16},{32,40},{40,32},{48,56},{56,48},{64,72... | collective-permute-start | bytes 835592 | tf_op jit(solution)/shard_map/ppermute | solution.py:370
  18.0 22.6 %collective-permute-start = (bf16[1024,256]{1,0:T(8,128)(2,1)S(1)}, bf16[1024,256]{1,0:T(8,128)(2,1)S(1)}, u32[]{:S(2)}, u32[]{:S(2)}) collective-permute-start(bf16[1024,256]{1,0:T(8,128)(2,1)S(1)} %get-tuple-element.49), channel_id=1, source_target_pairs={{0,8},{8,16},{16,24},{24,0},{32,40},{40,48},{48,56},{56,32},{64,72... | collective-permute-start | bytes 1572872 | tf_op jit(solution)/shard_map/ppermute | solution.py:366
  24.5 29.1 %collective-permute-start.3 = (bf16[1024,256]{1,0:T(8,128)(2,1)S(1)}, bf16[1024,256]{1,0:T(8,128)(2,1)S(1)}, u32[]{:S(2)}, u32[]{:S(2)}) collective-permute-start(bf16[1024,256]{1,0:T(8,128)(2,1)S(1)} %get-tuple-element.49), channel_id=1, source_target_pairs={{0,24},{8,0},{16,8},{24,16},{32,56},{40,32},{48,40},{56,48},{64,88... | collective-permute-start | bytes 1572872 | tf_op jit(solution)/shard_map/ppermute | solution.py:366
  45.0 56.8 %collective-permute-start.9 = (bf16[2048,256]{1,0:T(8,128)(2,1)S(1)}, bf16[2048,256]{1,0:T(8,128)(2,1)}, u32[]{:S(2)}, u32[]{:S(2)}) collective-permute-start(bf16[2048,256]{1,0:T(8,128)(2,1)S(1)} %pad_maximum_fusion.1.refs_2_), channel_id=1, source_target_pairs={{0,8},{8,16},{16,24},{24,0},{32,40},{40,48},{48,56},{56,32},{64,72... | collective-permute-start | bytes 3145736 | tf_op jit(solution)/shard_map/ppermute | solution.py:366
  47.2 56.4 %collective-permute-start.1 = (bf16[2048,256]{1,0:T(8,128)(2,1)S(1)}, bf16[2048,256]{1,0:T(8,128)(2,1)}, u32[]{:S(2)}, u32[]{:S(2)}) collective-permute-start(bf16[2048,256]{1,0:T(8,128)(2,1)S(1)} %pad_maximum_fusion.refs_0_), channel_id=1, source_target_pairs={{0,32},{8,40},{16,48},{24,56},{32,64},{40,72},{48,80},{56,88},{64,... | collective-permute-start | bytes 3145736 | tf_op jit(solution)/shard_map/ppermute | solution.py:366
  49.6 28.1 %collective-permute-start.19 = (bf16[136,1024]{1,0:T(8,128)(2,1)}, bf16[136,1024]{1,0:T(8,128)(2,1)}, u32[]{:S(2)}, u32[]{:S(2)}) collective-permute-start(bf16[136,1024]{1,0:T(8,128)(2,1)} %get-tuple-element.47), channel_id=1, source_target_pairs={{0,96},{8,104},{16,112},{24,120},{32,64},{40,72},{48,80},{56,88},{... | collective-permute-start | bytes 835592 | tf_op jit(solution)/shard_map/ppermute | solution.py:370
  53.6 25.8 %collective-permute-start.4 = (bf16[512,256]{1,0:T(8,128)(2,1)}, bf16[512,256]{1,0:T(8,128)(2,1)}, u32[]{:S(2)}, u32[]{:S(2)}) collective-permute-start(bf16[512,256]{1,0:T(8,128)(2,1)} %slice.108), channel_id=1, source_target_pairs={{0,8},{8,16},{16,24},{24,0},{32,40},{40,48},{48,56},{56,32},{64,72... | collective-permute-start | bytes 786440 | tf_op jit(solution)/shard_map/ppermute | solution.py:366
  56.9 22.5 %collective-permute-start.5 = (bf16[512,256]{1,0:T(8,128)(2,1)}, bf16[512,256]{1,0:T(8,128)(2,1)}, u32[]{:S(2)}, u32[]{:S(2)}) collective-permute-start(bf16[512,256]{1,0:T(8,128)(2,1)} %slice.109), channel_id=1, source_target_pairs={{0,24},{8,0},{16,8},{24,16},{32,56},{40,32},{48,40},{56,48},{64,88... | collective-permute-start | bytes 786440 | tf_op jit(solution)/shard_map/ppermute | solution.py:366
  77.8 31.9 %collective-permute-start.25 = (bf16[2048,256]{1,0:T(8,128)(2,1)S(1)}, bf16[2048,256]{1,0:T(8,128)(2,1)}, u32[]{:S(2)}, u32[]{:S(2)}) collective-permute-start(bf16[2048,256]{1,0:T(8,128)(2,1)S(1)} %pad_maximum_fusion.1.refs_2_), channel_id=1, source_target_pairs={{0,24},{8,0},{16,8},{24,16},{32,56},{40,32},{48,40},{56,48},{64,88... | collective-permute-start | bytes 3145736 | tf_op jit(solution)/shard_map/ppermute | solution.py:366
  97.1 27.1 %collective-permute-start.23 = (bf16[2048,256]{1,0:T(8,128)(2,1)S(1)}, bf16[2048,256]{1,0:T(8,128)(2,1)}, u32[]{:S(2)}, u32[]{:S(2)}) collective-permute-start(bf16[2048,256]{1,0:T(8,128)(2,1)S(1)} %pad_maximum_fusion.refs_0_), channel_id=1, source_target_pairs={{0,96},{8,104},{16,112},{24,120},{32,0},{40,8},{48,16},{56,24},{64... | collective-permute-start | bytes 3145736 | tf_op jit(solution)/shard_map/ppermute | solution.py:366
  101.6 42.0 %collective-permute-start.6 = (bf16[2048,256]{1,0:T(8,128)(2,1)}, bf16[2048,256]{1,0:T(8,128)(2,1)}, u32[]{:S(2)}, u32[]{:S(2)}) collective-permute-start(bf16[2048,256]{1,0:T(8,128)(2,1)} %constant_dynamic-update-slice_fusion.refs_1_), channel_id=1, source_target_pairs={{0,96},{8,104},{16,112},{24,120},{32,0},{40,8},{48,16},{56,24},{64... | collective-permute-start | bytes 3145736 | tf_op jit(solution)/shard_map/ppermute | solution.py:366
  101.8 42.0 %collective-permute-start.22 = (bf16[2048,256]{1,0:T(8,128)(2,1)}, bf16[2048,256]{1,0:T(8,128)(2,1)}, u32[]{:S(2)}, u32[]{:S(2)}) collective-permute-start(bf16[2048,256]{1,0:T(8,128)(2,1)} %constant_dynamic-update-slice_fusion.refs_1_), channel_id=1, source_target_pairs={{0,32},{8,40},{16,48},{24,56},{32,64},{40,72},{48,80},{56,88},{64,... | collective-permute-start | bytes 3145736 | tf_op jit(solution)/shard_map/ppermute | solution.py:366
  103.6 20.9 %collective-permute-start.14 = (bf16[2048,256]{1,0:T(8,128)(2,1)}, bf16[2048,256]{1,0:T(8,128)(2,1)}, u32[]{:S(2)}, u32[]{:S(2)}) collective-permute-start(bf16[2048,256]{1,0:T(8,128)(2,1)} %constant_dynamic-update-slice_fusion.3.refs_3_), channel_id=1, source_target_pairs={{0,24},{8,0},{16,8},{24,16},{32,56},{40,32},{48,40},{56,48},{64,88... | collective-permute-start | bytes 3145736 | tf_op jit(solution)/shard_map/ppermute | solution.py:366
  109.7 45.9 %collective-permute-start.24 = (bf16[2048,256]{1,0:T(8,128)(2,1)}, bf16[2048,256]{1,0:T(8,128)(2,1)}, u32[]{:S(2)}, u32[]{:S(2)}) collective-permute-start(bf16[2048,256]{1,0:T(8,128)(2,1)} %constant_dynamic-update-slice_fusion.3.refs_3_), channel_id=1, source_target_pairs={{0,8},{8,16},{16,24},{24,0},{32,40},{40,48},{48,56},{56,32},{64,72... | collective-permute-start | bytes 3145736 | tf_op jit(solution)/shard_map/ppermute | solution.py:366
  124.2 47.4 %collective-permute-start.10 = (bf16[2048,256]{1,0:T(8,128)(2,1)}, bf16[2048,256]{1,0:T(8,128)(2,1)S(1)}, u32[]{:S(2)}, u32[]{:S(2)}) collective-permute-start(bf16[2048,256]{1,0:T(8,128)(2,1)} %collective-permute-done.9.refs_4_), channel_id=1, source_target_pairs={{0,8},{8,16},{16,24},{24,0},{32,40},{40,48},{48,56},{56,32},{64,72... | collective-permute-start | bytes 3145736 | tf_op jit(solution)/shard_map/ppermute | solution.py:366
  124.6 47.0 %collective-permute-start.2 = (bf16[2048,256]{1,0:T(8,128)(2,1)}, bf16[2048,256]{1,0:T(8,128)(2,1)S(1)}, u32[]{:S(2)}, u32[]{:S(2)}) collective-permute-start(bf16[2048,256]{1,0:T(8,128)(2,1)} %collective-permute-done.1.refs_0_), channel_id=1, source_target_pairs={{0,32},{8,40},{16,48},{24,56},{32,64},{40,72},{48,80},{56,88},{64,... | collective-permute-start | bytes 3145736 | tf_op jit(solution)/shard_map/ppermute | solution.py:366
  143.6 28.0 %collective-permute-start.7 = (bf16[2048,256]{1,0:T(8,128)(2,1)}, bf16[2048,256]{1,0:T(8,128)(2,1)S(1)}, u32[]{:S(2)}, u32[]{:S(2)}) collective-permute-start(bf16[2048,256]{1,0:T(8,128)(2,1)} %collective-permute-done.6.refs_3_), channel_id=1, source_target_pairs={{0,96},{8,104},{16,112},{24,120},{32,0},{40,8},{48,16},{56,24},{64... | collective-permute-start | bytes 3145736 | tf_op jit(solution)/shard_map/ppermute | solution.py:366
  143.8 27.8 %collective-permute-start.15 = (bf16[2048,256]{1,0:T(8,128)(2,1)}, bf16[2048,256]{1,0:T(8,128)(2,1)}, u32[]{:S(2)}, u32[]{:S(2)}) collective-permute-start(bf16[2048,256]{1,0:T(8,128)(2,1)} %collective-permute-done.14.refs_7_), channel_id=1, source_target_pairs={{0,24},{8,0},{16,8},{24,16},{32,56},{40,32},{48,40},{56,48},{64,88... | collective-permute-start | bytes 3145736 | tf_op jit(solution)/shard_map/ppermute | solution.py:366
  189.1 16.7 %collective-permute-start.26 = (bf16[136,1024]{1,0:T(8,128)(2,1)}, bf16[136,1024]{1,0:T(8,128)(2,1)S(1)}, u32[]{:S(2)}, u32[]{:S(2)}) collective-permute-start(bf16[136,1024]{1,0:T(8,128)(2,1)} %head.1), channel_id=1, source_target_pairs={{0,24},{8,16},{16,8},{24,0},{32,56},{40,48},{48,40},{56,32},{64,88... | collective-permute-start | bytes 835592 | tf_op jit(solution)/shard_map/ppermute | solution.py:370
  189.3 16.5 %collective-permute-start.27 = (bf16[136,1024]{1,0:T(8,128)(2,1)}, bf16[136,1024]{1,0:T(8,128)(2,1)S(1)}, u32[]{:S(2)}, u32[]{:S(2)}) collective-permute-start(bf16[136,1024]{1,0:T(8,128)(2,1)} %head.1), channel_id=1, source_target_pairs={{0,16},{8,24},{16,0},{24,8},{32,48},{40,56},{48,32},{56,40},{64,80... | collective-permute-start | bytes 835592 | tf_op jit(solution)/shard_map/ppermute | solution.py:370
  (37 other events, 477.0 us)
Sparse Core Ops, SparseCore 0:
  181.0 48.8 reduce-scatter.1

commit v6 on v5

--- a/solution.py
+++ b/solution.py
@@ -412,12 +412,12 @@
         return [payloads[0]] + [swap(payloads[k], "z", k) for k in (1, 2, 3)]
 
     def chosen(got, sources):
-        return [pick(got, (at(sources, me ^ (4 * k)) & 3) ^ xi) for k in range(SIDE)]
+        columns = (sources & 3) ^ xi
+        return [pick(got, at(columns, me ^ (4 * k))) for k in range(SIDE)]
 
     def landed(got, sources):
-        source = at(sources, me)
-        value = pick(got, ((source >> 2) & 3) ^ zi)
-        return jnp.where(source >= 0, value, jnp.zeros_like(value))
+        value = pick(got, at(((sources >> 2) & 3) ^ zi, me))
+        return jnp.where(at(sources, me) >= 0, value, jnp.zeros_like(value))
 
     near = projected[1:, rows - BLK - PAD :].astype(f32)
     tail = jnp.zeros((2, BLK, chans), f32)
@@ -442,8 +442,8 @@
     grid = (chans // tile,)
     nb = rows // BLK
 
-    def col(*lead):
-        return pl.BlockSpec((*lead, tile), lambda i, *_: (*([0] * len(lead)), i))
+    def col(*lead, t=tile):
+        return pl.BlockSpec((*lead, t), lambda i, *_: (*([0] * len(lead)), i))
 
     const = pl.BlockSpec((2 * BLK, 2 * BLK), lambda i, *_: (0, 0))
     const_inv = pl.BlockSpec((BLK, 2 * BLK), lambda i, *_: (0, 0))
@@ -491,30 +491,31 @@
     def out_grad_rows(n):
         return [pl.BlockSpec((n, width), lambda i, c, j=j: (0, c[1 + 6 * SIDE + j])) for j in range(2 * SIDE)]
 
-    def first_rows(n, *lead):
+    def first_rows(n, *lead, t=tile):
         zeros = [0] * len(lead)
-        return pl.BlockSpec((*lead, n, tile), lambda i, c: (*zeros, 0, i))
-
+        return pl.BlockSpec((*lead, n, t), lambda i, c: (*zeros, 0, i))
+
+    big = 2 * tile
     head = pl.pallas_call(
         head_kernel,
         grid_spec=pltpu.PrefetchScalarGridSpec(
             num_scalar_prefetch=1,
-            grid=grid,
+            grid=(chans // big,),
             in_specs=[
-                first_rows(BLK + PAD),
-                first_rows(BLK + PAD, 1),
+                first_rows(BLK + PAD, t=big),
+                first_rows(BLK + PAD, 1, t=big),
                 pl.BlockSpec(
-                    (pl.Element(2), pl.Element(PAD), pl.Element(tile)),
-                    lambda i, c: (1, 0, i * tile),
+                    (pl.Element(2), pl.Element(PAD), pl.Element(big)),
+                    lambda i, c: (1, 0, i * big),
                 ),
-                first_rows(PAD),
-                col(BLK),
-                col(1),
+                first_rows(PAD, t=big),
+                col(BLK, t=big),
+                col(1, t=big),
                 *out_grad_rows(BLK + PAD),
-                *[last_spec] * 4,
+                *[pl.BlockSpec((2, big, width), lambda i, c: (0, i, 0))] * 4,
             ],
-            out_specs=col(BLK + PAD),
-            scratch_shapes=[pltpu.VMEM((BLK + PAD, tile), f32)],
+            out_specs=col(BLK + PAD, t=big),
+            scratch_shapes=[pltpu.VMEM((BLK + PAD, big), f32)],
         ),
         out_shape=jax.ShapeDtypeStruct((BLK + PAD, chans), bf16),
         cost_estimate=pl.CostEstimate(
@@ -573,20 +574,20 @@
     my_quarter = (sums[0] + sums[1]) + (sums[2] + sums[3])
 
     (out1,) = multiply_pieces(
-        far_a + far_b, table, gated, None, 16, (12, out1), per=2
+        far_a + far_b, table, gated, None, 8, (6, out1)
     )
     out1 = scatter(out1)
 
     low = rows - BLK - PAD
 
-    def rows_at(start, n, *lead):
+    def rows_at(start, n, *lead, t=tile):
         zeros = [0] * len(lead)
-        dims = [pl.Element(d) for d in (*lead, n, tile)]
-        return pl.BlockSpec(tuple(dims), lambda i: (*zeros, start, i * tile))
-
-    def acts_at(start, n):
+        dims = [pl.Element(d) for d in (*lead, n, t)]
+        return pl.BlockSpec(tuple(dims), lambda i: (*zeros, start, i * t))
+
+    def acts_at(start, n, t=tile):
         return pl.BlockSpec(
-            (pl.Element(2), pl.Element(n), pl.Element(tile)), lambda i: (1, start, i * tile)
+            (pl.Element(2), pl.Element(n), pl.Element(t)), lambda i: (1, start, i * t)
         )
 
     gp_shape = jax.ShapeDtypeStruct((3, rows, chans), bf16)
@@ -611,15 +612,15 @@
     rest = rows - low
     bottom = pl.pallas_call(
         bottom_kernel,
-        grid=grid,
+        grid=(chans // big,),
         in_specs=[
-            rows_at(low, rest), rows_at(low, rest), rows_at(low, rest), acts_at(low, rest),
-            col(BLK + PAD), rows_at(low, rest, 3), col(3, 3), col(2 * BLK), const, const_inv, col(16),
+            rows_at(low, rest, t=big), rows_at(low, rest, t=big), rows_at(low, rest, t=big), acts_at(low, rest, t=big),
+            col(BLK + PAD, t=big), rows_at(low, rest, 3, t=big), col(3, 3, t=big), col(2 * BLK, t=big), const, const_inv, col(16, t=big),
             pl.BlockSpec(memory_space=pl.ANY),
         ],
-        out_specs=[rows_at(low, rest, 3), col(16)],
+        out_specs=[rows_at(low, rest, 3, t=big), col(16, t=big)],
         out_shape=[gp_shape, short_shape],
-        scratch_shapes=[pltpu.VMEM((3, rest + PAD, tile), f32), pltpu.VMEM((rest, tile), f32)],
+        scratch_shapes=[pltpu.VMEM((3, rest + PAD, big), f32), pltpu.VMEM((rest, big), f32)],
         input_output_aliases={11: 0},
         cost_estimate=pl.CostEstimate(
             flops=2_000_000_000, bytes_accessed=5 << 20, transcendentals=0

time: 259 us -> 262 us (1.012)
  between operations: 22.2 us -> 35.1 us
  waiting for transfers between devices: 75.1 us -> 70.2 us
  local copies, waits for them, and re-layouts: 17.7 us -> 14.7 us
    ppermute x20, waiting for transfers between devices: 44.5 us -> 39 us  [ring(): return lax.ppermute(value, 'ctx', pairs)]
    slice x4, local copies, waits for them, and re-layouts: 3.44 us -> 0.07 us  [gather(): t, b = (ring(p[:h], first, 1), ring(q[h:], first, -1))]
    dynamic_slice x1 -> x6, local copies, waits for them, and re-layouts: 0.7 us -> 3.72 us  [at(): return lax.dynamic_index_in_dim(table, index, 0, keepdims=False)]
    unnamed x50 -> x40, local copies, waits for them, and re-layouts: 8.38 us -> 6.96 us
  transfers between devices with their start and end apart: 39 -> 39, of which waited for: 14 -> 14; matrix products, arithmetic and copies ran while one was open for 10% -> 7% of each run, Pallas kernels for 26% -> 25%
where the time goes in v6:
time: 262 us; the launch traced here: 260 us
  Pallas kernels  76.1 us (29%)
  waiting for transfers between devices  70.2 us (27%)
  starting transfers between devices  53.4 us (20%)
  between operations  35.1 us (13%)
  local copies, waits for them, and re-layouts  14.7 us (6%)
  other arithmetic  10.6 us (4%)
    ppermute x20, waiting for transfers between devices, ring(): return lax.ppermute(value, 'ctx', pairs)  39 us
    pallas_call x3, Pallas kernels, multiply_pieces(): pl.pallas_call(kernel, grid_spec=pltpu.PrefetchScalarGridSpec(num_scalar_...  33.1 us
    ppermute x18, waiting for transfers between devices, swap(): lax.ppermute(value, 'ctx', [(d, d ^ shift) for d in range(ctx_count)])  31.2 us
    ppermute x20, starting transfers between devices, ring(): return lax.ppermute(value, 'ctx', pairs)  28.5 us
    ppermute x18, starting transfers between devices, swap(): lax.ppermute(value, 'ctx', [(d, d ^ shift) for d in range(ctx_count)])  24.9 us
    pallas_call x1, Pallas kernels, on_device(): backward(table, acc, act, mspec, fspec, skip_row, fwd, inv_now, inv_lag,...  12.4 us
    pallas_call x1, Pallas kernels, on_device(): forward(projected, left, short_filter, long_filter, skip_row, fwd, inv_late)  8.93 us
    pallas_call x1, Pallas kernels, on_device(): top(bg, conv, gmix, act, bg, conv, gmix, act, projected, short_filter)  7.84 us
  transfers between devices with their start and end apart: 39, of which 14 were waited for; matrix products, arithmetic and copies ran while one was open for 7% of the time, Pallas kernels for 25%

profile of v6, /device:TPU:24, one launch (start us, length us, event | category | flops | bytes accessed | tf_op | source)
XLA Modules:
  0.0 260.0 jit_solution(1797174651914108762)
XLA Ops:
  25.9 6.1 %collective-permute-done.8 = bf16[1024,256]{1,0:T(8,128)(2,1)S(1)} collective-permute-done((bf16[1024,256]{1,0:T(8,128)(2,1)S(1)}, bf16[1024,256]{1,0:T(8,128)(2,1)S(1)}, u32[]{:S(2)}, u32[]{:S(2)}) %collective-permute-start.8) | collective-permute-done | bytes 524320 | tf_op jit(solution)/shard_map/ppermute | solution.py:366
  33.9 4.6 %collective-permute-done = bf16[1024,256]{1,0:T(8,128)(2,1)S(1)} collective-permute-done((bf16[1024,256]{1,0:T(8,128)(2,1)S(1)}, bf16[1024,256]{1,0:T(8,128)(2,1)S(1)}, u32[]{:S(2)}, u32[]{:S(2)}) %collective-permute-start) | collective-permute-done | bytes 524320 | tf_op jit(solution)/shard_map/ppermute | solution.py:366
  38.5 4.0 %collective-permute-start.11 = (bf16[1024,256]{1,0:T(8,128)(2,1)S(1)}, bf16[1024,256]{1,0:T(8,128)(2,1)S(1)}, u32[]{:S(2)}, u32[]{:S(2)}) collective-permute-start(bf16[1024,256]{1,0:T(8,128)(2,1)S(1)} %get-tuple-element.50), channel_id=1, source_target_pairs={{0,96},{8,104},{16,112},{24,120},{32,0},{40,8},{48,16},{56,24},{64... | collective-permute-start | bytes 1572872 | tf_op jit(solution)/shard_map/ppermute | solution.py:366
  46.3 3.3 %collective-permute-start.19 = (bf16[136,1024]{1,0:T(8,128)(2,1)S(1)}, bf16[136,1024]{1,0:T(8,128)(2,1)S(1)}, u32[]{:S(2)}, u32[]{:S(2)}) collective-permute-start(bf16[136,1024]{1,0:T(8,128)(2,1)S(1)} %get-tuple-element.49), channel_id=1, source_target_pairs={{0,96},{8,104},{16,112},{24,120},{32,64},{40,72},{48,80},{56,88},{... | collective-permute-start | bytes 835592 | tf_op jit(solution)/shard_map/ppermute | solution.py:370
  50.0 4.9 %collective-permute-done.11 = bf16[1024,256]{1,0:T(8,128)(2,1)S(1)} collective-permute-done((bf16[1024,256]{1,0:T(8,128)(2,1)S(1)}, bf16[1024,256]{1,0:T(8,128)(2,1)S(1)}, u32[]{:S(2)}, u32[]{:S(2)}) %collective-permute-start.11) | collective-permute-done | bytes 524320 | tf_op jit(solution)/shard_map/ppermute | solution.py:366
  54.9 3.4 %collective-permute-start.5 = (bf16[512,256]{1,0:T(8,128)(2,1)S(1)}, bf16[512,256]{1,0:T(8,128)(2,1)S(1)}, u32[]{:S(2)}, u32[]{:S(2)}) collective-permute-start(bf16[512,256]{1,0:T(8,128)(2,1)S(1)} %slice.109), channel_id=1, source_target_pairs={{0,24},{8,0},{16,8},{24,16},{32,56},{40,32},{48,40},{56,48},{64,88... | collective-permute-start | bytes 786440 | tf_op jit(solution)/shard_map/ppermute | solution.py:366
  58.3 16.9 %collective-permute-done.19 = bf16[136,1024]{1,0:T(8,128)(2,1)S(1)} collective-permute-done((bf16[136,1024]{1,0:T(8,128)(2,1)S(1)}, bf16[136,1024]{1,0:T(8,128)(2,1)S(1)}, u32[]{:S(2)}, u32[]{:S(2)}) %collective-permute-start.19) | collective-permute-done | bytes 278560 | tf_op jit(solution)/shard_map/ppermute | solution.py:370
  76.9 3.2 %collective-permute-start.13 = (bf16[512,256]{1,0:T(8,128)(2,1)S(1)}, bf16[512,256]{1,0:T(8,128)(2,1)S(1)}, u32[]{:S(2)}, u32[]{:S(2)}) collective-permute-start(bf16[512,256]{1,0:T(8,128)(2,1)S(1)} %slice.111), channel_id=1, source_target_pairs={{0,96},{8,104},{16,112},{24,120},{32,0},{40,8},{48,16},{56,24},{64... | collective-permute-start | bytes 786440 | tf_op jit(solution)/shard_map/ppermute | solution.py:366
  84.5 3.7 %collective-permute-done.13 = bf16[512,256]{1,0:T(8,128)(2,1)S(1)} collective-permute-done((bf16[512,256]{1,0:T(8,128)(2,1)S(1)}, bf16[512,256]{1,0:T(8,128)(2,1)S(1)}, u32[]{:S(2)}, u32[]{:S(2)}) %collective-permute-start.13) | collective-permute-done | bytes 262176 | tf_op jit(solution)/shard_map/ppermute | solution.py:366
  90.3 3.4 %collective-permute-done.20 = bf16[136,1024]{1,0:T(8,128)(2,1)S(1)} collective-permute-done((bf16[136,1024]{1,0:T(8,128)(2,1)S(1)}, bf16[136,1024]{1,0:T(8,128)(2,1)S(1)}, u32[]{:S(2)}, u32[]{:S(2)}) %collective-permute-start.20) | collective-permute-done | bytes 278560 | tf_op jit(solution)/shard_map/ppermute | solution.py:370
  95.1 3.3 %collective-permute-done.21 = bf16[136,1024]{1,0:T(8,128)(2,1)S(1)} collective-permute-done((bf16[136,1024]{1,0:T(8,128)(2,1)S(1)}, bf16[136,1024]{1,0:T(8,128)(2,1)S(1)}, u32[]{:S(2)}, u32[]{:S(2)}) %collective-permute-start.21) | collective-permute-done | bytes 278560 | tf_op jit(solution)/shard_map/ppermute | solution.py:370
  111.8 8.9 %forward.1 = (bf16[512,1024]{1,0:T(8,128)(2,1)}, f32[512,1024]{1,0:T(8,128)}, f32[3,512,1024]{2,1,0:T(8,128)}, f32[4,256,1024]{2,1,0:T(8,128)}, f32[256,1024]{1,0:T(8,128)}) custom-call(bf16[3,512,1024]{2,1,0:T(8,128)(2,1)} %proj.5, bf16[136,1024]{1,0:T(8,128)(2,1)} %select_select_fusion.3.halo, f32[3,3,1024]{2,1,0:T(4,128)} %sf.5, bf16[128,1024]{1,0:T(8,128)(2,1)} %lf.3, ...), custom_call_target="tpu_custom_call" | custom-call | flops 8000000000 | bytes 20971520 | tf_op jit(solution)/shard_map/forward/pallas_call | solution.py:476
  122.8 17.5 %collective-permute-done.6.refs_3_ = bf16[2048,256]{1,0:T(8,128)(2,1)} collective-permute-done((bf16[2048,256]{1,0:T(8,128)(2,1)}, bf16[2048,256]{1,0:T(8,128)(2,1)}, u32[]{:S(2)}, u32[]{:S(2)}) %collective-permute-start.6) | collective-permute-done | bytes 1048608 | tf_op jit(solution)/shard_map/ppermute | solution.py:366
  142.7 10.1 %pieces.3 = (bf16[512,8192]{1,0:T(8,128)(2,1)}, f32[512,1024]{1,0:T(8,128)}) custom-call(s32[33]{0:T(128)} %pad_add_fusion.cols_ref.cols.place, bf16[2048,256]{1,0:T(8,128)(2,1)} %copy-done.4, bf16[2048,256]{1,0:T(8,128)(2,1)} %constant_dynamic-update-slice_fusion.refs_1_, bf16[2048,256]{1,0:T(8,128)(2,1)} %copy-done.3, ...), custom_call_target="tpu_custom_call" | custom-call | flops 4294967296 | bytes 11534336 | tf_op jit(solution)/shard_map/pieces/pallas_call | solution.py:315
  152.8 16.0 %pieces.4 = (bf16[512,8192]{1,0:T(8,128)(2,1)}, f32[512,1024]{1,0:T(8,128)}) custom-call(s32[33]{0:T(128)} %pad_add_fusion.cols_ref.cols.place, bf16[2048,256]{1,0:T(8,128)(2,1)} %collective-permute-done.1.refs_0_, bf16[2048,256]{1,0:T(8,128)(2,1)} %collective-permute-done.22.refs_1_, bf16[2048,256]{1,0:T(8,128)(2,1)} %copy-done.7, ...), custom_call_target="tpu_custom_call", output_to_operand_aliasing={{0}: (15, {})} | custom-call | flops 8589934592 | bytes 19922944 | tf_op jit(solution)/shard_map/pieces/pallas_call | solution.py:315
  170.5 7.0 %pieces.5 = bf16[512,8192]{1,0:T(8,128)(2,1)} custom-call(s32[33]{0:T(128)} %pad_add_fusion.cols_ref.cols.place, bf16[2048,256]{1,0:T(8,128)(2,1)} %copy-done.1, bf16[2048,256]{1,0:T(8,128)(2,1)} %copy-done.2, bf16[2048,256]{1,0:T(8,128)(2,1)} %copy-done, bf16[2048,256]{1,0:T(8,128)(2,1)} %collective-permute-done.15.refs_3_, ...), custom_call_target="tpu_custom_call", output_to_operand_aliasing={{}: (6, {})} | custom-call | flops 2147483648 | bytes 11534336 | tf_op jit(solution)/shard_map/pieces/pallas_call | solution.py:315
  183.7 5.7 %head.1 = bf16[136,1024]{1,0:T(8,128)(2,1)} custom-call(s32[33]{0:T(128)} %pad_add_fusion.cols_ref.cols.place, f32[512,1024]{1,0:T(8,128)} %get-tuple-element.27.acc, f32[3,512,1024]{2,1,0:T(8,128)} %get-tuple-element.28.act0.act12.act.actn, f32[3,512,1024]{2,1,0:T(8,128)} %get-tuple-element.28.act0.act12.act.actn, ...), custom_call_target="tpu_custom_call" | custom-call | flops 600000000 | bytes 6291456 | tf_op jit(solution)/shard_map/head/pallas_call | solution.py:526
  189.5 2.8 %collective-permute-start.27 = (bf16[136,1024]{1,0:T(8,128)(2,1)}, bf16[136,1024]{1,0:T(8,128)(2,1)S(1)}, u32[]{:S(2)}, u32[]{:S(2)}) collective-permute-start(bf16[136,1024]{1,0:T(8,128)(2,1)} %head.1), channel_id=1, source_target_pairs={{0,16},{8,24},{16,0},{24,8},{32,48},{40,56},{48,32},{56,40},{64,80... | collective-permute-start | bytes 835592 | tf_op jit(solution)/shard_map/ppermute | solution.py:370
  193.6 12.4 %backward.1 = (f32[512,1024]{1,0:T(8,128)}, bf16[32,1024]{1,0:T(8,128)(2,1)}, bf16[32,1024]{1,0:T(8,128)(2,1)}, bf16[32,1024]{1,0:T(8,128)(2,1)}, bf16[32,1024]{1,0:T(8,128)(2,1)}, /*index=5*/f32[512,1024]{1,0:T(8,128)}) custom-call(s32[33]{0:T(128)} %pad_add_fusion.cols_ref.cols.place, f32[512,1024]{1,0:T(8,128)} %get-tuple-element.27.acc, ...), custom_call_target="tpu_custom_call" | custom-call | flops 8000000000 | bytes 20971520 | tf_op jit(solution)/shard_map/backward/pallas_call | solution.py:565
  207.0 2.9 %collective-permute-start.29 = (bf16[168,1024]{1,0:T(8,128)(2,1)S(1)}, bf16[168,1024]{1,0:T(8,128)(2,1)S(1)}, u32[]{:S(2)}, u32[]{:S(2)}) collective-permute-start(bf16[168,1024]{1,0:T(8,128)(2,1)S(1)} %pad_maximum_fusion.2), channel_id=1, source_target_pairs={{0,96},{8,104},{16,112},{24,120},{32,64},{40,72},{48,80},{56,88},{... | collective-permute-start | bytes 1032200 | tf_op jit(solution)/shard_map/ppermute | solution.py:370
  217.2 7.8 %top.1 = (bf16[3,512,1024]{2,1,0:T(8,128)(2,1)}, f32[16,1024]{1,0:T(8,128)}) custom-call(f32[512,1024]{1,0:T(8,128)} %get-tuple-element.31.bg.bgn, f32[512,1024]{1,0:T(8,128)} %get-tuple-element.32.convh.conv.convn, f32[512,1024]{1,0:T(8,128)} %get-tuple-element.33.gmix.gmixn, f32[3,512,1024]{2,1,0:T(8,128)} %get-tuple-element.28.act0.act12.act.actn, ...), custom_call_target="tpu_custom_call" | custom-call | flops 200000000 | bytes 10485760 | tf_op jit(solution)/shard_map/top/pallas_call | solution.py:611
  225.9 5.0 %bottom.1 = (bf16[3,512,1024]{2,1,0:T(8,128)(2,1)}, f32[16,1024]{1,0:T(8,128)}) custom-call(f32[512,1024]{1,0:T(8,128)} %get-tuple-element.31.bg.bgn, f32[512,1024]{1,0:T(8,128)} %get-tuple-element.32.convh.conv.convn, f32[512,1024]{1,0:T(8,128)} %get-tuple-element.33.gmix.gmixn, ...), custom_call_target="tpu_custom_call", output_to_operand_aliasing={{0}: (11, {})} | custom-call | flops 2000000000 | bytes 5242880 | tf_op jit(solution)/shard_map/bottom/pallas_call | solution.py:630
  233.5 3.1 %collective-permute-start.34 = (bf16[48,1024]{1,0:T(8,128)(2,1)S(1)}, bf16[48,1024]{1,0:T(8,128)(2,1)S(1)}, u32[]{:S(2)}, u32[]{:S(2)}) collective-permute-start(bf16[48,1024]{1,0:T(8,128)(2,1)S(1)} %pad_maximum_fusion.5), channel_id=1, source_target_pairs={{0,24},{8,16},{16,8},{24,0},{32,56},{40,48},{48,40},{56,32},{64,88... | collective-permute-start | bytes 294920 | tf_op jit(solution)/shard_map/ppermute | solution.py:370
  250.0 3.1 %collect.1 = bf16[64,8192]{1,0:T(8,128)(2,1)} custom-call(s32[33]{0:T(128)} %pad_add_fusion.cols_ref.cols.place, bf16[64,8192]{1,0:T(8,128)(2,1)} %reduce-scatter.2.cloned.1.call-done.refs_0_), custom_call_target="tpu_custom_call" | custom-call | flops 10000000 | bytes 5242880 | tf_op jit(solution)/shard_map/collect/pallas_call | solution.py:656
  (150 shorter events, 65.6 us)
Async XLA Ops:
  7.2 242.9 %reduce-scatter.2.cloned.1.call-start = ((), (), s32[]{:S(2)}) async-start(), calls=%async_computation.1 | async-start | bytes 9437184 | tf_op jit(solution)/shard_map/reduce_scatter | solution.py:481
  11.5 31.1 %collective-permute-start.16 = (bf16[136,1024]{1,0:T(8,128)(2,1)}, bf16[136,1024]{1,0:T(8,128)(2,1)}, u32[]{:S(2)}, u32[]{:S(2)}) collective-permute-start(bf16[136,1024]{1,0:T(8,128)(2,1)} %maximum_maximum_fusion), channel_id=1, source_target_pairs={{0,24},{8,16},{16,8},{24,0},{32,56},{40,48},{48,40},{56,32},{64,88... | collective-permute-start | bytes 835592 | tf_op jit(solution)/shard_map/ppermute | solution.py:370
  14.2 30.6 %collective-permute-start.17 = (bf16[136,1024]{1,0:T(8,128)(2,1)}, bf16[136,1024]{1,0:T(8,128)(2,1)}, u32[]{:S(2)}, u32[]{:S(2)}) collective-permute-start(bf16[136,1024]{1,0:T(8,128)(2,1)} %maximum_maximum_fusion), channel_id=1, source_target_pairs={{0,16},{8,24},{16,0},{24,8},{32,48},{40,56},{48,32},{56,40},{64,80... | collective-permute-start | bytes 835592 | tf_op jit(solution)/shard_map/ppermute | solution.py:370
  15.0 29.8 %collective-permute-start.18 = (bf16[136,1024]{1,0:T(8,128)(2,1)}, bf16[136,1024]{1,0:T(8,128)(2,1)}, u32[]{:S(2)}, u32[]{:S(2)}) collective-permute-start(bf16[136,1024]{1,0:T(8,128)(2,1)} %maximum_maximum_fusion), channel_id=1, source_target_pairs={{0,8},{8,0},{16,24},{24,16},{32,40},{40,32},{48,56},{56,48},{64,72... | collective-permute-start | bytes 835592 | tf_op jit(solution)/shard_map/ppermute | solution.py:370
  15.7 22.9 %collective-permute-start = (bf16[1024,256]{1,0:T(8,128)(2,1)S(1)}, bf16[1024,256]{1,0:T(8,128)(2,1)S(1)}, u32[]{:S(2)}, u32[]{:S(2)}) collective-permute-start(bf16[1024,256]{1,0:T(8,128)(2,1)S(1)} %get-tuple-element.51), channel_id=1, source_target_pairs={{0,8},{8,16},{16,24},{24,0},{32,40},{40,48},{48,56},{56,32},{64,72... | collective-permute-start | bytes 1572872 | tf_op jit(solution)/shard_map/ppermute | solution.py:366
  32.1 17.6 %collective-permute-start.3 = (bf16[1024,256]{1,0:T(8,128)(2,1)S(1)}, bf16[1024,256]{1,0:T(8,128)(2,1)S(1)}, u32[]{:S(2)}, u32[]{:S(2)}) collective-permute-start(bf16[1024,256]{1,0:T(8,128)(2,1)S(1)} %get-tuple-element.51), channel_id=1, source_target_pairs={{0,24},{8,0},{16,8},{24,16},{32,56},{40,32},{48,40},{56,48},{64,88... | collective-permute-start | bytes 1572872 | tf_op jit(solution)/shard_map/ppermute | solution.py:366
  42.6 56.4 %collective-permute-start.9 = (bf16[2048,256]{1,0:T(8,128)(2,1)S(1)}, bf16[2048,256]{1,0:T(8,128)(2,1)}, u32[]{:S(2)}, u32[]{:S(2)}) collective-permute-start(bf16[2048,256]{1,0:T(8,128)(2,1)S(1)} %pad_maximum_fusion.1.refs_2_), channel_id=1, source_target_pairs={{0,8},{8,16},{16,24},{24,0},{32,40},{40,48},{48,56},{56,32},{64,72... | collective-permute-start | bytes 3145736 | tf_op jit(solution)/shard_map/ppermute | solution.py:366
  44.8 55.6 %collective-permute-start.1 = (bf16[2048,256]{1,0:T(8,128)(2,1)S(1)}, bf16[2048,256]{1,0:T(8,128)(2,1)}, u32[]{:S(2)}, u32[]{:S(2)}) collective-permute-start(bf16[2048,256]{1,0:T(8,128)(2,1)S(1)} %pad_maximum_fusion.refs_0_), channel_id=1, source_target_pairs={{0,32},{8,40},{16,48},{24,56},{32,64},{40,72},{48,80},{56,88},{64,... | collective-permute-start | bytes 3145736 | tf_op jit(solution)/shard_map/ppermute | solution.py:366
  46.3 28.9 %collective-permute-start.19 = (bf16[136,1024]{1,0:T(8,128)(2,1)S(1)}, bf16[136,1024]{1,0:T(8,128)(2,1)S(1)}, u32[]{:S(2)}, u32[]{:S(2)}) collective-permute-start(bf16[136,1024]{1,0:T(8,128)(2,1)S(1)} %get-tuple-element.49), channel_id=1, source_target_pairs={{0,96},{8,104},{16,112},{24,120},{32,64},{40,72},{48,80},{56,88},{... | collective-permute-start | bytes 835592 | tf_op jit(solution)/shard_map/ppermute | solution.py:370
  49.7 27.2 %collective-permute-start.4 = (bf16[512,256]{1,0:T(8,128)(2,1)S(1)}, bf16[512,256]{1,0:T(8,128)(2,1)S(1)}, u32[]{:S(2)}, u32[]{:S(2)}) collective-permute-start(bf16[512,256]{1,0:T(8,128)(2,1)S(1)} %slice.108), channel_id=1, source_target_pairs={{0,8},{8,16},{16,24},{24,0},{32,40},{40,48},{48,56},{56,32},{64,72... | collective-permute-start | bytes 786440 | tf_op jit(solution)/shard_map/ppermute | solution.py:366
  54.9 22.0 %collective-permute-start.5 = (bf16[512,256]{1,0:T(8,128)(2,1)S(1)}, bf16[512,256]{1,0:T(8,128)(2,1)S(1)}, u32[]{:S(2)}, u32[]{:S(2)}) collective-permute-start(bf16[512,256]{1,0:T(8,128)(2,1)S(1)} %slice.109), channel_id=1, source_target_pairs={{0,24},{8,0},{16,8},{24,16},{32,56},{40,32},{48,40},{56,48},{64,88... | collective-permute-start | bytes 786440 | tf_op jit(solution)/shard_map/ppermute | solution.py:366
  75.3 35.1 %collective-permute-start.25 = (bf16[2048,256]{1,0:T(8,128)(2,1)S(1)}, bf16[2048,256]{1,0:T(8,128)(2,1)S(1)}, u32[]{:S(2)}, u32[]{:S(2)}) collective-permute-start(bf16[2048,256]{1,0:T(8,128)(2,1)S(1)} %pad_maximum_fusion.1.refs_2_), channel_id=1, source_target_pairs={{0,24},{8,0},{16,8},{24,16},{32,56},{40,32},{48,40},{56,48},{64,88... | collective-permute-start | bytes 3145736 | tf_op jit(solution)/shard_map/ppermute | solution.py:366
  93.7 27.1 %collective-permute-start.23 = (bf16[2048,256]{1,0:T(8,128)(2,1)S(1)}, bf16[2048,256]{1,0:T(8,128)(2,1)S(1)}, u32[]{:S(2)}, u32[]{:S(2)}) collective-permute-start(bf16[2048,256]{1,0:T(8,128)(2,1)S(1)} %pad_maximum_fusion.refs_0_), channel_id=1, source_target_pairs={{0,96},{8,104},{16,112},{24,120},{32,0},{40,8},{48,16},{56,24},{64... | collective-permute-start | bytes 3145736 | tf_op jit(solution)/shard_map/ppermute | solution.py:366
  98.4 42.0 %collective-permute-start.6 = (bf16[2048,256]{1,0:T(8,128)(2,1)}, bf16[2048,256]{1,0:T(8,128)(2,1)}, u32[]{:S(2)}, u32[]{:S(2)}) collective-permute-start(bf16[2048,256]{1,0:T(8,128)(2,1)} %constant_dynamic-update-slice_fusion.refs_1_), channel_id=1, source_target_pairs={{0,96},{8,104},{16,112},{24,120},{32,0},{40,8},{48,16},{56,24},{64... | collective-permute-start | bytes 3145736 | tf_op jit(solution)/shard_map/ppermute | solution.py:366
  99.1 42.0 %collective-permute-start.22 = (bf16[2048,256]{1,0:T(8,128)(2,1)}, bf16[2048,256]{1,0:T(8,128)(2,1)}, u32[]{:S(2)}, u32[]{:S(2)}) collective-permute-start(bf16[2048,256]{1,0:T(8,128)(2,1)} %constant_dynamic-update-slice_fusion.refs_1_), channel_id=1, source_target_pairs={{0,32},{8,40},{16,48},{24,56},{32,64},{40,72},{48,80},{56,88},{64,... | collective-permute-start | bytes 3145736 | tf_op jit(solution)/shard_map/ppermute | solution.py:366
  100.4 21.5 %collective-permute-start.14 = (bf16[2048,256]{1,0:T(8,128)(2,1)}, bf16[2048,256]{1,0:T(8,128)(2,1)S(1)}, u32[]{:S(2)}, u32[]{:S(2)}) collective-permute-start(bf16[2048,256]{1,0:T(8,128)(2,1)} %constant_dynamic-update-slice_fusion.3.refs_3_), channel_id=1, source_target_pairs={{0,24},{8,0},{16,8},{24,16},{32,56},{40,32},{48,40},{56,48},{64,88... | collective-permute-start | bytes 3145736 | tf_op jit(solution)/shard_map/ppermute | solution.py:366
  111.4 41.4 %collective-permute-start.24 = (bf16[2048,256]{1,0:T(8,128)(2,1)}, bf16[2048,256]{1,0:T(8,128)(2,1)}, u32[]{:S(2)}, u32[]{:S(2)}) collective-permute-start(bf16[2048,256]{1,0:T(8,128)(2,1)} %constant_dynamic-update-slice_fusion.3.refs_3_), channel_id=1, source_target_pairs={{0,8},{8,16},{16,24},{24,0},{32,40},{40,48},{48,56},{56,32},{64,72... | collective-permute-start | bytes 3145736 | tf_op jit(solution)/shard_map/ppermute | solution.py:366
  120.8 48.0 %collective-permute-start.10 = (bf16[2048,256]{1,0:T(8,128)(2,1)}, bf16[2048,256]{1,0:T(8,128)(2,1)S(1)}, u32[]{:S(2)}, u32[]{:S(2)}) collective-permute-start(bf16[2048,256]{1,0:T(8,128)(2,1)} %collective-permute-done.9.refs_4_), channel_id=1, source_target_pairs={{0,8},{8,16},{16,24},{24,0},{32,40},{40,48},{48,56},{56,32},{64,72... | collective-permute-start | bytes 3145736 | tf_op jit(solution)/shard_map/ppermute | solution.py:366
  121.9 47.0 %collective-permute-start.2 = (bf16[2048,256]{1,0:T(8,128)(2,1)}, bf16[2048,256]{1,0:T(8,128)(2,1)S(1)}, u32[]{:S(2)}, u32[]{:S(2)}) collective-permute-start(bf16[2048,256]{1,0:T(8,128)(2,1)} %collective-permute-done.1.refs_0_), channel_id=1, source_target_pairs={{0,32},{8,40},{16,48},{24,56},{32,64},{40,72},{48,80},{56,88},{64,... | collective-permute-start | bytes 3145736 | tf_op jit(solution)/shard_map/ppermute | solution.py:366
  140.4 28.5 %collective-permute-start.7 = (bf16[2048,256]{1,0:T(8,128)(2,1)}, bf16[2048,256]{1,0:T(8,128)(2,1)S(1)}, u32[]{:S(2)}, u32[]{:S(2)}) collective-permute-start(bf16[2048,256]{1,0:T(8,128)(2,1)} %collective-permute-done.6.refs_3_), channel_id=1, source_target_pairs={{0,96},{8,104},{16,112},{24,120},{32,0},{40,8},{48,16},{56,24},{64... | collective-permute-start | bytes 3145736 | tf_op jit(solution)/shard_map/ppermute | solution.py:366
  141.1 27.8 %collective-permute-start.15 = (bf16[2048,256]{1,0:T(8,128)(2,1)}, bf16[2048,256]{1,0:T(8,128)(2,1)}, u32[]{:S(2)}, u32[]{:S(2)}) collective-permute-start(bf16[2048,256]{1,0:T(8,128)(2,1)} %copy-done.8), channel_id=1, source_target_pairs={{0,24},{8,0},{16,8},{24,16},{32,56},{40,32},{48,40},{56,48},{64,88... | collective-permute-start | bytes 3145736 | tf_op jit(solution)/shard_map/ppermute | solution.py:366
  189.4 16.6 %collective-permute-start.26 = (bf16[136,1024]{1,0:T(8,128)(2,1)}, bf16[136,1024]{1,0:T(8,128)(2,1)S(1)}, u32[]{:S(2)}, u32[]{:S(2)}) collective-permute-start(bf16[136,1024]{1,0:T(8,128)(2,1)} %head.1), channel_id=1, source_target_pairs={{0,24},{8,16},{16,8},{24,0},{32,56},{40,48},{48,40},{56,32},{64,88... | collective-permute-start | bytes 835592 | tf_op jit(solution)/shard_map/ppermute | solution.py:370
  189.5 16.5 %collective-permute-start.27 = (bf16[136,1024]{1,0:T(8,128)(2,1)}, bf16[136,1024]{1,0:T(8,128)(2,1)S(1)}, u32[]{:S(2)}, u32[]{:S(2)}) collective-permute-start(bf16[136,1024]{1,0:T(8,128)(2,1)} %head.1), channel_id=1, source_target_pairs={{0,16},{8,24},{16,0},{24,8},{32,48},{40,56},{48,32},{56,40},{64,80... | collective-permute-start | bytes 835592 | tf_op jit(solution)/shard_map/ppermute | solution.py:370
  207.0 18.1 %collective-permute-start.29 = (bf16[168,1024]{1,0:T(8,128)(2,1)S(1)}, bf16[168,1024]{1,0:T(8,128)(2,1)S(1)}, u32[]{:S(2)}, u32[]{:S(2)}) collective-permute-start(bf16[168,1024]{1,0:T(8,128)(2,1)S(1)} %pad_maximum_fusion.2), channel_id=1, source_target_pairs={{0,96},{8,104},{16,112},{24,120},{32,64},{40,72},{48,80},{56,88},{... | collective-permute-start | bytes 1032200 | tf_op jit(solution)/shard_map/ppermute | solution.py:370
  (32 other events, 360.7 us)
Sparse Core Ops, SparseCore 0:
  177.6 48.9 reduce-scatter.1

commit v7 on v6

--- a/solution.py
+++ b/solution.py
@@ -412,12 +412,12 @@
         return [payloads[0]] + [swap(payloads[k], "z", k) for k in (1, 2, 3)]
 
     def chosen(got, sources):
-        columns = (sources & 3) ^ xi
-        return [pick(got, at(columns, me ^ (4 * k))) for k in range(SIDE)]
+        return [pick(got, (at(sources, me ^ (4 * k)) & 3) ^ xi) for k in range(SIDE)]
 
     def landed(got, sources):
-        value = pick(got, at(((sources >> 2) & 3) ^ zi, me))
-        return jnp.where(at(sources, me) >= 0, value, jnp.zeros_like(value))
+        source = at(sources, me)
+        value = pick(got, ((source >> 2) & 3) ^ zi)
+        return jnp.where(source >= 0, value, jnp.zeros_like(value))
 
     near = projected[1:, rows - BLK - PAD :].astype(f32)
     tail = jnp.zeros((2, BLK, chans), f32)

time: 262 us -> 256 us (0.977)
  between operations: 35.1 us -> 22.2 us
  waiting for transfers between devices: 70.2 us -> 75 us
  local copies, waits for them, and re-layouts: 14.7 us -> 17.7 us
    ppermute x20, waiting for transfers between devices: 39 us -> 44.5 us  [ring(): return lax.ppermute(value, 'ctx', pairs)]
    slice x4, local copies, waits for them, and re-layouts: 0.07 us -> 3.44 us  [gather(): t, b = (ring(p[:h], first, 1), ring(q[h:], first, -1))]
    dynamic_slice x6 -> x1, local copies, waits for them, and re-layouts: 3.72 us -> 0.7 us  [at(): return lax.dynamic_index_in_dim(table, index, 0, keepdims=False)]
    unnamed x40 -> x50, local copies, waits for them, and re-layouts: 6.96 us -> 8.38 us
  transfers between devices with their start and end apart: 39 -> 39, of which waited for: 14 -> 14; matrix products, arithmetic and copies ran while one was open for 7% -> 10% of each run, Pallas kernels for 25% -> 26%
where the time goes in v7:
time: 256 us; the launch traced here: 255 us
  Pallas kernels  75.7 us (30%)
  waiting for transfers between devices  75 us (29%)
  starting transfers between devices  51.7 us (20%)
  between operations  22.2 us (9%)
  local copies, waits for them, and re-layouts  17.7 us (7%)
  other arithmetic  12.6 us (5%)
    ppermute x20, waiting for transfers between devices, ring(): return lax.ppermute(value, 'ctx', pairs)  44.5 us
    pallas_call x3, Pallas kernels, multiply_pieces(): pl.pallas_call(kernel, grid_spec=pltpu.PrefetchScalarGridSpec(num_scalar_...  33.1 us
    ppermute x18, waiting for transfers between devices, swap(): lax.ppermute(value, 'ctx', [(d, d ^ shift) for d in range(ctx_count)])  30.6 us
    ppermute x20, starting transfers between devices, ring(): return lax.ppermute(value, 'ctx', pairs)  26.8 us
    ppermute x18, starting transfers between devices, swap(): lax.ppermute(value, 'ctx', [(d, d ^ shift) for d in range(ctx_count)])  24.8 us
    pallas_call x1, Pallas kernels, on_device(): backward(table, acc, act, mspec, fspec, skip_row, fwd, inv_now, inv_lag,...  12.4 us
    pallas_call x1, Pallas kernels, on_device(): forward(projected, left, short_filter, long_filter, skip_row, fwd, inv_late)  8.91 us
    unnamed x50, local copies, waits for them, and re-layouts  8.38 us
  transfers between devices with their start and end apart: 39, of which 14 were waited for; matrix products, arithmetic and copies ran while one was open for 10% of the time, Pallas kernels for 26%

profile of v7, /device:TPU:24, one launch (start us, length us, event | category | flops | bytes accessed | tf_op | source)
XLA Modules:
  0.0 255.0 jit_solution(7624491156868554970)
XLA Ops:
  13.9 2.8 %collective-permute-start.16 = (bf16[136,1024]{1,0:T(8,128)(2,1)}, bf16[136,1024]{1,0:T(8,128)(2,1)}, u32[]{:S(2)}, u32[]{:S(2)}) collective-permute-start(bf16[136,1024]{1,0:T(8,128)(2,1)} %maximum_maximum_fusion), channel_id=1, source_target_pairs={{0,24},{8,16},{16,8},{24,0},{32,56},{40,48},{48,40},{56,32},{64,88... | collective-permute-start | bytes 835592 | tf_op jit(solution)/shard_map/ppermute | solution.py:370
  24.5 2.8 %collective-permute-start.3 = (bf16[1024,256]{1,0:T(8,128)(2,1)S(1)}, bf16[1024,256]{1,0:T(8,128)(2,1)S(1)}, u32[]{:S(2)}, u32[]{:S(2)}) collective-permute-start(bf16[1024,256]{1,0:T(8,128)(2,1)S(1)} %get-tuple-element.49), channel_id=1, source_target_pairs={{0,24},{8,0},{16,8},{24,16},{32,56},{40,32},{48,40},{56,48},{64,88... | collective-permute-start | bytes 1572872 | tf_op jit(solution)/shard_map/ppermute | solution.py:366
  27.4 13.2 %collective-permute-done = bf16[1024,256]{1,0:T(8,128)(2,1)S(1)} collective-permute-done((bf16[1024,256]{1,0:T(8,128)(2,1)S(1)}, bf16[1024,256]{1,0:T(8,128)(2,1)S(1)}, u32[]{:S(2)}, u32[]{:S(2)}) %collective-permute-start) | collective-permute-done | bytes 524320 | tf_op jit(solution)/shard_map/ppermute | solution.py:366
  49.6 3.2 %collective-permute-start.19 = (bf16[136,1024]{1,0:T(8,128)(2,1)}, bf16[136,1024]{1,0:T(8,128)(2,1)}, u32[]{:S(2)}, u32[]{:S(2)}) collective-permute-start(bf16[136,1024]{1,0:T(8,128)(2,1)} %get-tuple-element.47), channel_id=1, source_target_pairs={{0,96},{8,104},{16,112},{24,120},{32,64},{40,72},{48,80},{56,88},{... | collective-permute-start | bytes 835592 | tf_op jit(solution)/shard_map/ppermute | solution.py:370
  56.9 3.4 %collective-permute-start.5 = (bf16[512,256]{1,0:T(8,128)(2,1)}, bf16[512,256]{1,0:T(8,128)(2,1)}, u32[]{:S(2)}, u32[]{:S(2)}) collective-permute-start(bf16[512,256]{1,0:T(8,128)(2,1)} %slice.109), channel_id=1, source_target_pairs={{0,24},{8,0},{16,8},{24,16},{32,56},{40,32},{48,40},{56,48},{64,88... | collective-permute-start | bytes 786440 | tf_op jit(solution)/shard_map/ppermute | solution.py:366
  62.4 15.4 %collective-permute-done.19 = bf16[136,1024]{1,0:T(8,128)(2,1)} collective-permute-done((bf16[136,1024]{1,0:T(8,128)(2,1)}, bf16[136,1024]{1,0:T(8,128)(2,1)}, u32[]{:S(2)}, u32[]{:S(2)}) %collective-permute-start.19) | collective-permute-done | bytes 278560 | tf_op jit(solution)/shard_map/ppermute | solution.py:370
  79.4 3.2 %collective-permute-start.13 = (bf16[512,256]{1,0:T(8,128)(2,1)S(1)}, bf16[512,256]{1,0:T(8,128)(2,1)S(1)}, u32[]{:S(2)}, u32[]{:S(2)}) collective-permute-start(bf16[512,256]{1,0:T(8,128)(2,1)S(1)} %slice.111), channel_id=1, source_target_pairs={{0,96},{8,104},{16,112},{24,120},{32,0},{40,8},{48,16},{56,24},{64... | collective-permute-start | bytes 786440 | tf_op jit(solution)/shard_map/ppermute | solution.py:366
  87.0 3.2 %collective-permute-done.13 = bf16[512,256]{1,0:T(8,128)(2,1)S(1)} collective-permute-done((bf16[512,256]{1,0:T(8,128)(2,1)S(1)}, bf16[512,256]{1,0:T(8,128)(2,1)S(1)}, u32[]{:S(2)}, u32[]{:S(2)}) %collective-permute-start.13) | collective-permute-done | bytes 262176 | tf_op jit(solution)/shard_map/ppermute | solution.py:366
  93.4 3.7 %collective-permute-done.20 = bf16[136,1024]{1,0:T(8,128)(2,1)S(1)} collective-permute-done((bf16[136,1024]{1,0:T(8,128)(2,1)}, bf16[136,1024]{1,0:T(8,128)(2,1)S(1)}, u32[]{:S(2)}, u32[]{:S(2)}) %collective-permute-start.20) | collective-permute-done | bytes 278560 | tf_op jit(solution)/shard_map/ppermute | solution.py:370
  98.3 3.3 %collective-permute-done.21 = bf16[136,1024]{1,0:T(8,128)(2,1)S(1)} collective-permute-done((bf16[136,1024]{1,0:T(8,128)(2,1)S(1)}, bf16[136,1024]{1,0:T(8,128)(2,1)S(1)}, u32[]{:S(2)}, u32[]{:S(2)}) %collective-permute-start.21) | collective-permute-done | bytes 278560 | tf_op jit(solution)/shard_map/ppermute | solution.py:370
  110.1 8.9 %forward.1 = (bf16[512,1024]{1,0:T(8,128)(2,1)}, f32[512,1024]{1,0:T(8,128)}, f32[3,512,1024]{2,1,0:T(8,128)}, f32[4,256,1024]{2,1,0:T(8,128)}, f32[256,1024]{1,0:T(8,128)}) custom-call(bf16[3,512,1024]{2,1,0:T(8,128)(2,1)} %proj.5, bf16[136,1024]{1,0:T(8,128)(2,1)} %select_select_fusion.3.halo, f32[3,3,1024]{2,1,0:T(4,128)} %sf.5, bf16[128,1024]{1,0:T(8,128)(2,1)} %lf.3, ...), custom_call_target="tpu_custom_call" | custom-call | flops 8000000000 | bytes 20971520 | tf_op jit(solution)/shard_map/forward/pallas_call | solution.py:476
  119.0 5.2 %collective-permute-done.23.refs_2_ = bf16[2048,256]{1,0:T(8,128)(2,1)} collective-permute-done((bf16[2048,256]{1,0:T(8,128)(2,1)S(1)}, bf16[2048,256]{1,0:T(8,128)(2,1)}, u32[]{:S(2)}, u32[]{:S(2)}) %collective-permute-start.23) | collective-permute-done | bytes 1048608 | tf_op jit(solution)/shard_map/ppermute | solution.py:366
  124.6 19.1 %collective-permute-done.6.refs_3_ = bf16[2048,256]{1,0:T(8,128)(2,1)} collective-permute-done((bf16[2048,256]{1,0:T(8,128)(2,1)}, bf16[2048,256]{1,0:T(8,128)(2,1)}, u32[]{:S(2)}, u32[]{:S(2)}) %collective-permute-start.6) | collective-permute-done | bytes 1048608 | tf_op jit(solution)/shard_map/ppermute | solution.py:366
  145.5 10.1 %pieces.3 = (bf16[512,8192]{1,0:T(8,128)(2,1)}, f32[512,1024]{1,0:T(8,128)}) custom-call(s32[33]{0:T(128)} %pad_add_fusion.cols_ref.cols.place, bf16[2048,256]{1,0:T(8,128)(2,1)} %copy-done.4, bf16[2048,256]{1,0:T(8,128)(2,1)} %constant_dynamic-update-slice_fusion.refs_1_, bf16[2048,256]{1,0:T(8,128)(2,1)} %copy-done.3, ...), custom_call_target="tpu_custom_call" | custom-call | flops 4294967296 | bytes 11534336 | tf_op jit(solution)/shard_map/pieces/pallas_call | solution.py:315
  155.6 16.0 %pieces.4 = (bf16[512,8192]{1,0:T(8,128)(2,1)}, f32[512,1024]{1,0:T(8,128)}) custom-call(s32[33]{0:T(128)} %pad_add_fusion.cols_ref.cols.place, bf16[2048,256]{1,0:T(8,128)(2,1)} %collective-permute-done.1.refs_0_, bf16[2048,256]{1,0:T(8,128)(2,1)} %collective-permute-done.22.refs_1_, ...), custom_call_target="tpu_custom_call", output_to_operand_aliasing={{0}: (15, {})} | custom-call | flops 8589934592 | bytes 19922944 | tf_op jit(solution)/shard_map/pieces/pallas_call | solution.py:315
  173.2 7.0 %pieces.5 = bf16[512,8192]{1,0:T(8,128)(2,1)} custom-call(s32[33]{0:T(128)} %pad_add_fusion.cols_ref.cols.place, bf16[2048,256]{1,0:T(8,128)(2,1)} %copy-done.1, bf16[2048,256]{1,0:T(8,128)(2,1)} %copy-done.2, bf16[2048,256]{1,0:T(8,128)(2,1)} %copy-done, bf16[2048,256]{1,0:T(8,128)(2,1)} %collective-permute-done.15.refs_3_, ...), custom_call_target="tpu_custom_call", output_to_operand_aliasing={{}: (6, {})} | custom-call | flops 2147483648 | bytes 11534336 | tf_op jit(solution)/shard_map/pieces/pallas_call | solution.py:315
  182.3 5.3 %head.1 = bf16[136,1024]{1,0:T(8,128)(2,1)} custom-call(s32[33]{0:T(128)} %pad_add_fusion.cols_ref.cols.place, f32[512,1024]{1,0:T(8,128)} %get-tuple-element.27.acc, f32[3,512,1024]{2,1,0:T(8,128)} %get-tuple-element.28.act0.act12.act.actn, f32[3,512,1024]{2,1,0:T(8,128)} %get-tuple-element.28.act0.act12.act.actn, ...), custom_call_target="tpu_custom_call" | custom-call | flops 600000000 | bytes 6291456 | tf_op jit(solution)/shard_map/head/pallas_call | solution.py:526
  191.8 12.4 %backward.1 = (f32[512,1024]{1,0:T(8,128)}, bf16[32,1024]{1,0:T(8,128)(2,1)}, bf16[32,1024]{1,0:T(8,128)(2,1)}, bf16[32,1024]{1,0:T(8,128)(2,1)}, bf16[32,1024]{1,0:T(8,128)(2,1)}, /*index=5*/f32[512,1024]{1,0:T(8,128)}) custom-call(s32[33]{0:T(128)} %pad_add_fusion.cols_ref.cols.place, f32[512,1024]{1,0:T(8,128)} %get-tuple-element.27.acc, ...), custom_call_target="tpu_custom_call" | custom-call | flops 8000000000 | bytes 20971520 | tf_op jit(solution)/shard_map/backward/pallas_call | solution.py:565
  205.2 2.6 %collective-permute-start.29 = (bf16[168,1024]{1,0:T(8,128)(2,1)S(1)}, bf16[168,1024]{1,0:T(8,128)(2,1)S(1)}, u32[]{:S(2)}, u32[]{:S(2)}) collective-permute-start(bf16[168,1024]{1,0:T(8,128)(2,1)S(1)} %pad_maximum_fusion.2), channel_id=1, source_target_pairs={{0,96},{8,104},{16,112},{24,120},{32,64},{40,72},{48,80},{56,88},{... | collective-permute-start | bytes 1032200 | tf_op jit(solution)/shard_map/ppermute | solution.py:370
  211.7 7.8 %top.1 = (bf16[3,512,1024]{2,1,0:T(8,128)(2,1)}, f32[16,1024]{1,0:T(8,128)}) custom-call(f32[512,1024]{1,0:T(8,128)} %get-tuple-element.31.bg.bgn, f32[512,1024]{1,0:T(8,128)} %get-tuple-element.32.convh.conv.convn, f32[512,1024]{1,0:T(8,128)} %get-tuple-element.33.gmix.gmixn, f32[3,512,1024]{2,1,0:T(8,128)} %get-tuple-element.28.act0.act12.act.actn, ...), custom_call_target="tpu_custom_call" | custom-call | flops 200000000 | bytes 10485760 | tf_op jit(solution)/shard_map/top/pallas_call | solution.py:611
  220.7 5.0 %bottom.1 = (bf16[3,512,1024]{2,1,0:T(8,128)(2,1)}, f32[16,1024]{1,0:T(8,128)}) custom-call(f32[512,1024]{1,0:T(8,128)} %get-tuple-element.31.bg.bgn, f32[512,1024]{1,0:T(8,128)} %get-tuple-element.32.convh.conv.convn, f32[512,1024]{1,0:T(8,128)} %get-tuple-element.33.gmix.gmixn, ...), custom_call_target="tpu_custom_call", output_to_operand_aliasing={{0}: (11, {})} | custom-call | flops 2000000000 | bytes 5242880 | tf_op jit(solution)/shard_map/bottom/pallas_call | solution.py:630
  228.6 2.7 %collective-permute-start.34 = (bf16[48,1024]{1,0:T(8,128)(2,1)S(1)}, bf16[48,1024]{1,0:T(8,128)(2,1)S(1)}, u32[]{:S(2)}, u32[]{:S(2)}) collective-permute-start(bf16[48,1024]{1,0:T(8,128)(2,1)S(1)} %pad_maximum_fusion.5), channel_id=1, source_target_pairs={{0,24},{8,16},{16,8},{24,0},{32,56},{40,48},{48,40},{56,32},{64,88... | collective-permute-start | bytes 294920 | tf_op jit(solution)/shard_map/ppermute | solution.py:370
  240.7 2.8 %collective-permute-done.36 = bf16[48,1024]{1,0:T(8,128)(2,1)S(1)} collective-permute-done((bf16[48,1024]{1,0:T(8,128)(2,1)S(1)}, bf16[48,1024]{1,0:T(8,128)(2,1)S(1)}, u32[]{:S(2)}, u32[]{:S(2)}) %collective-permute-start.36) | collective-permute-done | bytes 98336 | tf_op jit(solution)/shard_map/ppermute | solution.py:370
  245.1 3.1 %collect.1 = bf16[64,8192]{1,0:T(8,128)(2,1)} custom-call(s32[33]{0:T(128)} %pad_add_fusion.cols_ref.cols.place, bf16[64,8192]{1,0:T(8,128)(2,1)} %reduce-scatter.2.cloned.1.call-done.refs_0_), custom_call_target="tpu_custom_call" | custom-call | flops 10000000 | bytes 5242880 | tf_op jit(solution)/shard_map/collect/pallas_call | solution.py:656
  (154 shorter events, 70.6 us)
Async XLA Ops:
  7.2 237.9 %reduce-scatter.2.cloned.1.call-start = ((), (), s32[]{:S(2)}) async-start(), calls=%async_computation.1 | async-start | bytes 9437184 | tf_op jit(solution)/shard_map/reduce_scatter | solution.py:481
  8.5 16.0 %collective-permute-start.8 = (bf16[1024,256]{1,0:T(8,128)(2,1)S(1)}, bf16[1024,256]{1,0:T(8,128)(2,1)S(1)}, u32[]{:S(2)}, u32[]{:S(2)}) collective-permute-start(bf16[1024,256]{1,0:T(8,128)(2,1)S(1)} %get-tuple-element.48), channel_id=1, source_target_pairs={{0,32},{8,40},{16,48},{24,56},{32,64},{40,72},{48,80},{56,88},{64,... | collective-permute-start | bytes 1572872 | tf_op jit(solution)/shard_map/ppermute | solution.py:366
  13.9 31.2 %collective-permute-start.16 = (bf16[136,1024]{1,0:T(8,128)(2,1)}, bf16[136,1024]{1,0:T(8,128)(2,1)}, u32[]{:S(2)}, u32[]{:S(2)}) collective-permute-start(bf16[136,1024]{1,0:T(8,128)(2,1)} %maximum_maximum_fusion), channel_id=1, source_target_pairs={{0,24},{8,16},{16,8},{24,0},{32,56},{40,48},{48,40},{56,32},{64,88... | collective-permute-start | bytes 835592 | tf_op jit(solution)/shard_map/ppermute | solution.py:370
  16.6 30.6 %collective-permute-start.17 = (bf16[136,1024]{1,0:T(8,128)(2,1)}, bf16[136,1024]{1,0:T(8,128)(2,1)}, u32[]{:S(2)}, u32[]{:S(2)}) collective-permute-start(bf16[136,1024]{1,0:T(8,128)(2,1)} %maximum_maximum_fusion), channel_id=1, source_target_pairs={{0,16},{8,24},{16,0},{24,8},{32,48},{40,56},{48,32},{56,40},{64,80... | collective-permute-start | bytes 835592 | tf_op jit(solution)/shard_map/ppermute | solution.py:370
  17.4 29.8 %collective-permute-start.18 = (bf16[136,1024]{1,0:T(8,128)(2,1)}, bf16[136,1024]{1,0:T(8,128)(2,1)}, u32[]{:S(2)}, u32[]{:S(2)}) collective-permute-start(bf16[136,1024]{1,0:T(8,128)(2,1)} %maximum_maximum_fusion), channel_id=1, source_target_pairs={{0,8},{8,0},{16,24},{24,16},{32,40},{40,32},{48,56},{56,48},{64,72... | collective-permute-start | bytes 835592 | tf_op jit(solution)/shard_map/ppermute | solution.py:370
  18.0 22.6 %collective-permute-start = (bf16[1024,256]{1,0:T(8,128)(2,1)S(1)}, bf16[1024,256]{1,0:T(8,128)(2,1)S(1)}, u32[]{:S(2)}, u32[]{:S(2)}) collective-permute-start(bf16[1024,256]{1,0:T(8,128)(2,1)S(1)} %get-tuple-element.49), channel_id=1, source_target_pairs={{0,8},{8,16},{16,24},{24,0},{32,40},{40,48},{48,56},{56,32},{64,72... | collective-permute-start | bytes 1572872 | tf_op jit(solution)/shard_map/ppermute | solution.py:366
  24.5 29.1 %collective-permute-start.3 = (bf16[1024,256]{1,0:T(8,128)(2,1)S(1)}, bf16[1024,256]{1,0:T(8,128)(2,1)S(1)}, u32[]{:S(2)}, u32[]{:S(2)}) collective-permute-start(bf16[1024,256]{1,0:T(8,128)(2,1)S(1)} %get-tuple-element.49), channel_id=1, source_target_pairs={{0,24},{8,0},{16,8},{24,16},{32,56},{40,32},{48,40},{56,48},{64,88... | collective-permute-start | bytes 1572872 | tf_op jit(solution)/shard_map/ppermute | solution.py:366
  45.0 56.8 %collective-permute-start.9 = (bf16[2048,256]{1,0:T(8,128)(2,1)S(1)}, bf16[2048,256]{1,0:T(8,128)(2,1)}, u32[]{:S(2)}, u32[]{:S(2)}) collective-permute-start(bf16[2048,256]{1,0:T(8,128)(2,1)S(1)} %pad_maximum_fusion.1.refs_2_), channel_id=1, source_target_pairs={{0,8},{8,16},{16,24},{24,0},{32,40},{40,48},{48,56},{56,32},{64,72... | collective-permute-start | bytes 3145736 | tf_op jit(solution)/shard_map/ppermute | solution.py:366
  47.2 56.4 %collective-permute-start.1 = (bf16[2048,256]{1,0:T(8,128)(2,1)S(1)}, bf16[2048,256]{1,0:T(8,128)(2,1)}, u32[]{:S(2)}, u32[]{:S(2)}) collective-permute-start(bf16[2048,256]{1,0:T(8,128)(2,1)S(1)} %pad_maximum_fusion.refs_0_), channel_id=1, source_target_pairs={{0,32},{8,40},{16,48},{24,56},{32,64},{40,72},{48,80},{56,88},{64,... | collective-permute-start | bytes 3145736 | tf_op jit(solution)/shard_map/ppermute | solution.py:366
  49.6 28.1 %collective-permute-start.19 = (bf16[136,1024]{1,0:T(8,128)(2,1)}, bf16[136,1024]{1,0:T(8,128)(2,1)}, u32[]{:S(2)}, u32[]{:S(2)}) collective-permute-start(bf16[136,1024]{1,0:T(8,128)(2,1)} %get-tuple-element.47), channel_id=1, source_target_pairs={{0,96},{8,104},{16,112},{24,120},{32,64},{40,72},{48,80},{56,88},{... | collective-permute-start | bytes 835592 | tf_op jit(solution)/shard_map/ppermute | solution.py:370
  53.6 25.8 %collective-permute-start.4 = (bf16[512,256]{1,0:T(8,128)(2,1)}, bf16[512,256]{1,0:T(8,128)(2,1)}, u32[]{:S(2)}, u32[]{:S(2)}) collective-permute-start(bf16[512,256]{1,0:T(8,128)(2,1)} %slice.108), channel_id=1, source_target_pairs={{0,8},{8,16},{16,24},{24,0},{32,40},{40,48},{48,56},{56,32},{64,72... | collective-permute-start | bytes 786440 | tf_op jit(solution)/shard_map/ppermute | solution.py:366
  56.9 22.5 %collective-permute-start.5 = (bf16[512,256]{1,0:T(8,128)(2,1)}, bf16[512,256]{1,0:T(8,128)(2,1)}, u32[]{:S(2)}, u32[]{:S(2)}) collective-permute-start(bf16[512,256]{1,0:T(8,128)(2,1)} %slice.109), channel_id=1, source_target_pairs={{0,24},{8,0},{16,8},{24,16},{32,56},{40,32},{48,40},{56,48},{64,88... | collective-permute-start | bytes 786440 | tf_op jit(solution)/shard_map/ppermute | solution.py:366
  77.8 31.9 %collective-permute-start.25 = (bf16[2048,256]{1,0:T(8,128)(2,1)S(1)}, bf16[2048,256]{1,0:T(8,128)(2,1)}, u32[]{:S(2)}, u32[]{:S(2)}) collective-permute-start(bf16[2048,256]{1,0:T(8,128)(2,1)S(1)} %pad_maximum_fusion.1.refs_2_), channel_id=1, source_target_pairs={{0,24},{8,0},{16,8},{24,16},{32,56},{40,32},{48,40},{56,48},{64,88... | collective-permute-start | bytes 3145736 | tf_op jit(solution)/shard_map/ppermute | solution.py:366
  97.1 27.1 %collective-permute-start.23 = (bf16[2048,256]{1,0:T(8,128)(2,1)S(1)}, bf16[2048,256]{1,0:T(8,128)(2,1)}, u32[]{:S(2)}, u32[]{:S(2)}) collective-permute-start(bf16[2048,256]{1,0:T(8,128)(2,1)S(1)} %pad_maximum_fusion.refs_0_), channel_id=1, source_target_pairs={{0,96},{8,104},{16,112},{24,120},{32,0},{40,8},{48,16},{56,24},{64... | collective-permute-start | bytes 3145736 | tf_op jit(solution)/shard_map/ppermute | solution.py:366
  101.6 42.0 %collective-permute-start.6 = (bf16[2048,256]{1,0:T(8,128)(2,1)}, bf16[2048,256]{1,0:T(8,128)(2,1)}, u32[]{:S(2)}, u32[]{:S(2)}) collective-permute-start(bf16[2048,256]{1,0:T(8,128)(2,1)} %constant_dynamic-update-slice_fusion.refs_1_), channel_id=1, source_target_pairs={{0,96},{8,104},{16,112},{24,120},{32,0},{40,8},{48,16},{56,24},{64... | collective-permute-start | bytes 3145736 | tf_op jit(solution)/shard_map/ppermute | solution.py:366
  101.8 42.0 %collective-permute-start.22 = (bf16[2048,256]{1,0:T(8,128)(2,1)}, bf16[2048,256]{1,0:T(8,128)(2,1)}, u32[]{:S(2)}, u32[]{:S(2)}) collective-permute-start(bf16[2048,256]{1,0:T(8,128)(2,1)} %constant_dynamic-update-slice_fusion.refs_1_), channel_id=1, source_target_pairs={{0,32},{8,40},{16,48},{24,56},{32,64},{40,72},{48,80},{56,88},{64,... | collective-permute-start | bytes 3145736 | tf_op jit(solution)/shard_map/ppermute | solution.py:366
  103.6 20.9 %collective-permute-start.14 = (bf16[2048,256]{1,0:T(8,128)(2,1)}, bf16[2048,256]{1,0:T(8,128)(2,1)}, u32[]{:S(2)}, u32[]{:S(2)}) collective-permute-start(bf16[2048,256]{1,0:T(8,128)(2,1)} %constant_dynamic-update-slice_fusion.3.refs_3_), channel_id=1, source_target_pairs={{0,24},{8,0},{16,8},{24,16},{32,56},{40,32},{48,40},{56,48},{64,88... | collective-permute-start | bytes 3145736 | tf_op jit(solution)/shard_map/ppermute | solution.py:366
  109.7 45.9 %collective-permute-start.24 = (bf16[2048,256]{1,0:T(8,128)(2,1)}, bf16[2048,256]{1,0:T(8,128)(2,1)}, u32[]{:S(2)}, u32[]{:S(2)}) collective-permute-start(bf16[2048,256]{1,0:T(8,128)(2,1)} %constant_dynamic-update-slice_fusion.3.refs_3_), channel_id=1, source_target_pairs={{0,8},{8,16},{16,24},{24,0},{32,40},{40,48},{48,56},{56,32},{64,72... | collective-permute-start | bytes 3145736 | tf_op jit(solution)/shard_map/ppermute | solution.py:366
  124.2 47.4 %collective-permute-start.10 = (bf16[2048,256]{1,0:T(8,128)(2,1)}, bf16[2048,256]{1,0:T(8,128)(2,1)S(1)}, u32[]{:S(2)}, u32[]{:S(2)}) collective-permute-start(bf16[2048,256]{1,0:T(8,128)(2,1)} %collective-permute-done.9.refs_4_), channel_id=1, source_target_pairs={{0,8},{8,16},{16,24},{24,0},{32,40},{40,48},{48,56},{56,32},{64,72... | collective-permute-start | bytes 3145736 | tf_op jit(solution)/shard_map/ppermute | solution.py:366
  124.6 47.0 %collective-permute-start.2 = (bf16[2048,256]{1,0:T(8,128)(2,1)}, bf16[2048,256]{1,0:T(8,128)(2,1)S(1)}, u32[]{:S(2)}, u32[]{:S(2)}) collective-permute-start(bf16[2048,256]{1,0:T(8,128)(2,1)} %collective-permute-done.1.refs_0_), channel_id=1, source_target_pairs={{0,32},{8,40},{16,48},{24,56},{32,64},{40,72},{48,80},{56,88},{64,... | collective-permute-start | bytes 3145736 | tf_op jit(solution)/shard_map/ppermute | solution.py:366
  143.6 28.0 %collective-permute-start.7 = (bf16[2048,256]{1,0:T(8,128)(2,1)}, bf16[2048,256]{1,0:T(8,128)(2,1)S(1)}, u32[]{:S(2)}, u32[]{:S(2)}) collective-permute-start(bf16[2048,256]{1,0:T(8,128)(2,1)} %collective-permute-done.6.refs_3_), channel_id=1, source_target_pairs={{0,96},{8,104},{16,112},{24,120},{32,0},{40,8},{48,16},{56,24},{64... | collective-permute-start | bytes 3145736 | tf_op jit(solution)/shard_map/ppermute | solution.py:366
  143.8 27.8 %collective-permute-start.15 = (bf16[2048,256]{1,0:T(8,128)(2,1)}, bf16[2048,256]{1,0:T(8,128)(2,1)}, u32[]{:S(2)}, u32[]{:S(2)}) collective-permute-start(bf16[2048,256]{1,0:T(8,128)(2,1)} %collective-permute-done.14.refs_7_), channel_id=1, source_target_pairs={{0,24},{8,0},{16,8},{24,16},{32,56},{40,32},{48,40},{56,48},{64,88... | collective-permute-start | bytes 3145736 | tf_op jit(solution)/shard_map/ppermute | solution.py:366
  187.6 16.6 %collective-permute-start.26 = (bf16[136,1024]{1,0:T(8,128)(2,1)}, bf16[136,1024]{1,0:T(8,128)(2,1)S(1)}, u32[]{:S(2)}, u32[]{:S(2)}) collective-permute-start(bf16[136,1024]{1,0:T(8,128)(2,1)} %head.1), channel_id=1, source_target_pairs={{0,24},{8,16},{16,8},{24,0},{32,56},{40,48},{48,40},{56,32},{64,88... | collective-permute-start | bytes 835592 | tf_op jit(solution)/shard_map/ppermute | solution.py:370
  187.8 16.5 %collective-permute-start.27 = (bf16[136,1024]{1,0:T(8,128)(2,1)}, bf16[136,1024]{1,0:T(8,128)(2,1)S(1)}, u32[]{:S(2)}, u32[]{:S(2)}) collective-permute-start(bf16[136,1024]{1,0:T(8,128)(2,1)} %head.1), channel_id=1, source_target_pairs={{0,16},{8,24},{16,0},{24,8},{32,48},{40,56},{48,32},{56,40},{64,80... | collective-permute-start | bytes 835592 | tf_op jit(solution)/shard_map/ppermute | solution.py:370
  (37 other events, 476.6 us)
Sparse Core Ops, SparseCore 0:
  180.4 48.8 reduce-scatter.1
